TPU v7x, 1024 devices: a whole 8x8x8 slice. The times are simulated.
1024 devices in a mesh: row: 16 (over x, y_lo), col: 64 (over y_hi, z, core).
Axes of the slice: x: 8, y: 8 (y_hi: 4, y_lo: 2; y = y_hi * 2 + y_lo), z: 8, core: 2. Of those that a mesh axis runs over, the one named last changes fastest.
Arguments:
- tokens: bfloat16 [640, 8192], P('col', 'row'), may hold values from -6 to 6
- cotangent: bfloat16 [640, 8192], P('col', 'row'), may hold values from -6 to 6
- gate_tiles: bfloat16 [96, 8192, 128], P('row', 'col'), may hold values from -0.125 to 0.125
- up_tiles: bfloat16 [96, 8192, 128], P('row', 'col'), may hold values from -0.125 to 0.125
- down_tiles: bfloat16 [96, 8192, 128], P('row', 'col'), may hold values from -0.09375 to 0.09375
- tile_index: int32 [3, 96, 128], P(None, 'row', 'col'), may hold values from 0 to 3, as said below
- tile_counts: int32 [3, 16, 64], P(None, 'row', 'col'), may hold values from 1 to 6, as said below
Outputs:
- output: bfloat16 [640, 8192], P('col', 'row')
- input_grad: bfloat16 [640, 8192], P('col', 'row')
- gate_grad: float32 [96, 8192, 128], P('row', 'col')
- up_grad: float32 [96, 8192, 128], P('row', 'col')
- down_grad: float32 [96, 8192, 128], P('row', 'col')
Inputs may be any that keep to these rules, and one draw needn't show every extreme that they name: `tile_index`: within one matrix, row group and column group, the 6 slots name distinct block pairs; for gate and up the row block is below 4 and the column block below 2, for down the row block is below 2 and the column block below 4. `tile_counts`: for each matrix some row group and column group has all 6 slots live.
All inputs are finite; a program needn't handle non-finite values.
Results may differ from a plain program's by a relative error of at most 0.0049.
Values may be sent and summed in bfloat16 or wider, within the bound.
No kernel may reach another device: no remote copies, remote signals or barrier semaphores. Data moves between devices by JAX's collectives and lax.ppermute only.
A program may use at most 32 MiB of HBM per device.

v0:
```python
import jax
import jax.numpy as jnp
from jax import lax
from jax.sharding import PartitionSpec as P

FF = 16384


def pick_blocks(data_rows, block_ids, tile_size):
    token_count = data_rows.shape[0]
    block_count = data_rows.shape[1] // tile_size
    split_rows = data_rows.reshape(token_count, block_count, tile_size)
    select = (block_ids[:, None] == jnp.arange(block_count)[None, :]).astype(jnp.bfloat16)
    picked = jnp.einsum("tbk,sb->tsk", split_rows, select, preferred_element_type=jnp.float32)
    return picked.astype(jnp.bfloat16)


def place_blocks(products, block_ids, live_mask, block_count):
    select = ((block_ids[:, None] == jnp.arange(block_count)[None, :]) & live_mask[:, None]).astype(
        jnp.float32
    )
    placed = jnp.einsum("tsn,sc->tcn", products, select, precision=lax.Precision.HIGHEST)
    return placed.reshape(products.shape[0], block_count * products.shape[2])


def sparse_apply(data_rows, tiles, in_ids, out_ids, live_mask, out_count):
    picked = pick_blocks(data_rows, in_ids, tiles.shape[-1])
    products = jnp.einsum("tsk,skn->tsn", picked, tiles, preferred_element_type=jnp.float32)
    return place_blocks(products, out_ids, live_mask, out_count)


def sparse_apply_back(data_rows, tiles, in_ids, out_ids, live_mask, out_count):
    picked = pick_blocks(data_rows, in_ids, tiles.shape[-1])
    products = jnp.einsum("tsn,skn->tsk", picked, tiles, preferred_element_type=jnp.float32)
    return place_blocks(products, out_ids, live_mask, out_count)


def tile_grads(left_rows, right_rows, left_ids, right_ids, live_mask, tile_size):
    left_picked = pick_blocks(left_rows, left_ids, tile_size)
    right_picked = pick_blocks(right_rows, right_ids, tile_size)
    gradient = jnp.einsum(
        "tsk,tsn->skn", left_picked, right_picked, preferred_element_type=jnp.float32
    )
    return jnp.where(live_mask[:, None, None], gradient, jnp.zeros_like(gradient))


def gated_units(gate_sum, up_sum, hidden_grad):
    sigmoid_gate = jax.nn.sigmoid(gate_sum)
    active = gate_sum * sigmoid_gate
    hidden = (active * up_sum).astype(jnp.bfloat16)
    gate_act = (
        hidden_grad * up_sum * sigmoid_gate * (1.0 + gate_sum * (1.0 - sigmoid_gate))
    ).astype(jnp.bfloat16)
    up_act = (hidden_grad * active).astype(jnp.bfloat16)
    return (hidden, gate_act, up_act)


def body(tokens, cotangent, gate_tiles, up_tiles, down_tiles, tile_index, tile_counts):
    tile_size = gate_tiles.shape[-1]
    row_blocks = tokens.shape[1] // tile_size
    col_blocks = FF // lax.axis_size("col") // tile_size
    slot_ids = jnp.arange(gate_tiles.shape[0])
    gate_live = slot_ids < tile_counts[0, 0, 0]
    up_live = slot_ids < tile_counts[1, 0, 0]
    down_live = slot_ids < tile_counts[2, 0, 0]
    gate_in, gate_out = (tile_index[0, :, 0], tile_index[0, :, 1])
    up_in, up_out = (tile_index[1, :, 0], tile_index[1, :, 1])
    down_in, down_out = (tile_index[2, :, 0], tile_index[2, :, 1])
    whole_tokens, whole_cotangent = (
        lax.all_gather(tokens, "col", axis=0, tiled=True),
        lax.all_gather(cotangent, "col", axis=0, tiled=True),
    )
    gate_part = sparse_apply(whole_tokens, gate_tiles, gate_in, gate_out, gate_live, col_blocks)
    up_part = sparse_apply(whole_tokens, up_tiles, up_in, up_out, up_live, col_blocks)
    grad_part = sparse_apply_back(
        whole_cotangent, down_tiles, down_out, down_in, down_live, col_blocks
    )
    gate_sum, up_sum, hidden_grad = (
        lax.psum_scatter(gate_part, "row", scatter_dimension=0, tiled=True),
        lax.psum_scatter(up_part, "row", scatter_dimension=0, tiled=True),
        lax.psum_scatter(grad_part, "row", scatter_dimension=0, tiled=True),
    )
    hidden, gate_act, up_act = gated_units(gate_sum, up_sum, hidden_grad)
    hidden_all, gate_all, up_all = (
        lax.all_gather(hidden, "row", axis=0, tiled=True),
        lax.all_gather(gate_act, "row", axis=0, tiled=True),
        lax.all_gather(up_act, "row", axis=0, tiled=True),
    )
    output_part = sparse_apply(hidden_all, down_tiles, down_in, down_out, down_live, row_blocks)
    input_part = sparse_apply_back(gate_all, gate_tiles, gate_out, gate_in, gate_live, row_blocks)
    input_part = input_part + sparse_apply_back(
        up_all, up_tiles, up_out, up_in, up_live, row_blocks
    )
    output_sum, input_sum = (
        lax.psum_scatter(output_part, "col", scatter_dimension=0, tiled=True),
        lax.psum_scatter(input_part, "col", scatter_dimension=0, tiled=True),
    )
    output = output_sum.astype(jnp.bfloat16)
    input_grad = input_sum.astype(jnp.bfloat16)
    gate_grad = tile_grads(whole_tokens, gate_all, gate_in, gate_out, gate_live, tile_size)
    up_grad = tile_grads(whole_tokens, up_all, up_in, up_out, up_live, tile_size)
    down_grad = tile_grads(hidden_all, whole_cotangent, down_in, down_out, down_live, tile_size)
    return (output, input_grad, gate_grad, up_grad, down_grad)


def solution(mesh):
    return jax.shard_map(
        body,
        mesh=mesh,
        in_specs=(
            P("col", "row"),
            P("col", "row"),
            P("row", "col", None),
            P("row", "col", None),
            P("row", "col", None),
            P(None, "row", "col"),
            P(None, "row", "col"),
        ),
        out_specs=(
            P("col", "row"),
            P("col", "row"),
            P("row", "col", None),
            P("row", "col", None),
            P("row", "col", None),
        ),
        check_vma=False,
    )
```

profile of v0, /device:TPU:1, one launch (start us, length us, event | category | flops | bytes accessed | tf_op | source)
XLA Modules:
  0.0 771.7 jit_solution(1059762085911590073)
XLA Ops:
  7.2 1.4 fusion.70
  10.0 100.6 %all-gather = bf16[64,10,512]{2,1,0:T(8,128)(2,1)S(1)} all-gather(bf16[1,10,512]{2,1,0:T(8,128)(2,1)} %bitcast.131), channel_id=1, replica_groups=mesh['row'=16,'col'=64] {'col'}, dimensions={0}, use_global_device_ids=true | all-gather | bytes 665600 | tf_op jit(solution)/shard_map/all_gather | solution.py:70
  111.6 1.2 copy.36
  113.3 2.4 fusion.10
  115.7 0.9 copy.82
  117.3 1.8 copy.38
  119.7 1.7 convolution_bitcast_fusion.4
  121.4 2.4 fusion.8
  123.8 0.9 copy.81
  124.8 79.9 %all-gather.1 = bf16[64,10,512]{2,1,0:T(8,128)(2,1)S(1)} all-gather(bf16[1,10,512]{2,1,0:T(8,128)(2,1)S(1)} %bitcast.132), channel_id=1, replica_groups=mesh['row'=16,'col'=64] {'col'}, dimensions={0}, use_global_device_ids=true | all-gather | bytes 665600 | tf_op jit(solution)/shard_map/all_gather | solution.py:71
  206.8 2.4 fusion.4
  209.2 0.9 copy.80
  210.1 1.4 dynamic-slice
  212.2 38.8 %reduce-scatter.6.cloned.1.call-done = f32[40,256]{1,0:T(8,128)} async-done(((f32[640,256]{1,0:T(8,128)}), f32[40,256]{1,0:T(8,128)}) %reduce-scatter.6.cloned.1.call-update) | async-done | bytes 40976 | tf_op jit(solution)/shard_map/reduce_scatter | solution.py:80
  250.9 77.8 %reduce-scatter.8.cloned.1.call-done = f32[40,256]{1,0:T(8,128)} async-done(((f32[640,256]{1,0:T(8,128)}), f32[40,256]{1,0:T(8,128)}) %reduce-scatter.8.cloned.1.call-update) | async-done | bytes 40976 | tf_op jit(solution)/shard_map/reduce_scatter | solution.py:81
  328.8 0.8 multiply_convert_fusion.1
  329.6 24.8 %all_gather.19 = bf16[640,256]{1,0:T(8,128)(2,1)S(1)} all-gather(bf16[40,256]{1,0:T(8,128)(2,1)S(1)} %get-tuple-element.8), channel_id=1, replica_groups=mesh['row'=16,'col'=64] {'row'}, dimensions={0}, use_global_device_ids=true | all-gather | bytes 348160 | tf_op jit(solution)/shard_map/all_gather | solution.py:87
  355.2 1.2 convolution_select_fusion.1
  356.8 25.8 %all_gather.18 = bf16[640,256]{1,0:T(8,128)(2,1)S(1)} all-gather(bf16[40,256]{1,0:T(8,128)(2,1)S(1)} %get-tuple-element.7), channel_id=1, replica_groups=mesh['row'=16,'col'=64] {'row'}, dimensions={0}, use_global_device_ids=true | all-gather | bytes 348160 | tf_op jit(solution)/shard_map/all_gather | solution.py:86
  383.4 1.6 fusion.19
  385.0 1.2 convolution_select_fusion.2
  386.2 1.7 convolution_bitcast_fusion.1
  387.9 25.5 %all_gather.16 = bf16[640,256]{1,0:T(8,128)(2,1)S(1)} all-gather(bf16[40,256]{1,0:T(8,128)(2,1)S(1)} %get-tuple-element.9), channel_id=1, replica_groups=mesh['row'=16,'col'=64] {'row'}, dimensions={0}, use_global_device_ids=true | all-gather | bytes 348160 | tf_op jit(solution)/shard_map/all_gather | solution.py:85
  413.5 0.8 reshape.80
  414.3 1.6 fusion.18
  415.8 1.8 copy.40
  417.7 2.9 convolution_select_fusion
  421.1 2.4 fusion
  423.5 2.6 fusion.15
  426.1 2.4 fusion.6
  428.6 335.2 %all-reduce.4 = (bf16[640,512]{1,0:T(8,128)(2,1)S(1)}, bf16[640,512]{1,0:T(8,128)(2,1)}) all-reduce(f32[640,512]{1,0:T(8,128)S(1)} %bitcast.122, f32[640,512]{1,0:T(8,128)S(1)} %bitcast.121), channel_id=4, replica_groups=mesh['row'=16,'col'=64] {'col'}, use_global_device_ids=true, to_apply=%region_2.0.clone | all-reduce | flops 655360 | bytes 3932160
  763.8 1.4 dynamic-slice_convert_fusion
  (45 shorter events, 9.0 us)
Async XLA Ops:
  7.2 112.6 %copy-start = (bf16[6,128,128]{2,1,0:T(8,128)(2,1)S(1)}, bf16[6,128,128]{2,1,0:T(8,128)(2,1)}, u32[]{:S(2)}) copy-start(bf16[6,128,128]{2,1,0:T(8,128)(2,1)} %param.10) | copy-start | bytes 589828
  7.2 205.0 %reduce-scatter.4.cloned.1.call-start = ((), (), s32[]{:S(2)}) async-start(), calls=%async_computation.3 | async-start | bytes 696320 | tf_op jit(solution)/shard_map/reduce_scatter | solution.py:79
  111.0 1.8 copy-start.5
  116.6 134.4 %reduce-scatter.6.cloned.1.call-start = ((), (), s32[]{:S(2)}) async-start(), calls=%async_computation.4 | async-start | bytes 696320 | tf_op jit(solution)/shard_map/reduce_scatter | solution.py:80
  121.4 3.4 copy-start.9
  124.8 204.0 %reduce-scatter.8.cloned.1.call-start = ((), (), s32[]{:S(2)}) async-start(), calls=%async_computation.5 | async-start | bytes 696320 | tf_op jit(solution)/shard_map/reduce_scatter | solution.py:81
  204.7 1.6 copy-start.7
  206.4 2.8 copy-start.2
  210.1 145.1 %copy-start.3 = (bf16[640,6,128]{0,2,1:T(8,128)(2,1)S(1)}, bf16[640,6,128]{0,2,1:T(8,128)(2,1)}, u32[]{:S(2)}) copy-start(bf16[640,6,128]{0,2,1:T(8,128)(2,1)} %copy.38) | copy-start | bytes 2949124
  383.4 2.8 copy-start.6
  417.7 2.9 copy-start.4
  417.7 2.9 copy-start.8
  421.1 2.4 copy-start.1
Sparse Core Ops, SparseCore 0:
  116.7 56.2 reduce-scatter.3
  176.8 74.1 reduce-scatter.5
  254.3 74.4 reduce-scatter.7
where the time goes:
time: 776 us; the launch traced here: 772 us
  blocking collectives  592 us (76%)
  waiting for transfers between devices  117 us (15%)
  matrix products  30.6 us (4%)
  local copies, waits for them, and re-layouts  15 us (2%)
  between operations  14.7 us (2%)
    unnamed x1, blocking collectives  335 us
    all_gather x1, blocking collectives, body(): lax.all_gather(tokens, 'col', axis=0, tiled=True)  101 us
    all_gather x1, blocking collectives, body(): lax.all_gather(cotangent, 'col', axis=0, tiled=True)  79.9 us
    reduce_scatter x1, waiting for transfers between devices, body(): lax.psum_scatter(grad_part, 'row', scatter_dimension=0, tiled=True)  77.8 us
    reduce_scatter x1, waiting for transfers between devices, body(): lax.psum_scatter(up_part, 'row', scatter_dimension=0, tiled=True)  38.8 us
    all_gather x1, blocking collectives, body(): lax.all_gather(gate_act, 'row', axis=0, tiled=True)  25.8 us
    all_gather x1, blocking collectives, body(): lax.all_gather(hidden, 'row', axis=0, tiled=True)  25.5 us
    all_gather x1, blocking collectives, body(): lax.all_gather(up_act, 'row', axis=0, tiled=True)  24.8 us
  transfers between devices with their start and end apart: 3, of which 2 were waited for; matrix products, arithmetic and copies ran while one was open for 2% of the time, Pallas kernels for 0%

commit v1 on v0

v1 whole, which is shorter than its diff:
```python
import jax
import jax.numpy as jnp
from jax import lax
from jax.experimental import pallas as pl
from jax.experimental.pallas import tpu as pltpu
from jax.sharding import Mesh
from jax.sharding import PartitionSpec as P

F32 = jnp.float32
BF16 = jnp.bfloat16
VMEM = pl.BlockSpec(memory_space=pltpu.VMEM)
SMEM = pl.BlockSpec(memory_space=pltpu.SMEM)
NT = (((1,), (1,)), ((), ()))
TN = (((0,), (0,)), ((), ()))


def dot(left, right, dims=None):
    if dims is None:
        return jnp.dot(left, right, preferred_element_type=F32)
    return lax.dot_general(left, right, dims, preferred_element_type=F32)


def fill_weight(dense, tiles, index, counts, which):
    dense[...] = jnp.zeros_like(dense)
    side = tiles.shape[-1]
    for slot in range(tiles.shape[0]):

        @pl.when(slot < counts[which])
        def _():
            rows = pl.ds(pl.multiple_of(index[which, slot, 0] * side, side), side)
            cols = pl.ds(pl.multiple_of(index[which, slot, 1] * side, side), side)
            dense[rows, cols] = tiles[slot]


def take_tiles(out, dense, index, counts, which, col_offset=0):
    side = out.shape[-1]
    for slot in range(out.shape[0]):
        live = slot < counts[which]

        @pl.when(live)
        def _():
            rows = pl.ds(pl.multiple_of(index[which, slot, 0] * side, side), side)
            cols = pl.ds(
                pl.multiple_of(index[which, slot, 1] * side + col_offset, side), side
            )
            out[slot] = dense[rows, cols]

        @pl.when(jnp.logical_not(live))
        def _():
            out[slot] = jnp.zeros(out.shape[1:], out.dtype)


def spread_kernel(tokens, cotangent, out, stage):
    rows, lanes = tokens.shape
    side = out.shape[-1]
    for q in range(lanes // side):
        cols = slice(q * side, (q + 1) * side)
        stage[(2 * q) * rows : (2 * q + 1) * rows, :] = tokens[:, cols].astype(F32)
        stage[(2 * q + 1) * rows : (2 * q + 2) * rows, :] = cotangent[:, cols].astype(F32)
    block = stage[...].astype(out.dtype)
    for peer in range(out.shape[0]):
        out[peer] = block


def partial_kernel(
    index, counts, own_t, own_c, far_t, far_c, gate, up, down, out, w_gate, w_up, w_down
):
    fill_weight(w_gate, gate, index, counts, 0)
    fill_weight(w_up, up, index, counts, 1)
    fill_weight(w_down, down, index, counts, 2)
    half = own_t.shape[0]
    units = w_gate.shape[1]
    for start, toks, cots in ((0, own_t, own_c), (half, far_t, far_c)):
        rows = slice(start, start + half)
        out[rows, 0:units] = dot(toks[...], w_gate[...]).astype(out.dtype)
        out[rows, units : 2 * units] = dot(toks[...], w_up[...]).astype(out.dtype)
        out[rows, 2 * units :] = dot(cots[...], w_down[...], NT).astype(out.dtype)


def units_kernel(parts, out):
    total = parts[0].astype(F32)
    for peer in range(1, parts.shape[0]):
        total = total + parts[peer].astype(F32)
    units = total.shape[1] // 3
    gate_sum = total[:, 0:units]
    up_sum = total[:, units : 2 * units]
    hidden_grad = total[:, 2 * units :]
    sigmoid_gate = jax.nn.sigmoid(gate_sum)
    active = gate_sum * sigmoid_gate
    hidden = (active * up_sum).astype(out.dtype)
    gate_act = (
        hidden_grad * up_sum * sigmoid_gate * (1.0 + gate_sum * (1.0 - sigmoid_gate))
    ).astype(out.dtype)
    up_act = (hidden_grad * active).astype(out.dtype)
    for peer in range(out.shape[0]):
        out[peer, :, 0:units] = hidden
        out[peer, :, units : 2 * units] = gate_act
        out[peer, :, 2 * units :] = up_act


def apply_back(acts, rows, w_gate, w_up, w_down, out):
    units = w_gate.shape[1]
    lanes = w_gate.shape[0]
    out[:, 0:lanes] = dot(acts[rows, 0:units], w_down[...]).astype(out.dtype)
    out[:, lanes:] = (
        dot(acts[rows, units : 2 * units], w_gate[...], NT)
        + dot(acts[rows, 2 * units :], w_up[...], NT)
    ).astype(out.dtype)


def far_kernel(index, counts, acts, gate, up, down, out, w_gate, w_up, w_down):
    fill_weight(w_gate, gate, index, counts, 0)
    fill_weight(w_up, up, index, counts, 1)
    fill_weight(w_down, down, index, counts, 2)
    half = out.shape[0]
    apply_back(acts, slice(half, 2 * half), w_gate, w_up, w_down, out)


def own_kernel(index, counts, acts, gate, up, down, out, w_gate, w_up, w_down):
    fill_weight(w_gate, gate, index, counts, 0)
    fill_weight(w_up, up, index, counts, 1)
    fill_weight(w_down, down, index, counts, 2)
    apply_back(acts, slice(0, out.shape[0]), w_gate, w_up, w_down, out)


def grads_kernel(
    index, counts, acts, own_t, own_c, far_t, far_c, gate_out, up_out, down_out, dense, dense_down
):
    half = own_t.shape[0]
    units = dense_down.shape[0]
    dense[...] = dot(own_t[...], acts[0:half, units:], TN) + dot(far_t[...], acts[half:, units:], TN)
    dense_down[...] = dot(acts[0:half, 0:units], own_c[...], TN) + dot(
        acts[half:, 0:units], far_c[...], TN
    )
    take_tiles(gate_out, dense, index, counts, 0)
    take_tiles(up_out, dense, index, counts, 1, units)
    take_tiles(down_out, dense_down, index, counts, 2)


def finish_kernel(parts, output, input_grad):
    total = parts[0].astype(F32)
    for peer in range(1, parts.shape[0]):
        total = total + parts[peer].astype(F32)
    rows = output.shape[0]
    side = total.shape[1]
    chunks = output.shape[1] // side
    for q in range(chunks):
        cols = slice(q * side, (q + 1) * side)
        output[:, cols] = total[q * rows : (q + 1) * rows].astype(output.dtype)
        input_grad[:, cols] = total[(chunks + q) * rows : (chunks + q + 1) * rows].astype(
            input_grad.dtype
        )


def call(kernel, outs, specs, *args, scratch=(), flops=0):
    moved = sum(a.size * a.dtype.itemsize for a in args) + sum(
        o.size * jnp.dtype(o.dtype).itemsize for o in outs
    )
    return pl.pallas_call(
        kernel,
        out_shape=outs if len(outs) > 1 else outs[0],
        in_specs=specs,
        out_specs=(VMEM,) * len(outs) if len(outs) > 1 else VMEM,
        scratch_shapes=scratch,
        cost_estimate=pl.CostEstimate(flops=flops, bytes_accessed=moved, transcendentals=0),
    )(*args)


def body(tokens, cotangent, gate_tiles, up_tiles, down_tiles, tile_index, tile_counts):
    rows, lanes = tokens.shape
    slots, side, _ = gate_tiles.shape
    row_size = lax.axis_size("row")
    peers = lax.axis_size("yz")
    units = 2 * side
    chunks = lanes // side
    half = peers * rows
    share = 2 * half // row_size
    counts = tile_counts.reshape(3)
    shape = jax.ShapeDtypeStruct
    weights = (
        pltpu.VMEM((lanes, units), BF16),
        pltpu.VMEM((lanes, units), BF16),
        pltpu.VMEM((units, lanes), BF16),
    )
    swap = [(0, 1), (1, 0)]

    spread = call(
        spread_kernel,
        (shape((peers, 2 * chunks * rows, side), BF16),),
        (VMEM, VMEM),
        tokens,
        cotangent,
        scratch=(pltpu.VMEM((2 * chunks * rows, side), F32),),
    )
    own = lax.all_to_all(spread, "yz", split_axis=0, concat_axis=0, tiled=True)
    far = lax.ppermute(own, "core", swap)

    def unpack(blocks):
        split = blocks.reshape(peers, chunks, 2, rows, side).transpose(2, 0, 3, 1, 4)
        split = split.reshape(2, half, lanes)
        return split[0], split[1]

    own_t, own_c = unpack(own)
    far_t, far_c = unpack(far)
    parts = call(
        partial_kernel,
        (shape((2 * half, 3 * units), BF16),),
        (SMEM, SMEM) + (VMEM,) * 7,
        tile_index,
        counts,
        own_t,
        own_c,
        far_t,
        far_c,
        gate_tiles,
        up_tiles,
        down_tiles,
        scratch=weights,
        flops=12 * half * lanes * units,
    )
    parts = parts.reshape(row_size, share, 3 * units)
    parts = lax.all_to_all(parts, "row", split_axis=0, concat_axis=0, tiled=True)
    acts = call(units_kernel, (shape(parts.shape, BF16),), (VMEM,), parts)
    acts = lax.all_to_all(acts, "row", split_axis=0, concat_axis=0, tiled=True)
    acts = acts.reshape(2 * half, 3 * units)

    weight_args = (tile_index, counts, acts, gate_tiles, up_tiles, down_tiles)
    weight_specs = (SMEM, SMEM) + (VMEM,) * 4
    far_part = call(
        far_kernel,
        (shape((half, 2 * lanes), BF16),),
        weight_specs,
        *weight_args,
        scratch=weights,
        flops=6 * half * lanes * units,
    )
    far_part = lax.ppermute(far_part, "core", swap)
    own_part = call(
        own_kernel,
        (shape((half, 2 * lanes), F32),),
        weight_specs,
        *weight_args,
        scratch=weights,
        flops=6 * half * lanes * units,
    )
    tile_shape = shape((slots, side, side), F32)
    gate_grad, up_grad, down_grad = call(
        grads_kernel,
        (tile_shape,) * 3,
        (SMEM, SMEM) + (VMEM,) * 5,
        tile_index,
        counts,
        acts,
        own_t,
        own_c,
        far_t,
        far_c,
        scratch=(pltpu.VMEM((lanes, 2 * units), F32), pltpu.VMEM((units, lanes), F32)),
        flops=12 * half * lanes * units,
    )
    both = own_part + far_part.astype(F32)
    both = both.reshape(peers, rows, 2 * chunks, side).transpose(0, 2, 1, 3)
    both = both.reshape(peers, 2 * chunks * rows, side).astype(BF16)
    both = lax.all_to_all(both, "yz", split_axis=0, concat_axis=0, tiled=True)
    output, input_grad = call(
        finish_kernel,
        (shape((rows, lanes), BF16),) * 2,
        (VMEM,),
        both,
    )
    return (output, input_grad, gate_grad, up_grad, down_grad)


def solution(mesh):
    row_size, col_size = mesh.shape["row"], mesh.shape["col"]
    split = Mesh(
        mesh.devices.reshape(row_size, col_size // 2, 2), ("row", "yz", "core")
    )
    col = ("yz", "core")
    blocks = P(col, "row")
    tiles = P("row", col, None)
    small = P(None, "row", col)
    return jax.shard_map(
        body,
        mesh=split,
        in_specs=(blocks, blocks, tiles, tiles, tiles, small, small),
        out_specs=(blocks, blocks, tiles, tiles, tiles),
        check_vma=False,
    )
```

time: 776 us -> 167 us (0.22)
  blocking collectives: 592 us -> 104 us
  waiting for transfers between devices: 117 us -> 17.4 us
  matrix products: 30.6 us -> 0 us
  Pallas kernels: 0 us -> 18.8 us
  starting transfers between devices: 0.12 us -> 17.4 us
  between operations: 14.7 us -> 0.75 us
  local copies, waits for them, and re-layouts: 15 us -> 6.27 us
    unnamed x1 -> x0, blocking collectives: 335 us -> none
    all_gather x5 -> x0, blocking collectives: 257 us -> none  [the longest x1 101 us: body(): lax.all_gather(tokens, 'col', axis=0, tiled=True)]
    reduce_scatter x3 -> x0, waiting for transfers between devices: 117 us -> none  [the longest x1 77.8 us: body(): lax.psum_scatter(grad_part, 'row', scatter_dimension=0, tiled=True)]
    all_to_all x0 -> x3, blocking collectives: none -> 104 us  [the longest x1 43.2 us: body(): own = lax.all_to_all(spread, 'yz', split_axis=0, concat_axis=0, tiled=True)]
    dot_general x21 -> x0, matrix products: 30.6 us -> none  [the longest x6 14.5 us: place_blocks(): jnp.einsum('tsn,sc->tcn', products, select, precision=lax.Precision.HIGHEST)]
    pallas_call x0 -> x7, Pallas kernels: none -> 18.8 us  [call(): pl.pallas_call(kernel, out_shape=outs if len(outs) > 1 else outs[0], in_s...]
    all_to_all x0 -> x1, waiting for transfers between devices: none -> 17.4 us  [body(): both = lax.all_to_all(both, 'yz', split_axis=0, concat_axis=0, tiled=True)]
    ppermute x0 -> x2, starting transfers between devices: none -> 10.8 us  [the longest x1 6.41 us: body(): far_part = lax.ppermute(far_part, 'core', swap)]
  transfers between devices with their start and end apart: 3 -> 3, of which waited for: 2 -> 1; matrix products, arithmetic and copies ran while one was open for 2% -> 1% of each run, Pallas kernels for 0% -> 4%
where the time goes in v1:
time: 167 us
  blocking collectives  104 us (62%)
  Pallas kernels  18.8 us (11%)
  starting transfers between devices  17.4 us (10%)
  waiting for transfers between devices  17.4 us (10%)
  local copies, waits for them, and re-layouts  6.27 us (4%)
    all_to_all x1, blocking collectives, body(): own = lax.all_to_all(spread, 'yz', split_axis=0, concat_axis=0, tiled=True)  43.2 us
    all_to_all x1, blocking collectives, body(): lax.all_to_all(parts, 'row', split_axis=0, concat_axis=0, tiled=True)  33 us
    all_to_all x1, blocking collectives, body(): acts = lax.all_to_all(acts, 'row', split_axis=0, concat_axis=0, tiled=True)  28.1 us
    pallas_call x7, Pallas kernels, call(): pl.pallas_call(kernel, out_shape=outs if len(outs) > 1 else outs[0], in_s...  18.8 us
    all_to_all x1, waiting for transfers between devices, body(): both = lax.all_to_all(both, 'yz', split_axis=0, concat_axis=0, tiled=True)  17.4 us
    all_to_all x1, starting transfers between devices, body(): both = lax.all_to_all(both, 'yz', split_axis=0, concat_axis=0, tiled=True)  6.56 us
    ppermute x1, starting transfers between devices, body(): far_part = lax.ppermute(far_part, 'core', swap)  6.41 us
    ppermute x1, starting transfers between devices, body(): far = lax.ppermute(own, 'core', swap)  4.43 us
  transfers between devices with their start and end apart: 3, of which 1 were waited for; matrix products, arithmetic and copies ran while one was open for 1% of the time, Pallas kernels for 4%

profile of v1, /device:TPU:1, one launch (start us, length us, event | category | flops | bytes accessed | tf_op | source)
XLA Modules:
  0.0 166.6 jit_solution(3144796476494229168)
XLA Ops:
  0.6 0.0 copy-start.1
  0.6 1.6 shard_map.110
  2.3 43.2 %all_to_all.20 = bf16[32,80,128]{2,1,0:T(8,128)(2,1)S(1)} all-to-all(bf16[32,80,128]{2,1,0:T(8,128)(2,1)} %shard_map.110), channel_id=1, replica_groups=mesh['row'=16,'yz'=32,'core'=2] {'yz'}, dimensions={0} | all-to-all | bytes 1310720 | tf_op jit(solution)/shard_map/all_to_all | solution.py:195
  45.5 4.4 %collective-permute-start = (bf16[32,80,128]{2,1,0:T(8,128)(2,1)S(1)}, bf16[32,80,128]{2,1,0:T(8,128)(2,1)S(1)}, u32[]{:S(2)}, u32[]{:S(2)}) collective-permute-start(bf16[32,80,128]{2,1,0:T(8,128)(2,1)S(1)} %all_to_all.20), channel_id=1, source_target_pairs={{0,1},{1,0},{2,3},{3,2},{4,5},{5,4},{6,7},{7,6},{8,9},{9,8},{10,11... | collective-permute-start | bytes 1966088 | tf_op jit(solution)/shard_map/ppermute | solution.py:196
  49.9 0.0 copy-done.1
  49.9 0.7 copy.26.index
  50.6 0.2 copy.19
  50.9 0.3 copy.21
  51.1 0.3 copy.20
  51.4 0.9 copy_bitcast_fusion.2
  52.3 0.0 collective-permute-done
  52.3 0.2 copy.22
  52.6 0.3 copy.24
  52.8 0.3 copy.23
  53.1 0.9 copy_bitcast_fusion
  54.0 3.3 %shard_map.111 = bf16[640,768]{1,0:T(8,128)(2,1)} custom-call(s32[3,6,2]{2,1,0:T(8,128)} %copy.26.index, s32[3]{0:T(128)} %bitcast.44, bf16[320,512]{1,0:T(8,128)(2,1)} %get-tuple-element.22.own_t, bf16[320,512]{1,0:T(8,128)(2,1)} %get-tuple-element.21.own_c, bf16[320,512]{1,0:T(8,128)(2,1)} %get-tuple-element.20.far_t, ...), custom_call_target="tpu_custom_call" | custom-call | flops 503316480 | bytes 2883740 | tf_op jit(solution)/shard_map/pallas_call | solution.py:159
  57.3 33.0 %all_to_all.21.parts = bf16[16,40,768]{2,1,0:T(8,128)(2,1)} all-to-all(bf16[16,40,768]{2,1,0:T(8,128)(2,1)} %bitcast.35), channel_id=1, replica_groups=mesh['row'=16,'yz'=32,'core'=2] {'row'}, dimensions={0} | all-to-all | bytes 1966080 | tf_op jit(solution)/shard_map/all_to_all | solution.py:222
  90.3 2.3 %shard_map.112 = bf16[16,40,768]{2,1,0:T(8,128)(2,1)} custom-call(bf16[16,40,768]{2,1,0:T(8,128)(2,1)} %all_to_all.21.parts), custom_call_target="tpu_custom_call" | custom-call | bytes 1966080 | tf_op jit(solution)/shard_map/pallas_call | solution.py:159
  92.6 28.1 %all_to_all.22 = bf16[16,40,768]{2,1,0:T(8,128)(2,1)} all-to-all(bf16[16,40,768]{2,1,0:T(8,128)(2,1)} %shard_map.112), channel_id=1, replica_groups=mesh['row'=16,'yz'=32,'core'=2] {'row'}, dimensions={0} | all-to-all | bytes 1966080 | tf_op jit(solution)/shard_map/all_to_all | solution.py:224
  120.8 2.9 %shard_map.114 = bf16[320,1024]{1,0:T(8,128)(2,1)} custom-call(s32[3,6,2]{2,1,0:T(8,128)} %copy.26.index, s32[3]{0:T(128)} %bitcast.45, bf16[640,768]{1,0:T(8,128)(2,1)} %bitcast.32, bf16[6,128,128]{2,1,0:T(8,128)(2,1)} %gate.5, bf16[6,128,128]{2,1,0:T(8,128)(2,1)} %up.5, bf16[6,128,128]{2,1,0:T(8,128)(2,1)} %down.5), custom_call_target="tpu_custom_call" | custom-call | flops 251658240 | bytes 2228380 | tf_op jit(solution)/shard_map/pallas_call | solution.py:159
  123.6 6.4 %collective-permute-start.1 = (bf16[320,1024]{1,0:T(8,128)(2,1)}, bf16[320,1024]{1,0:T(8,128)(2,1)S(1)}, u32[]{:S(2)}, u32[]{:S(2)}) collective-permute-start(bf16[320,1024]{1,0:T(8,128)(2,1)} %shard_map.114), channel_id=1, source_target_pairs={{0,1},{1,0},{2,3},{3,2},{4,5},{5,4},{6,7},{7,6},{8,9},{9,8},{10,11... | collective-permute-start | bytes 1966088 | tf_op jit(solution)/shard_map/ppermute | solution.py:237
  130.0 3.1 %shard_map.113 = f32[320,1024]{1,0:T(8,128)} custom-call(s32[3,6,2]{2,1,0:T(8,128)} %copy.26.index, s32[3]{0:T(128)} %bitcast.46, bf16[640,768]{1,0:T(8,128)(2,1)} %bitcast.33, bf16[6,128,128]{2,1,0:T(8,128)(2,1)} %gate.5, bf16[6,128,128]{2,1,0:T(8,128)(2,1)} %up.5, bf16[6,128,128]{2,1,0:T(8,128)(2,1)} %down.5), custom_call_target="tpu_custom_call" | custom-call | flops 251658240 | bytes 2883740 | tf_op jit(solution)/shard_map/pallas_call | solution.py:159
  133.1 0.0 collective-permute-done.1
  133.1 1.5 fusion
  134.6 0.1 copy.35
  134.8 0.2 copy.28
  134.9 1.1 copy.29
  136.1 6.6 %all-to-all-start.3 = ((bf16[32,80,128]{2,1,0:T(8,128)(2,1)}), bf16[32,80,128]{2,1,0:T(8,128)(2,1)S(1)}, u32[]{:S(2)}, u32[]{:S(2)}) async-start(bf16[32,80,128]{2,1,0:T(8,128)(2,1)} %copy.29), calls=%async_computation.3 | async-start | bytes 1310720 | tf_op jit(solution)/shard_map/all_to_all | solution.py:264
  142.6 3.9 %shard_map.116 = (f32[6,128,128]{2,1,0:T(8,128)}, f32[6,128,128]{2,1,0:T(8,128)}, f32[6,128,128]{2,1,0:T(8,128)}) custom-call(s32[3,6,2]{2,1,0:T(8,128)} %copy.26.index, s32[3]{0:T(128)} %bitcast.47, bf16[640,768]{1,0:T(8,128)(2,1)} %bitcast.34, bf16[320,512]{1,0:T(8,128)(2,1)} %get-tuple-element.22.own_t, bf16[320,512]{1,0:T(8,128)(2,1)} %get-tuple-element.21.own_c, ...), custom_call_target="tpu_custom_call" | custom-call | flops 503316480 | bytes 3473564 | tf_op jit(solution)/shard_map/pallas_call | solution.py:159
  146.5 17.4 %all-to-all-done.3.parts = bf16[32,80,128]{2,1,0:T(8,128)(2,1)S(1)} async-done(((bf16[32,80,128]{2,1,0:T(8,128)(2,1)}), bf16[32,80,128]{2,1,0:T(8,128)(2,1)S(1)}, u32[]{:S(2)}, u32[]{:S(2)}) %all-to-all-start.3) | async-done | bytes 655392 | tf_op jit(solution)/shard_map/all_to_all | solution.py:264
  163.9 0.8 copy-done
  164.8 1.8 %shard_map.115 = (bf16[10,512]{1,0:T(8,128)(2,1)}, bf16[10,512]{1,0:T(8,128)(2,1)}) custom-call(bf16[32,80,128]{2,1,0:T(8,128)(2,1)} %copy-done), custom_call_target="tpu_custom_call" | custom-call | bytes 675840 | tf_op jit(solution)/shard_map/pallas_call | solution.py:159
  (3 shorter events, 0.1 us)
Async XLA Ops:
  0.6 49.3 %copy-start.1 = (s32[3,6,2]{1,2,0:T(2,128)S(1)}, s32[3,6,2]{1,2,0:T(2,128)}, u32[]{:S(2)}) copy-start(s32[3,6,2]{1,2,0:T(2,128)} %param.12) | copy-start | bytes 436
  45.5 6.8 %collective-permute-start = (bf16[32,80,128]{2,1,0:T(8,128)(2,1)S(1)}, bf16[32,80,128]{2,1,0:T(8,128)(2,1)S(1)}, u32[]{:S(2)}, u32[]{:S(2)}) collective-permute-start(bf16[32,80,128]{2,1,0:T(8,128)(2,1)S(1)} %all_to_all.20), channel_id=1, source_target_pairs={{0,1},{1,0},{2,3},{3,2},{4,5},{5,4},{6,7},{7,6},{8,9},{9,8},{10,11... | collective-permute-start | bytes 1966088 | tf_op jit(solution)/shard_map/ppermute | solution.py:196
  123.6 9.5 %collective-permute-start.1 = (bf16[320,1024]{1,0:T(8,128)(2,1)}, bf16[320,1024]{1,0:T(8,128)(2,1)S(1)}, u32[]{:S(2)}, u32[]{:S(2)}) collective-permute-start(bf16[320,1024]{1,0:T(8,128)(2,1)} %shard_map.114), channel_id=1, source_target_pairs={{0,1},{1,0},{2,3},{3,2},{4,5},{5,4},{6,7},{7,6},{8,9},{9,8},{10,11... | collective-permute-start | bytes 1966088 | tf_op jit(solution)/shard_map/ppermute | solution.py:237
  136.1 27.9 %all-to-all-start.3 = ((bf16[32,80,128]{2,1,0:T(8,128)(2,1)}), bf16[32,80,128]{2,1,0:T(8,128)(2,1)S(1)}, u32[]{:S(2)}, u32[]{:S(2)}) async-start(bf16[32,80,128]{2,1,0:T(8,128)(2,1)} %copy.29), calls=%async_computation.3 | async-start | bytes 1310720 | tf_op jit(solution)/shard_map/all_to_all | solution.py:264
  163.9 0.8 copy-start

commit v2 on v1

v2 whole, which is shorter than its diff:
```python
import jax
import jax.numpy as jnp
from jax import lax
from jax.experimental import pallas as pl
from jax.experimental.pallas import tpu as pltpu
from jax.sharding import Mesh
from jax.sharding import PartitionSpec as P

F32 = jnp.float32
BF16 = jnp.bfloat16
VMEM = pl.BlockSpec(memory_space=pltpu.VMEM)
SMEM = pl.BlockSpec(memory_space=pltpu.SMEM)
NT = (((1,), (1,)), ((), ()))
TN = (((0,), (0,)), ((), ()))


def dot(left, right, dims=None):
    if dims is None:
        return jnp.dot(left, right, preferred_element_type=F32)
    return lax.dot_general(left, right, dims, preferred_element_type=F32)


def place_tiles(dense, tiles, index, counts, which, row_offset, col_offset):
    side = tiles.shape[-1]
    for slot in range(tiles.shape[0]):

        @pl.when(slot < counts[which])
        def _():
            row = pl.multiple_of(index[which, slot, 0] * side + row_offset, side)
            col = pl.multiple_of(index[which, slot, 1] * side + col_offset, side)
            dense[pl.ds(row, side), pl.ds(col, side)] = tiles[slot]


def weights_kernel(index, counts, gate, up, down, dense):
    lanes = dense.shape[1]
    dense[...] = jnp.zeros_like(dense)
    place_tiles(dense, gate, index, counts, 0, 0, 0)
    place_tiles(dense, up, index, counts, 1, 0, lanes // 2)
    place_tiles(dense, down, index, counts, 2, lanes, 0)


def take_tiles(out, own, far, index, counts, which, row_offset, col_offset):
    side = out.shape[-1]
    for slot in range(out.shape[0]):
        live = slot < counts[which]

        @pl.when(live)
        def _():
            row = pl.multiple_of(index[which, slot, 0] * side + row_offset, side)
            col = pl.multiple_of(index[which, slot, 1] * side + col_offset, side)
            place = (pl.ds(row, side), pl.ds(col, side))
            out[slot] = own[place] + far[place].astype(out.dtype)

        @pl.when(jnp.logical_not(live))
        def _():
            out[slot] = jnp.zeros(out.shape[1:], out.dtype)


def tiles_kernel(index, counts, own, far, gate_out, up_out, down_out):
    lanes = own.shape[1]
    take_tiles(gate_out, own, far, index, counts, 0, 0, 0)
    take_tiles(up_out, own, far, index, counts, 1, 0, lanes // 2)
    take_tiles(down_out, own, far, index, counts, 2, lanes, 0)


def spread_kernel(tokens, cotangent, out, stage):
    rows, lanes = tokens.shape
    side = out.shape[-1]
    chunks = lanes // side
    for start, block in ((0, tokens), (chunks, cotangent)):
        for q in range(chunks):
            piece = block[:, q * side : (q + 1) * side].astype(F32)
            stage[(start + q) * rows : (start + q + 1) * rows, :] = piece
    packed = stage[...].astype(out.dtype)
    for peer in range(out.shape[0]):
        out[peer] = packed


def partial_kernel(blocks, own, far, out, tokens, cotangent, stage):
    peers = blocks.shape[0]
    half, lanes = tokens.shape
    side = blocks.shape[-1]
    rows = half // peers
    chunks = lanes // side
    for peer in range(peers):
        block = blocks[peer].astype(F32)
        for q in range(2 * chunks):
            stage[peer * rows : (peer + 1) * rows, q * side : (q + 1) * side] = block[
                q * rows : (q + 1) * rows
            ]
    tokens[...] = stage[:, 0:lanes].astype(tokens.dtype)
    cotangent[...] = stage[:, lanes:].astype(cotangent.dtype)
    for start, weights in ((0, own), (half, far)):
        out[start : start + half, 0:lanes] = dot(tokens[...], weights[0:lanes, :]).astype(out.dtype)
        out[start : start + half, lanes:] = dot(cotangent[...], weights[lanes:, :], NT).astype(
            out.dtype
        )


def sum_parts(parts):
    total = parts[0].astype(F32)
    for peer in range(1, parts.shape[0]):
        total = total + parts[peer].astype(F32)
    return total


def units_kernel(parts, out):
    total = sum_parts(parts)
    units = total.shape[1] // 3
    gate_sum = total[:, 0:units]
    up_sum = total[:, units : 2 * units]
    hidden_grad = total[:, 2 * units :]
    sigmoid_gate = jax.nn.sigmoid(gate_sum)
    active = gate_sum * sigmoid_gate
    hidden = (active * up_sum).astype(out.dtype)
    gate_act = (
        hidden_grad * up_sum * sigmoid_gate * (1.0 + gate_sum * (1.0 - sigmoid_gate))
    ).astype(out.dtype)
    up_act = (hidden_grad * active).astype(out.dtype)
    for peer in range(out.shape[0]):
        out[peer, :, 0:units] = hidden
        out[peer, :, units : 2 * units] = gate_act
        out[peer, :, 2 * units :] = up_act


def apply_kernel(acts, own, far, out, result, stage):
    half = result.shape[0]
    lanes = own.shape[1]
    units = own.shape[0] - lanes
    peers = out.shape[0]
    side = out.shape[-1]
    rows = half // peers
    near, other = slice(0, half), slice(half, 2 * half)
    result[:, 0:lanes] = dot(acts[near, 0:units], own[lanes:, :]) + dot(
        acts[other, 0:units], far[lanes:, :]
    )
    result[:, lanes:] = dot(acts[near, units:], own[0:lanes, :], NT) + dot(
        acts[other, units:], far[0:lanes, :], NT
    )
    for peer in range(peers):
        for q in range(2 * lanes // side):
            stage[peer, q * rows : (q + 1) * rows, :] = result[
                peer * rows : (peer + 1) * rows, q * side : (q + 1) * side
            ]
        out[peer] = stage[peer].astype(out.dtype)


def grads_kernel(acts, tokens, cotangent, own, far):
    half, lanes = tokens.shape
    units = own.shape[0] - lanes
    for start, out in ((half, far), (0, own)):
        rows = slice(start, start + half)
        out[0:lanes, :] = dot(tokens[...], acts[rows, units:], TN).astype(out.dtype)
        out[lanes:, :] = dot(acts[rows, 0:units], cotangent[...], TN).astype(out.dtype)


def finish_kernel(parts, output, input_grad):
    total = sum_parts(parts)
    rows, lanes = output.shape
    side = total.shape[1]
    chunks = lanes // side
    for start, out in ((0, output), (chunks, input_grad)):
        for q in range(chunks):
            piece = total[(start + q) * rows : (start + q + 1) * rows]
            out[:, q * side : (q + 1) * side] = piece.astype(out.dtype)


def call(kernel, outs, args, smem=0, scratch=(), flops=0):
    moved = sum(a.size * a.dtype.itemsize for a in args) + sum(
        o.size * jnp.dtype(o.dtype).itemsize for o in outs
    )
    single = len(outs) == 1
    return pl.pallas_call(
        kernel,
        out_shape=outs[0] if single else outs,
        in_specs=(SMEM,) * smem + (VMEM,) * (len(args) - smem),
        out_specs=VMEM if single else (VMEM,) * len(outs),
        scratch_shapes=scratch,
        compiler_params=pltpu.CompilerParams(vmem_limit_bytes=20 << 20),
        cost_estimate=pl.CostEstimate(flops=flops, bytes_accessed=moved, transcendentals=0),
    )(*args)


def exchange(blocks, axis):
    return lax.all_to_all(blocks, axis, split_axis=0, concat_axis=0, tiled=True)


def swap(block):
    return lax.ppermute(block, "core", [(0, 1), (1, 0)])


def body(tokens, cotangent, gate_tiles, up_tiles, down_tiles, tile_index, tile_counts):
    rows, lanes = tokens.shape
    slots, side, _ = gate_tiles.shape
    row_size = lax.axis_size("row")
    peers = lax.axis_size("yz")
    units = 2 * side
    half = peers * rows
    share = 2 * half // row_size
    packed = 2 * lanes // side * rows
    flops = 12 * half * lanes * units
    counts = tile_counts.reshape(3)
    shape = jax.ShapeDtypeStruct

    spread = call(
        spread_kernel,
        (shape((peers, packed, side), BF16),),
        (tokens, cotangent),
        scratch=(pltpu.VMEM((packed, side), F32),),
    )
    blocks = exchange(spread, "yz")
    own = call(
        weights_kernel,
        (shape((lanes + units, lanes), BF16),),
        (tile_index, counts, gate_tiles, up_tiles, down_tiles),
        smem=2,
    )
    far = swap(own)
    parts, all_tokens, all_cotangent = call(
        partial_kernel,
        (
            shape((2 * half, 3 * units), BF16),
            shape((half, lanes), BF16),
            shape((half, lanes), BF16),
        ),
        (blocks, own, far),
        scratch=(pltpu.VMEM((half, 2 * lanes), F32),),
        flops=flops,
    )
    parts = exchange(parts.reshape(row_size, share, 3 * units), "row")
    acts = call(units_kernel, (shape(parts.shape, BF16),), (parts,))
    acts = exchange(acts, "row").reshape(2 * half, 3 * units)
    sums = call(
        apply_kernel,
        (shape((peers, packed, side), BF16),),
        (acts, own, far),
        scratch=(pltpu.VMEM((half, 2 * lanes), F32), pltpu.VMEM((peers, packed, side), F32)),
        flops=flops,
    )
    acts, sums = lax.optimization_barrier((acts, sums))
    sums = exchange(sums, "yz")
    own_grad, far_grad = call(
        grads_kernel,
        (shape((lanes + units, lanes), F32), shape((lanes + units, lanes), BF16)),
        (acts, all_tokens, all_cotangent),
        flops=flops,
    )
    gate_grad, up_grad, down_grad = call(
        tiles_kernel,
        (shape((slots, side, side), F32),) * 3,
        (tile_index, counts, own_grad, swap(far_grad)),
        smem=2,
    )
    sums, gate_grad, up_grad, down_grad = lax.optimization_barrier(
        (sums, gate_grad, up_grad, down_grad)
    )
    output, input_grad = call(finish_kernel, (shape((rows, lanes), BF16),) * 2, (sums,))
    return (output, input_grad, gate_grad, up_grad, down_grad)


def solution(mesh):
    row_size, col_size = mesh.shape["row"], mesh.shape["col"]
    split = Mesh(
        mesh.devices.reshape(row_size, col_size // 2, 2), ("row", "yz", "core")
    )
    col = ("yz", "core")
    blocks = P(col, "row")
    tiles = P("row", col, None)
    small = P(None, "row", col)
    return jax.shard_map(
        body,
        mesh=split,
        in_specs=(blocks, blocks, tiles, tiles, tiles, small, small),
        out_specs=(blocks, blocks, tiles, tiles, tiles),
        check_vma=False,
    )
```

time: 167 us -> 142 us (0.85)
  blocking collectives: 104 us -> 56.9 us
  starting transfers between devices: 17.4 us -> 44 us
  waiting for transfers between devices: 17.4 us -> 29.4 us
  Pallas kernels: 18.8 us -> 8.32 us
  local copies, waits for them, and re-layouts: 6.27 us -> 1.6 us
    all_to_all x3 -> x2, blocking collectives: 104 us -> 56.9 us  [exchange(): return lax.all_to_all(blocks, axis, split_axis=0, concat_axis=0, tiled=True)]
    all_to_all x1 -> x2, starting transfers between devices: 6.56 us -> 36.5 us  [exchange(): return lax.all_to_all(blocks, axis, split_axis=0, concat_axis=0, tiled=True)]
    pallas_call x7 -> x8, Pallas kernels: 18.8 us -> 8.32 us  [call(): pl.pallas_call(kernel, out_shape=outs[0] if single else outs, in_specs=(S...]
    all_to_all x1 -> x2, waiting for transfers between devices: 17.4 us -> 25.6 us  [exchange(): return lax.all_to_all(blocks, axis, split_axis=0, concat_axis=0, tiled=True)]
    ppermute x2, waiting for transfers between devices: 0.01 us -> 3.78 us  [swap(): return lax.ppermute(block, 'core', [(0, 1), (1, 0)])]
    ppermute x2, starting transfers between devices: 10.8 us -> 7.43 us  [swap(): return lax.ppermute(block, 'core', [(0, 1), (1, 0)])]
    squeeze x2 -> x0, local copies, waits for them, and re-layouts: 1.87 us -> none  [unpack(): return (split[0], split[1])]
  transfers between devices with their start and end apart: 3 -> 4, of which waited for: 1 -> 4; matrix products, arithmetic and copies ran while one was open for 1% -> 0% of each run, Pallas kernels for 4% -> 3%
where the time goes in v2:
time: 142 us; the launch traced here: 141 us
  blocking collectives  56.9 us (40%)
  starting transfers between devices  44 us (31%)
  waiting for transfers between devices  29.4 us (21%)
  Pallas kernels  8.32 us (6%)
  local copies, waits for them, and re-layouts  1.6 us (1%)
    all_to_all x2, blocking collectives, exchange(): return lax.all_to_all(blocks, axis, split_axis=0, concat_axis=0, tiled=True)  56.9 us
    all_to_all x2, starting transfers between devices, exchange(): return lax.all_to_all(blocks, axis, split_axis=0, concat_axis=0, tiled=True)  36.5 us
    all_to_all x2, waiting for transfers between devices, exchange(): return lax.all_to_all(blocks, axis, split_axis=0, concat_axis=0, tiled=True)  25.6 us
    pallas_call x8, Pallas kernels, call(): pl.pallas_call(kernel, out_shape=outs[0] if single else outs, in_specs=(S...  8.32 us
    ppermute x2, starting transfers between devices, swap(): return lax.ppermute(block, 'core', [(0, 1), (1, 0)])  7.43 us
    ppermute x2, waiting for transfers between devices, swap(): return lax.ppermute(block, 'core', [(0, 1), (1, 0)])  3.78 us
  transfers between devices with their start and end apart: 4, of which 4 were waited for; matrix products, arithmetic and copies ran while one was open for 0% of the time, Pallas kernels for 3%

profile of v2, /device:TPU:1, one launch (start us, length us, event | category | flops | bytes accessed | tf_op | source)
XLA Modules:
  0.0 140.9 jit_solution(6302818465428904889)
XLA Ops:
  0.6 0.0 copy-start.2
  0.6 0.0 copy-start.1
  0.7 0.0 copy-start.3
  0.7 0.8 copy-done.3
  1.4 0.0 copy-start.4
  1.4 0.7 copy-done.4
  2.1 0.0 copy-start.6
  2.1 0.0 copy-start
  2.1 0.9 shard_map.110
  3.0 23.3 %all-to-all-start = ((bf16[32,80,128]{2,1,0:T(8,128)(2,1)}), bf16[32,80,128]{2,1,0:T(8,128)(2,1)S(1)}, u32[]{:S(2)}, u32[]{:S(2)}) async-start(bf16[32,80,128]{2,1,0:T(8,128)(2,1)} %shard_map.110), calls=%async_computation | async-start | bytes 1310720 | tf_op jit(solution)/shard_map/all_to_all | solution.py:185
  26.4 0.0 copy-done.6
  26.4 0.1 copy.12.index
  26.5 0.0 copy-done.2
  26.5 0.0 copy-done.1
  26.5 0.0 copy-done
  26.5 0.0 copy-done.5
  26.5 1.0 shard_map.111.own
  27.5 2.8 %collective-permute-start = (bf16[768,512]{1,0:T(8,128)(2,1)S(1)}, bf16[768,512]{1,0:T(8,128)(2,1)S(1)}, u32[]{:S(2)}, u32[]{:S(2)}) collective-permute-start(bf16[768,512]{1,0:T(8,128)(2,1)S(1)} %shard_map.111.own), channel_id=1, source_target_pairs={{0,1},{1,0},{2,3},{3,2},{4,5},{5,4},{6,7},{7,6},{8,9},{9,8},{10,11... | collective-permute-start | bytes 2359304 | tf_op jit(solution)/shard_map/ppermute | solution.py:189
  30.4 1.9 %collective-permute-done.far = bf16[768,512]{1,0:T(8,128)(2,1)S(1)} collective-permute-done((bf16[768,512]{1,0:T(8,128)(2,1)S(1)}, bf16[768,512]{1,0:T(8,128)(2,1)S(1)}, u32[]{:S(2)}, u32[]{:S(2)}) %collective-permute-start) | collective-permute-done | bytes 786464 | tf_op jit(solution)/shard_map/ppermute | solution.py:189
  32.2 14.0 %all-to-all-done.blocks = bf16[32,80,128]{2,1,0:T(8,128)(2,1)S(1)} async-done(((bf16[32,80,128]{2,1,0:T(8,128)(2,1)}), bf16[32,80,128]{2,1,0:T(8,128)(2,1)S(1)}, u32[]{:S(2)}, u32[]{:S(2)}) %all-to-all-start) | async-done | bytes 655392 | tf_op jit(solution)/shard_map/all_to_all | solution.py:185
  46.3 0.8 shard_map.112
  47.1 29.9 %all_to_all.20.parts = bf16[16,40,768]{2,1,0:T(8,128)(2,1)S(1)} all-to-all(bf16[16,40,768]{2,1,0:T(8,128)(2,1)S(1)} %bitcast.5), channel_id=1, replica_groups=mesh['row'=16,'yz'=32,'core'=2] {'row'}, dimensions={0} | all-to-all | bytes 1966080 | tf_op jit(solution)/shard_map/all_to_all | solution.py:185
  77.0 0.2 shard_map.113
  77.1 27.0 %all_to_all.21 = bf16[16,40,768]{2,1,0:T(8,128)(2,1)S(1)} all-to-all(bf16[16,40,768]{2,1,0:T(8,128)(2,1)S(1)} %shard_map.113), channel_id=1, replica_groups=mesh['row'=16,'yz'=32,'core'=2] {'row'}, dimensions={0} | all-to-all | bytes 1966080 | tf_op jit(solution)/shard_map/all_to_all | solution.py:185
  104.2 1.7 %shard_map.114 = bf16[32,80,128]{2,1,0:T(8,128)(2,1)} custom-call(bf16[640,768]{1,0:T(8,128)(2,1)S(1)} %bitcast.3, bf16[768,512]{1,0:T(8,128)(2,1)S(1)} %shard_map.111.own, bf16[768,512]{1,0:T(8,128)(2,1)S(1)} %collective-permute-done.far), custom_call_target="tpu_custom_call" | custom-call | flops 503316480 | bytes 3211264 | tf_op jit(solution)/shard_map/pallas_call | solution.py:173
  105.9 13.2 %all-to-all-start.3 = ((bf16[32,80,128]{2,1,0:T(8,128)(2,1)}), bf16[32,80,128]{2,1,0:T(8,128)(2,1)S(1)}, u32[]{:S(2)}, u32[]{:S(2)}) async-start(bf16[32,80,128]{2,1,0:T(8,128)(2,1)} %shard_map.114), calls=%async_computation.3 | async-start | bytes 1310720 | tf_op jit(solution)/shard_map/all_to_all | solution.py:185
  119.1 1.0 shard_map.115
  120.1 4.6 %collective-permute-start.1 = (bf16[768,512]{1,0:T(8,128)(2,1)S(1)}, bf16[768,512]{1,0:T(8,128)(2,1)S(1)}, u32[]{:S(2)}, u32[]{:S(2)}) collective-permute-start(bf16[768,512]{1,0:T(8,128)(2,1)S(1)} %get-tuple-element.27), channel_id=1, source_target_pairs={{0,1},{1,0},{2,3},{3,2},{4,5},{5,4},{6,7},{7,6},{8,9},{9,8},{10,11... | collective-permute-start | bytes 2359304 | tf_op jit(solution)/shard_map/ppermute | solution.py:189
  124.7 1.9 %collective-permute-done.1.far = bf16[768,512]{1,0:T(8,128)(2,1)S(1)} collective-permute-done((bf16[768,512]{1,0:T(8,128)(2,1)S(1)}, bf16[768,512]{1,0:T(8,128)(2,1)S(1)}, u32[]{:S(2)}, u32[]{:S(2)}) %collective-permute-start.1) | collective-permute-done | bytes 786464 | tf_op jit(solution)/shard_map/ppermute | solution.py:189
  126.6 2.1 %shard_map.116 = (f32[6,128,128]{2,1,0:T(8,128)}, f32[6,128,128]{2,1,0:T(8,128)}, f32[6,128,128]{2,1,0:T(8,128)}) custom-call(s32[3,6,2]{2,1,0:T(8,128)S(1)} %copy.12.index, s32[3]{0:T(128)S(1)} %bitcast.7, f32[768,512]{1,0:T(8,128)S(1)} %get-tuple-element.26.own, bf16[768,512]{1,0:T(8,128)(2,1)S(1)} %collective-permute-done.1.far), custom_call_target="tpu_custom_call" | custom-call | bytes 3539100 | tf_op jit(solution)/shard_map/pallas_call | solution.py:173
  128.7 11.5 %all-to-all-done.3.parts = bf16[32,80,128]{2,1,0:T(8,128)(2,1)S(1)} async-done(((bf16[32,80,128]{2,1,0:T(8,128)(2,1)}), bf16[32,80,128]{2,1,0:T(8,128)(2,1)S(1)}, u32[]{:S(2)}, u32[]{:S(2)}) %all-to-all-start.3) | async-done | bytes 655392 | tf_op jit(solution)/shard_map/all_to_all | solution.py:185
  140.2 0.7 shard_map.117
  (1 shorter events, 0.0 us)
Async XLA Ops:
  0.6 25.9 %copy-start.2 = (bf16[6,128,128]{2,1,0:T(8,128)(2,1)S(1)}, bf16[6,128,128]{2,1,0:T(8,128)(2,1)}, u32[]{:S(2)}) copy-start(bf16[6,128,128]{2,1,0:T(8,128)(2,1)} %down.1) | copy-start | bytes 589828
  0.6 25.9 %copy-start.1 = (bf16[6,128,128]{2,1,0:T(8,128)(2,1)S(1)}, bf16[6,128,128]{2,1,0:T(8,128)(2,1)}, u32[]{:S(2)}) copy-start(bf16[6,128,128]{2,1,0:T(8,128)(2,1)} %up.1) | copy-start | bytes 589828
  0.7 0.8 copy-start.3
  1.4 0.7 copy-start.4
  2.1 24.3 %copy-start.6 = (s32[3,6,2]{1,2,0:T(2,128)S(1)}, s32[3,6,2]{1,2,0:T(2,128)}, u32[]{:S(2)}) copy-start(s32[3,6,2]{1,2,0:T(2,128)} %param.12) | copy-start | bytes 436
  2.1 24.4 %copy-start = (bf16[6,128,128]{2,1,0:T(8,128)(2,1)S(1)}, bf16[6,128,128]{2,1,0:T(8,128)(2,1)}, u32[]{:S(2)}) copy-start(bf16[6,128,128]{2,1,0:T(8,128)(2,1)} %gate.1) | copy-start | bytes 589828
  2.1 24.4 %copy-start.5 = (s32[3,1,1]{0,2,1:T(1,128)S(1)}, s32[3,1,1]{0,2,1:T(1,128)}, u32[]{:S(2)}) copy-start(s32[3,1,1]{0,2,1:T(1,128)} %param.13) | copy-start | bytes 40
  3.0 43.2 %all-to-all-start = ((bf16[32,80,128]{2,1,0:T(8,128)(2,1)}), bf16[32,80,128]{2,1,0:T(8,128)(2,1)S(1)}, u32[]{:S(2)}, u32[]{:S(2)}) async-start(bf16[32,80,128]{2,1,0:T(8,128)(2,1)} %shard_map.110), calls=%async_computation | async-start | bytes 1310720 | tf_op jit(solution)/shard_map/all_to_all | solution.py:185
  27.5 4.7 %collective-permute-start = (bf16[768,512]{1,0:T(8,128)(2,1)S(1)}, bf16[768,512]{1,0:T(8,128)(2,1)S(1)}, u32[]{:S(2)}, u32[]{:S(2)}) collective-permute-start(bf16[768,512]{1,0:T(8,128)(2,1)S(1)} %shard_map.111.own), channel_id=1, source_target_pairs={{0,1},{1,0},{2,3},{3,2},{4,5},{5,4},{6,7},{7,6},{8,9},{9,8},{10,11... | collective-permute-start | bytes 2359304 | tf_op jit(solution)/shard_map/ppermute | solution.py:189
  105.9 34.3 %all-to-all-start.3 = ((bf16[32,80,128]{2,1,0:T(8,128)(2,1)}), bf16[32,80,128]{2,1,0:T(8,128)(2,1)S(1)}, u32[]{:S(2)}, u32[]{:S(2)}) async-start(bf16[32,80,128]{2,1,0:T(8,128)(2,1)} %shard_map.114), calls=%async_computation.3 | async-start | bytes 1310720 | tf_op jit(solution)/shard_map/all_to_all | solution.py:185
  120.1 6.5 %collective-permute-start.1 = (bf16[768,512]{1,0:T(8,128)(2,1)S(1)}, bf16[768,512]{1,0:T(8,128)(2,1)S(1)}, u32[]{:S(2)}, u32[]{:S(2)}) collective-permute-start(bf16[768,512]{1,0:T(8,128)(2,1)S(1)} %get-tuple-element.27), channel_id=1, source_target_pairs={{0,1},{1,0},{2,3},{3,2},{4,5},{5,4},{6,7},{7,6},{8,9},{9,8},{10,11... | collective-permute-start | bytes 2359304 | tf_op jit(solution)/shard_map/ppermute | solution.py:189

commit v3 on v2

v3 whole, which is shorter than its diff:
```python
import jax
import jax.numpy as jnp
from jax import lax
from jax.experimental import pallas as pl
from jax.experimental.pallas import tpu as pltpu
from jax.sharding import Mesh
from jax.sharding import PartitionSpec as P

F32 = jnp.float32
BF16 = jnp.bfloat16
VMEM = pl.BlockSpec(memory_space=pltpu.VMEM)
SMEM = pl.BlockSpec(memory_space=pltpu.SMEM)
NT = (((1,), (1,)), ((), ()))
TN = (((0,), (0,)), ((), ()))


def dot(left, right, dims=None):
    if dims is None:
        return jnp.dot(left, right, preferred_element_type=F32)
    return lax.dot_general(left, right, dims, preferred_element_type=F32)


def place_tiles(dense, tiles, index, counts, which, row_offset, col_offset):
    side = tiles.shape[-1]
    for slot in range(tiles.shape[0]):

        @pl.when(slot < counts[which])
        def _():
            row = pl.multiple_of(index[which, slot, 0] * side + row_offset, side)
            col = pl.multiple_of(index[which, slot, 1] * side + col_offset, side)
            dense[pl.ds(row, side), pl.ds(col, side)] = tiles[slot]


def weights_kernel(index, counts, gate, up, down, dense):
    lanes = dense.shape[1]
    dense[...] = jnp.zeros_like(dense)
    place_tiles(dense, gate, index, counts, 0, 0, 0)
    place_tiles(dense, up, index, counts, 1, 0, lanes // 2)
    place_tiles(dense, down, index, counts, 2, lanes, 0)


def take_tiles(outs, index, counts, read):
    for which, out in enumerate(outs):
        slots, side, _ = out.shape
        for slot in range(slots):
            live = slot < counts[which]

            @pl.when(live)
            def _():
                row = pl.multiple_of(index[which, slot, 0] * side, side)
                col = pl.multiple_of(index[which, slot, 1] * side, side)
                out[slot] = read(which, slot, row, col)

            @pl.when(jnp.logical_not(live))
            def _():
                out[slot] = jnp.zeros(out.shape[1:], out.dtype)


def place(which, row, col, lanes, side):
    row = pl.multiple_of(row + (lanes if which == 2 else 0), side)
    col = pl.multiple_of(col + (lanes // 2 if which == 1 else 0), side)
    return pl.ds(row, side), pl.ds(col, side)


def pair_kernel(far_index, far_counts, mine, received, own, gate_out, up_out, down_out):
    _, _, lanes = mine.shape
    own[...] = mine[0] + received[0].astype(F32)

    def read(which, slot, row, col):
        at = place(which, row, col, lanes, gate_out.shape[-1])
        return (mine[(1, *at)] + received[(1, *at)].astype(F32)).astype(gate_out.dtype)

    take_tiles((gate_out, up_out, down_out), far_index, far_counts, read)


def tiles_kernel(index, counts, own, gate_far, up_far, down_far, gate_out, up_out, down_out):
    lanes = own.shape[1]
    far = (gate_far, up_far, down_far)

    def read(which, slot, row, col):
        at = place(which, row, col, lanes, gate_out.shape[-1])
        return own[at] + far[which][slot].astype(F32)

    take_tiles((gate_out, up_out, down_out), index, counts, read)


def spread_kernel(tokens, cotangent, out, stage):
    rows, lanes = tokens.shape
    side = out.shape[-1]
    chunks = lanes // side
    part = rows // 2
    peers = out.shape[0] // 2
    size = 2 * chunks * part
    for start, block in ((0, tokens), (chunks, cotangent)):
        for q in range(chunks):
            piece = block[:, q * side : (q + 1) * side].astype(F32)
            for group in range(2):
                row = group * size + (start + q) * part
                stage[row : row + part, :] = piece[group * part : (group + 1) * part]
    for group in range(2):
        packed = stage[group * size : (group + 1) * size, :].astype(out.dtype)
        for peer in range(peers):
            out[group * peers + peer] = packed


def partial_kernel(
    me, blocks, own, far, own_core, far_core, out, tokens, cotangent, stage
):
    _, quarter, lanes = tokens.shape
    side = blocks.shape[-1]
    peers = blocks.shape[0] // 2
    rows = quarter // peers
    chunks = lanes // side
    for group in range(2):
        base = (me[0] if group == 0 else 1 - me[0]) * peers
        for peer in range(peers):
            block = blocks[base + peer].astype(F32)
            for q in range(2 * chunks):
                stage[group, peer * rows : (peer + 1) * rows, q * side : (q + 1) * side] = block[
                    q * rows : (q + 1) * rows
                ]
        tokens[group] = stage[group, :, 0:lanes].astype(tokens.dtype)
        cotangent[group] = stage[group, :, lanes:].astype(cotangent.dtype)
    for start, near, other in ((0, own, far), (quarter, own_core, far_core)):
        rows_out = slice(start, start + quarter)
        out[rows_out, 0:lanes] = (
            dot(tokens[0], near[0:lanes, :]) + dot(tokens[1], other[0:lanes, :])
        ).astype(out.dtype)
        out[rows_out, lanes:] = (
            dot(cotangent[0], near[lanes:, :], NT) + dot(cotangent[1], other[lanes:, :], NT)
        ).astype(out.dtype)


def sum_parts(parts, start, stop):
    total = parts[start].astype(F32)
    for peer in range(start + 1, stop):
        total = total + parts[peer].astype(F32)
    return total


def units_kernel(parts, out):
    total = sum_parts(parts, 0, parts.shape[0])
    units = total.shape[1] // 3
    gate_sum = total[:, 0:units]
    up_sum = total[:, units : 2 * units]
    hidden_grad = total[:, 2 * units :]
    sigmoid_gate = jax.nn.sigmoid(gate_sum)
    active = gate_sum * sigmoid_gate
    hidden = (active * up_sum).astype(out.dtype)
    gate_act = (
        hidden_grad * up_sum * sigmoid_gate * (1.0 + gate_sum * (1.0 - sigmoid_gate))
    ).astype(out.dtype)
    up_act = (hidden_grad * active).astype(out.dtype)
    for peer in range(out.shape[0]):
        out[peer, :, 0:units] = hidden
        out[peer, :, units : 2 * units] = gate_act
        out[peer, :, 2 * units :] = up_act


def apply_kernel(me, acts, own, far, own_core, far_core, out, result, stage):
    quarter = result.shape[0]
    lanes = own.shape[1]
    units = own.shape[0] - lanes
    peers = out.shape[0] // 2
    side = out.shape[-1]
    rows = quarter // peers
    near, other = slice(0, quarter), slice(quarter, 2 * quarter)
    for group, first, second in ((0, own, own_core), (1, far, far_core)):
        result[:, 0:lanes] = dot(acts[near, 0:units], first[lanes:, :]) + dot(
            acts[other, 0:units], second[lanes:, :]
        )
        result[:, lanes:] = dot(acts[near, units:], first[0:lanes, :], NT) + dot(
            acts[other, units:], second[0:lanes, :], NT
        )
        base = (me[0] if group == 0 else 1 - me[0]) * peers
        for peer in range(peers):
            for q in range(2 * lanes // side):
                stage[peer, q * rows : (q + 1) * rows, :] = result[
                    peer * rows : (peer + 1) * rows, q * side : (q + 1) * side
                ]
            out[base + peer] = stage[peer].astype(out.dtype)


def grads_kernel(acts, tokens, cotangent, mine, sibling):
    _, quarter, lanes = tokens.shape
    units = mine.shape[1] - lanes
    for start, out in ((quarter, sibling), (0, mine)):
        rows = slice(start, start + quarter)
        for group in range(2):
            out[group, 0:lanes, :] = dot(tokens[group], acts[rows, units:], TN).astype(out.dtype)
            out[group, lanes:, :] = dot(acts[rows, 0:units], cotangent[group], TN).astype(out.dtype)


def finish_kernel(parts, output, input_grad):
    rows, lanes = output.shape
    part = rows // 2
    peers = parts.shape[0] // 2
    side = parts.shape[-1]
    chunks = lanes // side
    for group in range(2):
        total = sum_parts(parts, group * peers, (group + 1) * peers)
        for start, out in ((0, output), (chunks, input_grad)):
            for q in range(chunks):
                piece = total[(start + q) * part : (start + q + 1) * part]
                out[group * part : (group + 1) * part, q * side : (q + 1) * side] = piece.astype(
                    out.dtype
                )


def call(kernel, outs, args, smem=0, scratch=(), flops=0):
    moved = sum(a.size * a.dtype.itemsize for a in args) + sum(
        o.size * jnp.dtype(o.dtype).itemsize for o in outs
    )
    single = len(outs) == 1
    return pl.pallas_call(
        kernel,
        out_shape=outs[0] if single else outs,
        in_specs=(SMEM,) * smem + (VMEM,) * (len(args) - smem),
        out_specs=VMEM if single else (VMEM,) * len(outs),
        scratch_shapes=scratch,
        compiler_params=pltpu.CompilerParams(vmem_limit_bytes=20 << 20),
        cost_estimate=pl.CostEstimate(flops=flops, bytes_accessed=moved, transcendentals=0),
    )(*args)


def exchange(blocks, axis):
    return lax.all_to_all(blocks, axis, split_axis=0, concat_axis=0, tiled=True)


def swap(block, axis):
    return lax.ppermute(block, axis, [(0, 1), (1, 0)])


def body(tokens, cotangent, gate_tiles, up_tiles, down_tiles, tile_index, tile_counts):
    rows, lanes = tokens.shape
    slots, side, _ = gate_tiles.shape
    row_peers = lax.axis_size("xh") * lax.axis_size("yl")
    peers = lax.axis_size("yz")
    units = 2 * side
    quarter = peers * rows // 2
    share = 2 * quarter // row_peers
    packed = lanes // side * rows
    flops = 24 * quarter * lanes * units
    counts = tile_counts.reshape(3)
    me = lax.axis_index("xl").astype(jnp.int32).reshape(1)
    shape = jax.ShapeDtypeStruct

    spread = call(
        spread_kernel,
        (shape((2 * peers, packed, side), BF16),),
        (tokens, cotangent),
        scratch=(pltpu.VMEM((2 * packed, side), F32),),
    )
    spread, gate_tiles, up_tiles, down_tiles = lax.optimization_barrier(
        (spread, gate_tiles, up_tiles, down_tiles)
    )
    blocks = exchange(spread, ("xl", "yz"))
    own = call(
        weights_kernel,
        (shape((lanes + units, lanes), BF16),),
        (tile_index, counts, gate_tiles, up_tiles, down_tiles),
        smem=2,
    )
    far = swap(own, "xl")
    own_core = swap(own, "core")
    far_core = swap(far, "core")
    listing = jnp.concatenate([tile_index.reshape(3, 2 * slots), counts[:, None]], axis=1)
    listing = swap(listing, "xl")
    far_core, listing = lax.optimization_barrier((far_core, listing))
    far_index = listing[:, 0 : 2 * slots].reshape(3, slots, 2)
    far_counts = listing[:, 2 * slots]
    weights = (own, far, own_core, far_core)
    parts, all_tokens, all_cotangent = call(
        partial_kernel,
        (
            shape((2 * quarter, 3 * units), BF16),
            shape((2, quarter, lanes), BF16),
            shape((2, quarter, lanes), BF16),
        ),
        (me, blocks, *weights),
        smem=1,
        scratch=(pltpu.VMEM((2, quarter, 2 * lanes), F32),),
        flops=flops,
    )
    parts = exchange(parts.reshape(row_peers, share, 3 * units), ("xh", "yl"))
    acts = call(units_kernel, (shape(parts.shape, BF16),), (parts,))
    acts = exchange(acts, ("xh", "yl")).reshape(2 * quarter, 3 * units)
    sums = call(
        apply_kernel,
        (shape((2 * peers, packed, side), BF16),),
        (me, acts, *weights),
        smem=1,
        scratch=(pltpu.VMEM((quarter, 2 * lanes), F32), pltpu.VMEM((peers, packed, side), F32)),
        flops=flops,
    )
    acts, sums = lax.optimization_barrier((acts, sums))
    sums = exchange(sums, ("xl", "yz"))
    dense = (2, lanes + units, lanes)
    mine, sibling = call(
        grads_kernel,
        (shape(dense, F32), shape(dense, BF16)),
        (acts, all_tokens, all_cotangent),
        flops=flops,
    )
    tile_shape = (slots, side, side)
    own_grad, *far_grads = call(
        pair_kernel,
        (shape(dense[1:], F32),) + (shape(tile_shape, BF16),) * 3,
        (far_index, far_counts, mine, swap(sibling, "core")),
        smem=2,
    )
    far_grads = swap(jnp.concatenate(far_grads), "xl").reshape(3, *tile_shape)
    gate_grad, up_grad, down_grad = call(
        tiles_kernel,
        (shape(tile_shape, F32),) * 3,
        (tile_index, counts, own_grad, *far_grads),
        smem=2,
    )
    output, input_grad = call(finish_kernel, (shape((rows, lanes), BF16),) * 2, (sums,))
    return (output, input_grad, gate_grad, up_grad, down_grad)


def solution(mesh):
    row_size, col_size = mesh.shape["row"], mesh.shape["col"]
    split = Mesh(
        mesh.devices.reshape(row_size // 4, 2, 2, col_size // 2, 2),
        ("xh", "xl", "yl", "yz", "core"),
    )
    row, col = ("xh", "xl", "yl"), ("yz", "core")
    blocks = P(col, row)
    tiles = P(row, col, None)
    small = P(None, row, col)
    return jax.shard_map(
        body,
        mesh=split,
        in_specs=(blocks, blocks, tiles, tiles, tiles, small, small),
        out_specs=(blocks, blocks, tiles, tiles, tiles),
        check_vma=False,
    )
```

time: 142 us -> 142 us (level)
  blocking collectives: 56.9 us -> 33.8 us
  starting transfers between devices: 44 us -> 55.4 us
  local copies, waits for them, and re-layouts: 1.6 us -> 8.12 us
  Pallas kernels: 8.32 us -> 12.7 us
    all_to_all x2, blocking collectives: 56.9 us -> 33.8 us  [exchange(): return lax.all_to_all(blocks, axis, split_axis=0, concat_axis=0, tiled=True)]
    ppermute x2 -> x6, starting transfers between devices: 7.43 us -> 25.3 us  [swap(): return lax.ppermute(block, axis, [(0, 1), (1, 0)])]
    all_to_all x2, starting transfers between devices: 36.5 us -> 30.1 us  [exchange(): return lax.all_to_all(blocks, axis, split_axis=0, concat_axis=0, tiled=True)]
    unnamed x15 -> x21, local copies, waits for them, and re-layouts: 1.6 us -> 7.66 us
    pallas_call x8 -> x9, Pallas kernels: 8.32 us -> 12.7 us  [call(): pl.pallas_call(kernel, out_shape=outs[0] if single else outs, in_specs=(S...]
    ppermute x2 -> x6, waiting for transfers between devices: 3.78 us -> 1.5 us  [swap(): return lax.ppermute(block, axis, [(0, 1), (1, 0)])]
    all_to_all x2, waiting for transfers between devices: 25.6 us -> 27.1 us  [exchange(): return lax.all_to_all(blocks, axis, split_axis=0, concat_axis=0, tiled=True)]
  transfers between devices with their start and end apart: 4 -> 8, of which waited for: 4 -> 3; matrix products, arithmetic and copies ran while one was open for 0% -> 0% of each run, Pallas kernels for 3% -> 3%
where the time goes in v3:
time: 142 us; the launch traced here: 140 us
  starting transfers between devices  55.4 us (39%)
  blocking collectives  33.8 us (24%)
  waiting for transfers between devices  28.6 us (20%)
  Pallas kernels  12.7 us (9%)
  local copies, waits for them, and re-layouts  8.12 us (6%)
    all_to_all x2, blocking collectives, exchange(): return lax.all_to_all(blocks, axis, split_axis=0, concat_axis=0, tiled=True)  33.8 us
    all_to_all x2, starting transfers between devices, exchange(): return lax.all_to_all(blocks, axis, split_axis=0, concat_axis=0, tiled=True)  30.1 us
    all_to_all x2, waiting for transfers between devices, exchange(): return lax.all_to_all(blocks, axis, split_axis=0, concat_axis=0, tiled=True)  27.1 us
    ppermute x6, starting transfers between devices, swap(): return lax.ppermute(block, axis, [(0, 1), (1, 0)])  25.3 us
    pallas_call x9, Pallas kernels, call(): pl.pallas_call(kernel, out_shape=outs[0] if single else outs, in_specs=(S...  12.7 us
    unnamed x21, local copies, waits for them, and re-layouts  7.66 us
  transfers between devices with their start and end apart: 8, of which 3 were waited for; matrix products, arithmetic and copies ran while one was open for 0% of the time, Pallas kernels for 3%

profile of v3, /device:TPU:1, one launch (start us, length us, event | category | flops | bytes accessed | tf_op | source)
XLA Modules:
  0.0 139.6 jit_solution(13592597262136791271)
XLA Ops:
  0.6 0.8 copy.16.index
  1.4 0.7 copy-done.6
  2.1 0.7 copy-done.7
  2.9 0.9 shard_map.110
  3.8 0.9 copy-done.3
  4.7 0.9 copy-done.4
  5.6 0.9 copy-done.5
  6.5 0.7 copy-done.8
  7.2 1.0 shard_map.111.own
  8.2 3.9 %collective-permute-start = (bf16[768,512]{1,0:T(8,128)(2,1)S(1)}, bf16[768,512]{1,0:T(8,128)(2,1)S(1)}, u32[]{:S(2)}, u32[]{:S(2)}) collective-permute-start(bf16[768,512]{1,0:T(8,128)(2,1)S(1)} %shard_map.111.own), channel_id=1, source_target_pairs={{0,128},{128,0},{1,129},{129,1},{2,130},{130,2},{3,131},{131,3},{4... | collective-permute-start | bytes 2359304 | tf_op jit(solution)/shard_map/ppermute | solution.py:231
  12.1 23.4 %all-to-all-start = ((bf16[64,40,128]{2,1,0:T(8,128)(2,1)}), bf16[64,40,128]{2,1,0:T(8,128)(2,1)}, u32[]{:S(2)}, u32[]{:S(2)}) async-start(bf16[64,40,128]{2,1,0:T(8,128)(2,1)} %shard_map.110), calls=%async_computation | async-start | bytes 1310720 | tf_op jit(solution)/shard_map/all_to_all | solution.py:227
  35.5 3.2 %collective-permute-start.2 = (bf16[768,512]{1,0:T(8,128)(2,1)S(1)}, bf16[768,512]{1,0:T(8,128)(2,1)S(1)}, u32[]{:S(2)}, u32[]{:S(2)}) collective-permute-start(bf16[768,512]{1,0:T(8,128)(2,1)S(1)} %collective-permute-done.far), channel_id=1, source_target_pairs={{0,1},{1,0},{2,3},{3,2},{4,5},{5,4},{6,7},{7,6},{8,9},{9,8},{10,11... | collective-permute-start | bytes 2359304 | tf_op jit(solution)/shard_map/ppermute | solution.py:231
  38.7 1.9 %collective-permute-start.1 = (bf16[768,512]{1,0:T(8,128)(2,1)S(1)}, bf16[768,512]{1,0:T(8,128)(2,1)S(1)}, u32[]{:S(2)}, u32[]{:S(2)}) collective-permute-start(bf16[768,512]{1,0:T(8,128)(2,1)S(1)} %shard_map.111.own), channel_id=1, source_target_pairs={{0,1},{1,0},{2,3},{3,2},{4,5},{5,4},{6,7},{7,6},{8,9},{9,8},{10,11... | collective-permute-start | bytes 2359304 | tf_op jit(solution)/shard_map/ppermute | solution.py:231
  40.7 0.1 copy.18
  40.9 3.2 %collective-permute-start.3 = (s32[3,13]{1,0:T(4,128)S(1)}, s32[3,13]{1,0:T(4,128)S(1)}, u32[]{:S(2)}, u32[]{:S(2)}) collective-permute-start(s32[3,13]{1,0:T(4,128)S(1)} %pad_add_fusion), channel_id=1, source_target_pairs={{0,128},{128,0},{1,129},{129,1},{2,130},{130,2},{3,131},{131,3},{4... | collective-permute-start | bytes 476 | tf_op jit(solution)/shard_map/ppermute | solution.py:231
  44.1 1.5 %collective-permute-done.3 = s32[3,13]{1,0:T(4,128)S(1)} collective-permute-done((s32[3,13]{1,0:T(4,128)S(1)}, s32[3,13]{1,0:T(4,128)S(1)}, u32[]{:S(2)}, u32[]{:S(2)}) %collective-permute-start.3) | collective-permute-done | bytes 188 | tf_op jit(solution)/shard_map/ppermute | solution.py:231
  45.6 11.0 %all-to-all-done.blocks = bf16[64,40,128]{2,1,0:T(8,128)(2,1)} async-done(((bf16[64,40,128]{2,1,0:T(8,128)(2,1)}), bf16[64,40,128]{2,1,0:T(8,128)(2,1)}, u32[]{:S(2)}, u32[]{:S(2)}) %all-to-all-start) | async-done | bytes 655392 | tf_op jit(solution)/shard_map/all_to_all | solution.py:227
  56.6 2.1 %shard_map.112 = (bf16[320,768]{1,0:T(8,128)(2,1)S(1)}, bf16[2,160,512]{2,1,0:T(8,128)(2,1)S(1)}, bf16[2,160,512]{2,1,0:T(8,128)(2,1)S(1)}) custom-call(s32[1]{0:T(128)} %bitcast.me, bf16[64,40,128]{2,1,0:T(8,128)(2,1)} %all-to-all-done.blocks, bf16[768,512]{1,0:T(8,128)(2,1)S(1)} %shard_map.111.own, bf16[768,512]{1,0:T(8,128)(2,1)S(1)} %collective-permute-done.far, ...), custom_call_target="tpu_custom_call" | custom-call | flops 503316480 | bytes 4947972 | tf_op jit(solution)/shard_map/pallas_call | solution.py:215
  58.7 19.0 %all_to_all.20.parts = bf16[8,40,768]{2,1,0:T(8,128)(2,1)S(1)} all-to-all(bf16[8,40,768]{2,1,0:T(8,128)(2,1)S(1)} %bitcast.8), channel_id=1, replica_groups=mesh['xh'=4,'xl'=2,'yl'=2,'yz'=32,'core'=2] {'xh','yl'}, dimensions={0} | all-to-all | bytes 983040 | tf_op jit(solution)/shard_map/all_to_all | solution.py:227
  77.7 14.8 %all_to_all.21 = bf16[8,40,768]{2,1,0:T(8,128)(2,1)S(1)} all-to-all(bf16[8,40,768]{2,1,0:T(8,128)(2,1)S(1)} %shard_map.113), channel_id=1, replica_groups=mesh['xh'=4,'xl'=2,'yl'=2,'yz'=32,'core'=2] {'xh','yl'}, dimensions={0} | all-to-all | bytes 983040 | tf_op jit(solution)/shard_map/all_to_all | solution.py:227
  92.6 1.2 shard_map.114
  93.8 0.8 copy-done
  94.6 1.8 %shard_map.116 = (f32[2,768,512]{2,1,0:T(8,128)S(1)}, bf16[2,768,512]{2,1,0:T(8,128)(2,1)}) custom-call(bf16[320,768]{1,0:T(8,128)(2,1)S(1)} %bitcast.7, bf16[2,160,512]{2,1,0:T(8,128)(2,1)S(1)} %get-tuple-element.38.tokens, bf16[2,160,512]{2,1,0:T(8,128)(2,1)S(1)} %get-tuple-element.39.cotangent), custom_call_target="tpu_custom_call" | custom-call | flops 503316480 | bytes 5865472 | tf_op jit(solution)/shard_map/pallas_call | solution.py:215
  96.4 9.9 %collective-permute-start.4 = (bf16[2,768,512]{2,1,0:T(8,128)(2,1)}, bf16[2,768,512]{2,1,0:T(8,128)(2,1)}, u32[]{:S(2)}, u32[]{:S(2)}) collective-permute-start(bf16[2,768,512]{2,1,0:T(8,128)(2,1)} %get-tuple-element.41), channel_id=1, source_target_pairs={{0,1},{1,0},{2,3},{3,2},{4,5},{5,4},{6,7},{7,6},{8,9},{9,8},{10,11... | collective-permute-start | bytes 4718600 | tf_op jit(solution)/shard_map/ppermute | solution.py:231
  106.4 6.8 %all-to-all-start.3 = ((bf16[64,40,128]{2,1,0:T(8,128)(2,1)}), bf16[64,40,128]{2,1,0:T(8,128)(2,1)}, u32[]{:S(2)}, u32[]{:S(2)}) async-start(bf16[64,40,128]{2,1,0:T(8,128)(2,1)} %copy-done), calls=%async_computation.3 | async-start | bytes 1310720 | tf_op jit(solution)/shard_map/all_to_all | solution.py:227
  113.2 0.2 slice_reduce_fusion.far_counts
  113.4 1.9 %shard_map.117 = (f32[768,512]{1,0:T(8,128)S(1)}, bf16[6,128,128]{2,1,0:T(8,128)(2,1)S(1)}, bf16[6,128,128]{2,1,0:T(8,128)(2,1)S(1)}, bf16[6,128,128]{2,1,0:T(8,128)(2,1)S(1)}) custom-call(s32[3,6,2]{2,1,0:T(8,128)S(1)} %reshape.40.far_index, s32[3]{0:T(128)S(1)} %slice_reduce_fusion.far_counts, f32[2,768,512]{2,1,0:T(8,128)S(1)} %get-tuple-element.40.mine, ...), custom_call_target="tpu_custom_call" | custom-call | bytes 6881436 | tf_op jit(solution)/shard_map/pallas_call | solution.py:215
  115.3 1.2 copy-done.1
  116.5 3.1 %collective-permute-start.5 = (bf16[18,128,128]{2,1,0:T(8,128)(2,1)S(1)}, bf16[18,128,128]{2,1,0:T(8,128)(2,1)S(1)}, u32[]{:S(2)}, u32[]{:S(2)}) collective-permute-start(bf16[18,128,128]{2,1,0:T(8,128)(2,1)S(1)} %pad_maximum_fusion), channel_id=1, source_target_pairs={{0,128},{128,0},{1,129},{129,1},{2,130},{130,2},{3,131},{131,3},{4... | collective-permute-start | bytes 1769480 | tf_op jit(solution)/shard_map/ppermute | solution.py:231
  119.6 16.1 %all-to-all-done.3.parts = bf16[64,40,128]{2,1,0:T(8,128)(2,1)} async-done(((bf16[64,40,128]{2,1,0:T(8,128)(2,1)}), bf16[64,40,128]{2,1,0:T(8,128)(2,1)}, u32[]{:S(2)}, u32[]{:S(2)}) %all-to-all-start.3) | async-done | bytes 655392 | tf_op jit(solution)/shard_map/all_to_all | solution.py:227
  135.7 1.8 %shard_map.115 = (bf16[10,512]{1,0:T(8,128)(2,1)}, bf16[10,512]{1,0:T(8,128)(2,1)}) custom-call(bf16[64,40,128]{2,1,0:T(8,128)(2,1)} %all-to-all-done.3.parts), custom_call_target="tpu_custom_call" | custom-call | bytes 675840 | tf_op jit(solution)/shard_map/pallas_call | solution.py:215
  137.5 2.0 %shard_map.118 = (f32[6,128,128]{2,1,0:T(8,128)}, f32[6,128,128]{2,1,0:T(8,128)}, f32[6,128,128]{2,1,0:T(8,128)}) custom-call(s32[3,6,2]{2,1,0:T(8,128)S(1)} %copy.16.index, s32[3]{0:T(128)S(1)} %bitcast.11, f32[768,512]{1,0:T(8,128)S(1)} %copy-done.2, bf16[6,128,128]{2,1,0:T(8,128)(2,1)S(1)} %get-tuple-element.51.gate_far, ...), custom_call_target="tpu_custom_call" | custom-call | bytes 3342492 | tf_op jit(solution)/shard_map/pallas_call | solution.py:215
  (23 shorter events, 0.5 us)
Async XLA Ops:
  1.4 0.7 copy-start.6
  2.1 0.7 copy-start.7
  2.9 37.8 %copy-start.9 = (s32[3,1,1]{0,2,1:T(1,128)S(1)}, s32[3,1,1]{0,2,1:T(1,128)}, u32[]{:S(2)}) copy-start(s32[3,1,1]{0,2,1:T(1,128)} %param.13) | copy-start | bytes 40
  3.8 0.9 copy-start.3
  4.7 0.9 copy-start.4
  5.6 0.9 copy-start.5
  6.5 0.7 copy-start.8
  8.2 27.3 %collective-permute-start = (bf16[768,512]{1,0:T(8,128)(2,1)S(1)}, bf16[768,512]{1,0:T(8,128)(2,1)S(1)}, u32[]{:S(2)}, u32[]{:S(2)}) collective-permute-start(bf16[768,512]{1,0:T(8,128)(2,1)S(1)} %shard_map.111.own), channel_id=1, source_target_pairs={{0,128},{128,0},{1,129},{129,1},{2,130},{130,2},{3,131},{131,3},{4... | collective-permute-start | bytes 2359304 | tf_op jit(solution)/shard_map/ppermute | solution.py:231
  12.1 44.5 %all-to-all-start = ((bf16[64,40,128]{2,1,0:T(8,128)(2,1)}), bf16[64,40,128]{2,1,0:T(8,128)(2,1)}, u32[]{:S(2)}, u32[]{:S(2)}) async-start(bf16[64,40,128]{2,1,0:T(8,128)(2,1)} %shard_map.110), calls=%async_computation | async-start | bytes 1310720 | tf_op jit(solution)/shard_map/all_to_all | solution.py:227
  35.5 10.1 %collective-permute-start.2 = (bf16[768,512]{1,0:T(8,128)(2,1)S(1)}, bf16[768,512]{1,0:T(8,128)(2,1)S(1)}, u32[]{:S(2)}, u32[]{:S(2)}) collective-permute-start(bf16[768,512]{1,0:T(8,128)(2,1)S(1)} %collective-permute-done.far), channel_id=1, source_target_pairs={{0,1},{1,0},{2,3},{3,2},{4,5},{5,4},{6,7},{7,6},{8,9},{9,8},{10,11... | collective-permute-start | bytes 2359304 | tf_op jit(solution)/shard_map/ppermute | solution.py:231
  38.7 6.9 %collective-permute-start.1 = (bf16[768,512]{1,0:T(8,128)(2,1)S(1)}, bf16[768,512]{1,0:T(8,128)(2,1)S(1)}, u32[]{:S(2)}, u32[]{:S(2)}) collective-permute-start(bf16[768,512]{1,0:T(8,128)(2,1)S(1)} %shard_map.111.own), channel_id=1, source_target_pairs={{0,1},{1,0},{2,3},{3,2},{4,5},{5,4},{6,7},{7,6},{8,9},{9,8},{10,11... | collective-permute-start | bytes 2359304 | tf_op jit(solution)/shard_map/ppermute | solution.py:231
  40.9 4.7 %collective-permute-start.3 = (s32[3,13]{1,0:T(4,128)S(1)}, s32[3,13]{1,0:T(4,128)S(1)}, u32[]{:S(2)}, u32[]{:S(2)}) collective-permute-start(s32[3,13]{1,0:T(4,128)S(1)} %pad_add_fusion), channel_id=1, source_target_pairs={{0,128},{128,0},{1,129},{129,1},{2,130},{130,2},{3,131},{131,3},{4... | collective-permute-start | bytes 476 | tf_op jit(solution)/shard_map/ppermute | solution.py:231
  93.8 0.9 copy-start
  96.4 17.0 %collective-permute-start.4 = (bf16[2,768,512]{2,1,0:T(8,128)(2,1)}, bf16[2,768,512]{2,1,0:T(8,128)(2,1)}, u32[]{:S(2)}, u32[]{:S(2)}) collective-permute-start(bf16[2,768,512]{2,1,0:T(8,128)(2,1)} %get-tuple-element.41), channel_id=1, source_target_pairs={{0,1},{1,0},{2,3},{3,2},{4,5},{5,4},{6,7},{7,6},{8,9},{9,8},{10,11... | collective-permute-start | bytes 4718600 | tf_op jit(solution)/shard_map/ppermute | solution.py:231
  106.4 29.3 %all-to-all-start.3 = ((bf16[64,40,128]{2,1,0:T(8,128)(2,1)}), bf16[64,40,128]{2,1,0:T(8,128)(2,1)}, u32[]{:S(2)}, u32[]{:S(2)}) async-start(bf16[64,40,128]{2,1,0:T(8,128)(2,1)} %copy-done), calls=%async_computation.3 | async-start | bytes 1310720 | tf_op jit(solution)/shard_map/all_to_all | solution.py:227
  115.2 1.2 copy-start.1
  116.4 21.1 %copy-start.2 = (f32[768,512]{1,0:T(8,128)S(1)}, f32[768,512]{1,0:T(8,128)}, u32[]{:S(2)}) copy-start(f32[768,512]{1,0:T(8,128)} %copy-done.1) | copy-start | bytes 4718596
  116.5 21.0 %collective-permute-start.5 = (bf16[18,128,128]{2,1,0:T(8,128)(2,1)S(1)}, bf16[18,128,128]{2,1,0:T(8,128)(2,1)S(1)}, u32[]{:S(2)}, u32[]{:S(2)}) collective-permute-start(bf16[18,128,128]{2,1,0:T(8,128)(2,1)S(1)} %pad_maximum_fusion), channel_id=1, source_target_pairs={{0,128},{128,0},{1,129},{129,1},{2,130},{130,2},{3,131},{131,3},{4... | collective-permute-start | bytes 1769480 | tf_op jit(solution)/shard_map/ppermute | solution.py:231

commit v4 on v3

--- a/solution.py
+++ b/solution.py
@@ -6,6 +6,7 @@
 from jax.sharding import Mesh
 from jax.sharding import PartitionSpec as P
 
+LONG = 1 << 36
 F32 = jnp.float32
 BF16 = jnp.bfloat16
 VMEM = pl.BlockSpec(memory_space=pltpu.VMEM)
@@ -26,8 +27,8 @@
 
         @pl.when(slot < counts[which])
         def _():
-            row = pl.multiple_of(index[which, slot, 0] * side + row_offset, side)
-            col = pl.multiple_of(index[which, slot, 1] * side + col_offset, side)
+            row = pl.multiple_of(index[which, 0, slot] * side + row_offset, side)
+            col = pl.multiple_of(index[which, 1, slot] * side + col_offset, side)
             dense[pl.ds(row, side), pl.ds(col, side)] = tiles[slot]
 
 
@@ -47,8 +48,8 @@
 
             @pl.when(live)
             def _():
-                row = pl.multiple_of(index[which, slot, 0] * side, side)
-                col = pl.multiple_of(index[which, slot, 1] * side, side)
+                row = pl.multiple_of(index[which, 0, slot] * side, side)
+                col = pl.multiple_of(index[which, 1, slot] * side, side)
                 out[slot] = read(which, slot, row, col)
 
             @pl.when(jnp.logical_not(live))
@@ -62,24 +63,25 @@
     return pl.ds(row, side), pl.ds(col, side)
 
 
-def pair_kernel(far_index, far_counts, mine, received, own, gate_out, up_out, down_out):
-    _, _, lanes = mine.shape
-    own[...] = mine[0] + received[0].astype(F32)
+def pair_kernel(far_index, far_counts, mine, received, gate_out, up_out, down_out):
+    lanes = mine.shape[1]
 
     def read(which, slot, row, col):
         at = place(which, row, col, lanes, gate_out.shape[-1])
-        return (mine[(1, *at)] + received[(1, *at)].astype(F32)).astype(gate_out.dtype)
+        return (mine[at] + received[at].astype(F32)).astype(gate_out.dtype)
 
     take_tiles((gate_out, up_out, down_out), far_index, far_counts, read)
 
 
-def tiles_kernel(index, counts, own, gate_far, up_far, down_far, gate_out, up_out, down_out):
-    lanes = own.shape[1]
+def tiles_kernel(
+    index, counts, mine, received, gate_far, up_far, down_far, gate_out, up_out, down_out
+):
+    lanes = mine.shape[1]
     far = (gate_far, up_far, down_far)
 
     def read(which, slot, row, col):
         at = place(which, row, col, lanes, gate_out.shape[-1])
-        return own[at] + far[which][slot].astype(F32)
+        return mine[at] + received[at].astype(F32) + far[which][slot].astype(F32)
 
     take_tiles((gate_out, up_out, down_out), index, counts, read)
 
@@ -103,9 +105,7 @@
             out[group * peers + peer] = packed
 
 
-def partial_kernel(
-    me, blocks, own, far, own_core, far_core, out, tokens, cotangent, stage
-):
+def unpack_kernel(me, blocks, tokens, cotangent, stage):
     _, quarter, lanes = tokens.shape
     side = blocks.shape[-1]
     peers = blocks.shape[0] // 2
@@ -121,12 +121,16 @@
                 ]
         tokens[group] = stage[group, :, 0:lanes].astype(tokens.dtype)
         cotangent[group] = stage[group, :, lanes:].astype(cotangent.dtype)
+
+
+def partial_kernel(tokens, cotangent, own, far, own_core, far_core, out):
+    _, quarter, lanes = tokens.shape
     for start, near, other in ((0, own, far), (quarter, own_core, far_core)):
-        rows_out = slice(start, start + quarter)
-        out[rows_out, 0:lanes] = (
+        rows = slice(start, start + quarter)
+        out[rows, 0:lanes] = (
             dot(tokens[0], near[0:lanes, :]) + dot(tokens[1], other[0:lanes, :])
         ).astype(out.dtype)
-        out[rows_out, lanes:] = (
+        out[rows, lanes:] = (
             dot(cotangent[0], near[lanes:, :], NT) + dot(cotangent[1], other[lanes:, :], NT)
         ).astype(out.dtype)
 
@@ -181,14 +185,18 @@
             out[base + peer] = stage[peer].astype(out.dtype)
 
 
-def grads_kernel(acts, tokens, cotangent, mine, sibling):
+def grads_kernel(acts, tokens, cotangent, own, far, own_core, far_core):
     _, quarter, lanes = tokens.shape
-    units = mine.shape[1] - lanes
-    for start, out in ((quarter, sibling), (0, mine)):
+    units = own.shape[0] - lanes
+    for group, start, out in (
+        (1, quarter, far_core),
+        (1, 0, far),
+        (0, quarter, own_core),
+        (0, 0, own),
+    ):
         rows = slice(start, start + quarter)
-        for group in range(2):
-            out[group, 0:lanes, :] = dot(tokens[group], acts[rows, units:], TN).astype(out.dtype)
-            out[group, lanes:, :] = dot(acts[rows, 0:units], cotangent[group], TN).astype(out.dtype)
+        out[0:lanes, :] = dot(tokens[group], acts[rows, units:], TN).astype(out.dtype)
+        out[lanes:, :] = dot(acts[rows, 0:units], cotangent[group], TN).astype(out.dtype)
 
 
 def finish_kernel(parts, output, input_grad):
@@ -207,7 +215,7 @@
                 )
 
 
-def call(kernel, outs, args, smem=0, scratch=(), flops=0):
+def call(kernel, outs, args, smem=0, scratch=(), flops=0, limit=20 << 20):
     moved = sum(a.size * a.dtype.itemsize for a in args) + sum(
         o.size * jnp.dtype(o.dtype).itemsize for o in outs
     )
@@ -218,7 +226,7 @@
         in_specs=(SMEM,) * smem + (VMEM,) * (len(args) - smem),
         out_specs=VMEM if single else (VMEM,) * len(outs),
         scratch_shapes=scratch,
-        compiler_params=pltpu.CompilerParams(vmem_limit_bytes=20 << 20),
+        compiler_params=pltpu.CompilerParams(vmem_limit_bytes=limit),
         cost_estimate=pl.CostEstimate(flops=flops, bytes_accessed=moved, transcendentals=0),
     )(*args)
 
@@ -242,6 +250,7 @@
     packed = lanes // side * rows
     flops = 24 * quarter * lanes * units
     counts = tile_counts.reshape(3)
+    index = tile_index.transpose(0, 2, 1)
     me = lax.axis_index("xl").astype(jnp.int32).reshape(1)
     shape = jax.ShapeDtypeStruct
 
@@ -250,6 +259,7 @@
         (shape((2 * peers, packed, side), BF16),),
         (tokens, cotangent),
         scratch=(pltpu.VMEM((2 * packed, side), F32),),
+        limit=None,
     )
     spread, gate_tiles, up_tiles, down_tiles = lax.optimization_barrier(
         (spread, gate_tiles, up_tiles, down_tiles)
@@ -258,28 +268,31 @@
     own = call(
         weights_kernel,
         (shape((lanes + units, lanes), BF16),),
-        (tile_index, counts, gate_tiles, up_tiles, down_tiles),
+        (index, counts, gate_tiles, up_tiles, down_tiles),
         smem=2,
+        limit=None,
     )
     far = swap(own, "xl")
     own_core = swap(own, "core")
     far_core = swap(far, "core")
-    listing = jnp.concatenate([tile_index.reshape(3, 2 * slots), counts[:, None]], axis=1)
+    listing = jnp.concatenate([index.reshape(3, 2 * slots), counts[:, None]], axis=1)
     listing = swap(listing, "xl")
     far_core, listing = lax.optimization_barrier((far_core, listing))
-    far_index = listing[:, 0 : 2 * slots].reshape(3, slots, 2)
+    far_index = listing[:, 0 : 2 * slots].reshape(3, 2, slots)
     far_counts = listing[:, 2 * slots]
     weights = (own, far, own_core, far_core)
-    parts, all_tokens, all_cotangent = call(
-        partial_kernel,
-        (
-            shape((2 * quarter, 3 * units), BF16),
-            shape((2, quarter, lanes), BF16),
-            shape((2, quarter, lanes), BF16),
-        ),
-        (me, blocks, *weights),
+    all_tokens, all_cotangent = call(
+        unpack_kernel,
+        (shape((2, quarter, lanes), BF16),) * 2,
+        (me, blocks),
         smem=1,
         scratch=(pltpu.VMEM((2, quarter, 2 * lanes), F32),),
+        flops=LONG,
+    )
+    parts = call(
+        partial_kernel,
+        (shape((2 * quarter, 3 * units), BF16),),
+        (all_tokens, all_cotangent, *weights),
         flops=flops,
     )
     parts = exchange(parts.reshape(row_peers, share, 3 * units), ("xh", "yl"))
@@ -295,28 +308,28 @@
     )
     acts, sums = lax.optimization_barrier((acts, sums))
     sums = exchange(sums, ("xl", "yz"))
-    dense = (2, lanes + units, lanes)
-    mine, sibling = call(
+    dense = (lanes + units, lanes)
+    own_grad, far_grad, own_core, far_core = call(
         grads_kernel,
-        (shape(dense, F32), shape(dense, BF16)),
+        (shape(dense, F32),) * 2 + (shape(dense, BF16),) * 2,
         (acts, all_tokens, all_cotangent),
         flops=flops,
     )
     tile_shape = (slots, side, side)
-    own_grad, *far_grads = call(
+    far_grads = call(
         pair_kernel,
-        (shape(dense[1:], F32),) + (shape(tile_shape, BF16),) * 3,
-        (far_index, far_counts, mine, swap(sibling, "core")),
+        (shape(tile_shape, BF16),) * 3,
+        (far_index, far_counts, far_grad, swap(far_core, "core")),
         smem=2,
     )
     far_grads = swap(jnp.concatenate(far_grads), "xl").reshape(3, *tile_shape)
     gate_grad, up_grad, down_grad = call(
         tiles_kernel,
         (shape(tile_shape, F32),) * 3,
-        (tile_index, counts, own_grad, *far_grads),
+        (index, counts, own_grad, swap(own_core, "core"), *far_grads),
         smem=2,
     )
-    output, input_grad = call(finish_kernel, (shape((rows, lanes), BF16),) * 2, (sums,))
+    output, input_grad = call(finish_kernel, (shape((rows, lanes), BF16),) * 2, (sums,), flops=LONG)
     return (output, input_grad, gate_grad, up_grad, down_grad)
 
 

time: 142 us -> 142 us (level); the launches traced: 140 us -> 141 us
  local copies, waits for them, and re-layouts: 8.12 us -> 2.64 us
  starting transfers between devices: 55.4 us -> 60.7 us
  blocking collectives: 33.8 us -> 37.2 us
  waiting for transfers between devices: 28.6 us -> 26.4 us
    all_to_all x2, waiting for transfers between devices: 27.1 us -> 1.53 us  [exchange(): return lax.all_to_all(blocks, axis, split_axis=0, concat_axis=0, tiled=True)]
    ppermute x6 -> x7, waiting for transfers between devices: 1.5 us -> 24.9 us  [swap(): return lax.ppermute(block, axis, [(0, 1), (1, 0)])]
    all_to_all x2, starting transfers between devices: 30.1 us -> 37.2 us  [exchange(): return lax.all_to_all(blocks, axis, split_axis=0, concat_axis=0, tiled=True)]
    unnamed x21 -> x16, local copies, waits for them, and re-layouts: 7.66 us -> 2.16 us
    all_to_all x2, blocking collectives: 33.8 us -> 37.2 us  [exchange(): return lax.all_to_all(blocks, axis, split_axis=0, concat_axis=0, tiled=True)]
    ppermute x6 -> x7, starting transfers between devices: 25.3 us -> 23.5 us  [swap(): return lax.ppermute(block, axis, [(0, 1), (1, 0)])]
    pallas_call x9 -> x10, Pallas kernels: 12.7 us -> 13.3 us  [call(): pl.pallas_call(kernel, out_shape=outs[0] if single else outs, in_specs=(S...]
  transfers between devices with their start and end apart: 8 -> 9, of which waited for: 3 -> 4; matrix products, arithmetic and copies ran while one was open for 0% -> 0% of each run, Pallas kernels for 3% -> 5%
where the time goes in v4:
time: 142 us; the launch traced here: 141 us
  starting transfers between devices  60.7 us (43%)
  blocking collectives  37.2 us (26%)
  waiting for transfers between devices  26.4 us (19%)
  Pallas kernels  13.3 us (9%)
  local copies, waits for them, and re-layouts  2.64 us (2%)
    all_to_all x2, starting transfers between devices, exchange(): return lax.all_to_all(blocks, axis, split_axis=0, concat_axis=0, tiled=True)  37.2 us
    all_to_all x2, blocking collectives, exchange(): return lax.all_to_all(blocks, axis, split_axis=0, concat_axis=0, tiled=True)  37.2 us
    ppermute x7, waiting for transfers between devices, swap(): return lax.ppermute(block, axis, [(0, 1), (1, 0)])  24.9 us
    ppermute x7, starting transfers between devices, swap(): return lax.ppermute(block, axis, [(0, 1), (1, 0)])  23.5 us
    pallas_call x10, Pallas kernels, call(): pl.pallas_call(kernel, out_shape=outs[0] if single else outs, in_specs=(S...  13.3 us
  transfers between devices with their start and end apart: 9, of which 4 were waited for; matrix products, arithmetic and copies ran while one was open for 0% of the time, Pallas kernels for 5%

profile of v4, /device:TPU:1, one launch (start us, length us, event | category | flops | bytes accessed | tf_op | source)
XLA Modules:
  0.0 141.3 jit_solution(14427041908383527392)
XLA Ops:
  0.7 1.7 %shard_map.110 = bf16[64,40,128]{2,1,0:T(8,128)(2,1)} custom-call(bf16[10,512]{1,0:T(8,128)(2,1)} %tokens.1, bf16[10,512]{1,0:T(8,128)(2,1)} %cotangent.1), custom_call_target="tpu_custom_call" | custom-call | bytes 675840 | tf_op jit(solution)/shard_map/pallas_call | solution.py:223
  2.3 24.9 %all-to-all-start = ((bf16[64,40,128]{2,1,0:T(8,128)(2,1)}), bf16[64,40,128]{2,1,0:T(8,128)(2,1)S(1)}, u32[]{:S(2)}, u32[]{:S(2)}) async-start(bf16[64,40,128]{2,1,0:T(8,128)(2,1)} %shard_map.110), calls=%async_computation | async-start | bytes 1310720 | tf_op jit(solution)/shard_map/all_to_all | solution.py:235
  27.2 2.3 %shard_map.112.own = bf16[768,512]{1,0:T(8,128)(2,1)} custom-call(s32[3,2,6]{2,1,0:T(2,128)} %bitcast.10, s32[3]{0:T(128)} %bitcast.13, bf16[6,128,128]{2,1,0:T(8,128)(2,1)} %gate, bf16[6,128,128]{2,1,0:T(8,128)(2,1)} %up, bf16[6,128,128]{2,1,0:T(8,128)(2,1)} %down), custom_call_target="tpu_custom_call" | custom-call | bytes 1376412 | tf_op jit(solution)/shard_map/pallas_call | solution.py:223
  29.5 3.0 %collective-permute-start = (bf16[768,512]{1,0:T(8,128)(2,1)}, bf16[768,512]{1,0:T(8,128)(2,1)S(1)}, u32[]{:S(2)}, u32[]{:S(2)}) collective-permute-start(bf16[768,512]{1,0:T(8,128)(2,1)} %shard_map.112.own), channel_id=1, source_target_pairs={{0,128},{128,0},{1,129},{129,1},{2,130},{130,2},{3,131},{131,3},{4... | collective-permute-start | bytes 2359304 | tf_op jit(solution)/shard_map/ppermute | solution.py:239
  32.5 3.4 %collective-permute-start.1 = (bf16[768,512]{1,0:T(8,128)(2,1)}, bf16[768,512]{1,0:T(8,128)(2,1)S(1)}, u32[]{:S(2)}, u32[]{:S(2)}) collective-permute-start(bf16[768,512]{1,0:T(8,128)(2,1)} %shard_map.112.own), channel_id=1, source_target_pairs={{0,1},{1,0},{2,3},{3,2},{4,5},{5,4},{6,7},{7,6},{8,9},{9,8},{10,11... | collective-permute-start | bytes 2359304 | tf_op jit(solution)/shard_map/ppermute | solution.py:239
  36.0 0.1 reshape.37
  36.0 0.1 copy.13
  36.1 0.1 pad_add_fusion
  36.2 2.0 %collective-permute-start.3 = (s32[3,13]{1,0:T(4,128)S(1)}, s32[3,13]{1,0:T(4,128)S(1)}, u32[]{:S(2)}, u32[]{:S(2)}) collective-permute-start(s32[3,13]{1,0:T(4,128)S(1)} %pad_add_fusion), channel_id=1, source_target_pairs={{0,128},{128,0},{1,129},{129,1},{2,130},{130,2},{3,131},{131,3},{4... | collective-permute-start | bytes 476 | tf_op jit(solution)/shard_map/ppermute | solution.py:239
  38.2 13.7 %collective-permute-done.far = bf16[768,512]{1,0:T(8,128)(2,1)S(1)} collective-permute-done((bf16[768,512]{1,0:T(8,128)(2,1)}, bf16[768,512]{1,0:T(8,128)(2,1)S(1)}, u32[]{:S(2)}, u32[]{:S(2)}) %collective-permute-start) | collective-permute-done | bytes 786464 | tf_op jit(solution)/shard_map/ppermute | solution.py:239
  51.8 3.8 %collective-permute-start.2 = (bf16[768,512]{1,0:T(8,128)(2,1)S(1)}, bf16[768,512]{1,0:T(8,128)(2,1)S(1)}, u32[]{:S(2)}, u32[]{:S(2)}) collective-permute-start(bf16[768,512]{1,0:T(8,128)(2,1)S(1)} %collective-permute-done.far), channel_id=1, source_target_pairs={{0,1},{1,0},{2,3},{3,2},{4,5},{5,4},{6,7},{7,6},{8,9},{9,8},{10,11... | collective-permute-start | bytes 2359304 | tf_op jit(solution)/shard_map/ppermute | solution.py:239
  55.7 0.3 shard_map.111
  55.9 1.6 %collective-permute-done.2.far_core = bf16[768,512]{1,0:T(8,128)(2,1)S(1)} collective-permute-done((bf16[768,512]{1,0:T(8,128)(2,1)S(1)}, bf16[768,512]{1,0:T(8,128)(2,1)S(1)}, u32[]{:S(2)}, u32[]{:S(2)}) %collective-permute-start.2) | collective-permute-done | bytes 786464 | tf_op jit(solution)/shard_map/ppermute | solution.py:239
  57.5 0.8 shard_map.113
  58.4 20.4 %all_to_all.20.parts = bf16[8,40,768]{2,1,0:T(8,128)(2,1)S(1)} all-to-all(bf16[8,40,768]{2,1,0:T(8,128)(2,1)S(1)} %bitcast.9), channel_id=1, replica_groups=mesh['xh'=4,'xl'=2,'yl'=2,'yz'=32,'core'=2] {'xh','yl'}, dimensions={0} | all-to-all | bytes 983040 | tf_op jit(solution)/shard_map/all_to_all | solution.py:235
  78.8 0.1 shard_map.114
  78.9 16.8 %all_to_all.21 = bf16[8,40,768]{2,1,0:T(8,128)(2,1)S(1)} all-to-all(bf16[8,40,768]{2,1,0:T(8,128)(2,1)S(1)} %shard_map.114), channel_id=1, replica_groups=mesh['xh'=4,'xl'=2,'yl'=2,'yz'=32,'core'=2] {'xh','yl'}, dimensions={0} | all-to-all | bytes 983040 | tf_op jit(solution)/shard_map/all_to_all | solution.py:235
  95.7 2.1 %shard_map.115 = bf16[64,40,128]{2,1,0:T(8,128)(2,1)} custom-call(s32[1]{0:T(128)} %bitcast.me, bf16[320,768]{1,0:T(8,128)(2,1)S(1)} %bitcast.7, bf16[768,512]{1,0:T(8,128)(2,1)S(1)} %copy-done, bf16[768,512]{1,0:T(8,128)(2,1)S(1)} %collective-permute-done.far, bf16[768,512]{1,0:T(8,128)(2,1)S(1)} %collective-permute-done.1.own_core, ...), custom_call_target="tpu_custom_call" | custom-call | flops 503316480 | bytes 4292612 | tf_op jit(solution)/shard_map/pallas_call | solution.py:223
  97.7 12.4 %all-to-all-start.3 = ((bf16[64,40,128]{2,1,0:T(8,128)(2,1)}), bf16[64,40,128]{2,1,0:T(8,128)(2,1)}, u32[]{:S(2)}, u32[]{:S(2)}) async-start(bf16[64,40,128]{2,1,0:T(8,128)(2,1)} %shard_map.115), calls=%async_computation.3 | async-start | bytes 1310720 | tf_op jit(solution)/shard_map/all_to_all | solution.py:235
  110.1 1.0 copy-done.4
  111.1 1.3 shard_map.117
  112.4 1.2 copy-done.1
  113.6 6.2 %collective-permute-start.5 = (bf16[768,512]{1,0:T(8,128)(2,1)}, bf16[768,512]{1,0:T(8,128)(2,1)S(1)}, u32[]{:S(2)}, u32[]{:S(2)}) collective-permute-start(bf16[768,512]{1,0:T(8,128)(2,1)} %get-tuple-element.42), channel_id=1, source_target_pairs={{0,1},{1,0},{2,3},{3,2},{4,5},{5,4},{6,7},{7,6},{8,9},{9,8},{10,11... | collective-permute-start | bytes 2359304 | tf_op jit(solution)/shard_map/ppermute | solution.py:239
  119.7 0.1 reshape.40.far_index
  119.8 0.2 slice_reduce_fusion.far_counts
  120.0 1.9 %collective-permute-start.4 = (bf16[768,512]{1,0:T(8,128)(2,1)}, bf16[768,512]{1,0:T(8,128)(2,1)S(1)}, u32[]{:S(2)}, u32[]{:S(2)}) collective-permute-start(bf16[768,512]{1,0:T(8,128)(2,1)} %copy-done.7), channel_id=1, source_target_pairs={{0,1},{1,0},{2,3},{3,2},{4,5},{5,4},{6,7},{7,6},{8,9},{9,8},{10,11... | collective-permute-start | bytes 2359304 | tf_op jit(solution)/shard_map/ppermute | solution.py:239
  121.9 1.0 shard_map.118
  123.0 3.2 %collective-permute-start.6 = (bf16[18,128,128]{2,1,0:T(8,128)(2,1)S(1)}, bf16[18,128,128]{2,1,0:T(8,128)(2,1)S(1)}, u32[]{:S(2)}, u32[]{:S(2)}) collective-permute-start(bf16[18,128,128]{2,1,0:T(8,128)(2,1)S(1)} %pad_maximum_fusion), channel_id=1, source_target_pairs={{0,128},{128,0},{1,129},{129,1},{2,130},{130,2},{3,131},{131,3},{4... | collective-permute-start | bytes 1769480 | tf_op jit(solution)/shard_map/ppermute | solution.py:239
  126.2 1.5 %all-to-all-done.3.parts = bf16[64,40,128]{2,1,0:T(8,128)(2,1)} async-done(((bf16[64,40,128]{2,1,0:T(8,128)(2,1)}), bf16[64,40,128]{2,1,0:T(8,128)(2,1)}, u32[]{:S(2)}, u32[]{:S(2)}) %all-to-all-start.3) | async-done | bytes 655392 | tf_op jit(solution)/shard_map/all_to_all | solution.py:235
  127.7 1.9 %shard_map.116 = (bf16[10,512]{1,0:T(8,128)(2,1)}, bf16[10,512]{1,0:T(8,128)(2,1)}) custom-call(bf16[64,40,128]{2,1,0:T(8,128)(2,1)} %all-to-all-done.3.parts), custom_call_target="tpu_custom_call" | custom-call | flops 68719476736 | bytes 675840 | tf_op jit(solution)/shard_map/pallas_call | solution.py:223
  129.7 9.6 %collective-permute-done.6 = bf16[18,128,128]{2,1,0:T(8,128)(2,1)S(1)} collective-permute-done((bf16[18,128,128]{2,1,0:T(8,128)(2,1)S(1)}, bf16[18,128,128]{2,1,0:T(8,128)(2,1)S(1)}, u32[]{:S(2)}, u32[]{:S(2)}) %collective-permute-start.6) | collective-permute-done | bytes 589856 | tf_op jit(solution)/shard_map/ppermute | solution.py:239
  139.3 1.9 %shard_map.119 = (f32[6,128,128]{2,1,0:T(8,128)}, f32[6,128,128]{2,1,0:T(8,128)}, f32[6,128,128]{2,1,0:T(8,128)}) custom-call(s32[3,2,6]{2,1,0:T(2,128)S(1)} %bitcast.12, s32[3]{0:T(128)S(1)} %bitcast.15, f32[768,512]{1,0:T(8,128)S(1)} %copy-done.2, bf16[768,512]{1,0:T(8,128)(2,1)S(1)} %collective-permute-done.4.received, ...), custom_call_target="tpu_custom_call" | custom-call | bytes 4128924 | tf_op jit(solution)/shard_map/pallas_call | solution.py:223
  (21 shorter events, 0.2 us)
Async XLA Ops:
  0.6 35.3 %copy-start.5 = (s32[3,6,2]{1,2,0:T(2,128)S(1)}, s32[3,6,2]{1,2,0:T(2,128)}, u32[]{:S(2)}) copy-start(s32[3,6,2]{1,2,0:T(2,128)} %param.12) | copy-start | bytes 436
  0.6 35.4 %copy-start.6 = (s32[3,1,1]{0,2,1:T(1,128)S(1)}, s32[3,1,1]{0,2,1:T(1,128)}, u32[]{:S(2)}) copy-start(s32[3,1,1]{0,2,1:T(1,128)} %param.13) | copy-start | bytes 40
  2.3 53.3 %all-to-all-start = ((bf16[64,40,128]{2,1,0:T(8,128)(2,1)}), bf16[64,40,128]{2,1,0:T(8,128)(2,1)S(1)}, u32[]{:S(2)}, u32[]{:S(2)}) async-start(bf16[64,40,128]{2,1,0:T(8,128)(2,1)} %shard_map.110), calls=%async_computation | async-start | bytes 1310720 | tf_op jit(solution)/shard_map/all_to_all | solution.py:235
  29.5 22.3 %collective-permute-start = (bf16[768,512]{1,0:T(8,128)(2,1)}, bf16[768,512]{1,0:T(8,128)(2,1)S(1)}, u32[]{:S(2)}, u32[]{:S(2)}) collective-permute-start(bf16[768,512]{1,0:T(8,128)(2,1)} %shard_map.112.own), channel_id=1, source_target_pairs={{0,128},{128,0},{1,129},{129,1},{2,130},{130,2},{3,131},{131,3},{4... | collective-permute-start | bytes 2359304 | tf_op jit(solution)/shard_map/ppermute | solution.py:239
  32.5 25.0 %collective-permute-start.1 = (bf16[768,512]{1,0:T(8,128)(2,1)}, bf16[768,512]{1,0:T(8,128)(2,1)S(1)}, u32[]{:S(2)}, u32[]{:S(2)}) collective-permute-start(bf16[768,512]{1,0:T(8,128)(2,1)} %shard_map.112.own), channel_id=1, source_target_pairs={{0,1},{1,0},{2,3},{3,2},{4,5},{5,4},{6,7},{7,6},{8,9},{9,8},{10,11... | collective-permute-start | bytes 2359304 | tf_op jit(solution)/shard_map/ppermute | solution.py:239
  36.2 19.7 %collective-permute-start.3 = (s32[3,13]{1,0:T(4,128)S(1)}, s32[3,13]{1,0:T(4,128)S(1)}, u32[]{:S(2)}, u32[]{:S(2)}) collective-permute-start(s32[3,13]{1,0:T(4,128)S(1)} %pad_add_fusion), channel_id=1, source_target_pairs={{0,128},{128,0},{1,129},{129,1},{2,130},{130,2},{3,131},{131,3},{4... | collective-permute-start | bytes 476 | tf_op jit(solution)/shard_map/ppermute | solution.py:239
  51.8 5.7 %collective-permute-start.2 = (bf16[768,512]{1,0:T(8,128)(2,1)S(1)}, bf16[768,512]{1,0:T(8,128)(2,1)S(1)}, u32[]{:S(2)}, u32[]{:S(2)}) collective-permute-start(bf16[768,512]{1,0:T(8,128)(2,1)S(1)} %collective-permute-done.far), channel_id=1, source_target_pairs={{0,1},{1,0},{2,3},{3,2},{4,5},{5,4},{6,7},{7,6},{8,9},{9,8},{10,11... | collective-permute-start | bytes 2359304 | tf_op jit(solution)/shard_map/ppermute | solution.py:239
  55.6 1.9 %copy-start = (bf16[768,512]{1,0:T(8,128)(2,1)S(1)}, bf16[768,512]{1,0:T(8,128)(2,1)}, u32[]{:S(2)}) copy-start(bf16[768,512]{1,0:T(8,128)(2,1)} %shard_map.112.own) | copy-start | bytes 2359300
  55.9 2.4 %copy-start.3 = (bf16[2,160,512]{2,1,0:T(8,128)(2,1)}, bf16[2,160,512]{2,1,0:T(8,128)(2,1)S(1)}, u32[]{:S(2)}) copy-start(bf16[2,160,512]{2,1,0:T(8,128)(2,1)S(1)} %get-tuple-element.29.cotangent) | copy-start | bytes 983044
  97.7 30.0 %all-to-all-start.3 = ((bf16[64,40,128]{2,1,0:T(8,128)(2,1)}), bf16[64,40,128]{2,1,0:T(8,128)(2,1)}, u32[]{:S(2)}, u32[]{:S(2)}) async-start(bf16[64,40,128]{2,1,0:T(8,128)(2,1)} %shard_map.115), calls=%async_computation.3 | async-start | bytes 1310720 | tf_op jit(solution)/shard_map/all_to_all | solution.py:235
  110.1 1.0 copy-start.4
  112.4 1.2 copy-start.1
  113.5 6.2 %copy-start.7 = (bf16[768,512]{1,0:T(8,128)(2,1)}, bf16[768,512]{1,0:T(8,128)(2,1)S(1)}, u32[]{:S(2)}) copy-start(bf16[768,512]{1,0:T(8,128)(2,1)S(1)} %get-tuple-element.39) | copy-start | bytes 2359300
  113.6 8.4 %collective-permute-start.5 = (bf16[768,512]{1,0:T(8,128)(2,1)}, bf16[768,512]{1,0:T(8,128)(2,1)S(1)}, u32[]{:S(2)}, u32[]{:S(2)}) collective-permute-start(bf16[768,512]{1,0:T(8,128)(2,1)} %get-tuple-element.42), channel_id=1, source_target_pairs={{0,1},{1,0},{2,3},{3,2},{4,5},{5,4},{6,7},{7,6},{8,9},{9,8},{10,11... | collective-permute-start | bytes 2359304 | tf_op jit(solution)/shard_map/ppermute | solution.py:239
  120.0 19.3 %collective-permute-start.4 = (bf16[768,512]{1,0:T(8,128)(2,1)}, bf16[768,512]{1,0:T(8,128)(2,1)S(1)}, u32[]{:S(2)}, u32[]{:S(2)}) collective-permute-start(bf16[768,512]{1,0:T(8,128)(2,1)} %copy-done.7), channel_id=1, source_target_pairs={{0,1},{1,0},{2,3},{3,2},{4,5},{5,4},{6,7},{7,6},{8,9},{9,8},{10,11... | collective-permute-start | bytes 2359304 | tf_op jit(solution)/shard_map/ppermute | solution.py:239
  123.0 16.3 %collective-permute-start.6 = (bf16[18,128,128]{2,1,0:T(8,128)(2,1)S(1)}, bf16[18,128,128]{2,1,0:T(8,128)(2,1)S(1)}, u32[]{:S(2)}, u32[]{:S(2)}) collective-permute-start(bf16[18,128,128]{2,1,0:T(8,128)(2,1)S(1)} %pad_maximum_fusion), channel_id=1, source_target_pairs={{0,128},{128,0},{1,129},{129,1},{2,130},{130,2},{3,131},{131,3},{4... | collective-permute-start | bytes 1769480 | tf_op jit(solution)/shard_map/ppermute | solution.py:239
  127.7 11.6 %copy-start.2 = (f32[768,512]{1,0:T(8,128)S(1)}, f32[768,512]{1,0:T(8,128)}, u32[]{:S(2)}) copy-start(f32[768,512]{1,0:T(8,128)} %copy-done.1) | copy-start | bytes 4718596

commit v5 on v4

--- a/solution.py
+++ b/solution.py
@@ -7,6 +7,7 @@
 from jax.sharding import PartitionSpec as P
 
 LONG = 1 << 36
+UNPACK = 0
 F32 = jnp.float32
 BF16 = jnp.bfloat16
 VMEM = pl.BlockSpec(memory_space=pltpu.VMEM)
@@ -63,25 +64,12 @@
     return pl.ds(row, side), pl.ds(col, side)
 
 
-def pair_kernel(far_index, far_counts, mine, received, gate_out, up_out, down_out):
-    lanes = mine.shape[1]
+def tiles_kernel(index, counts, own, received, gate_out, up_out, down_out):
+    lanes = own.shape[1]
 
     def read(which, slot, row, col):
         at = place(which, row, col, lanes, gate_out.shape[-1])
-        return (mine[at] + received[at].astype(F32)).astype(gate_out.dtype)
-
-    take_tiles((gate_out, up_out, down_out), far_index, far_counts, read)
-
-
-def tiles_kernel(
-    index, counts, mine, received, gate_far, up_far, down_far, gate_out, up_out, down_out
-):
-    lanes = mine.shape[1]
-    far = (gate_far, up_far, down_far)
-
-    def read(which, slot, row, col):
-        at = place(which, row, col, lanes, gate_out.shape[-1])
-        return mine[at] + received[at].astype(F32) + far[which][slot].astype(F32)
+        return own[at] + received[at].astype(F32)
 
     take_tiles((gate_out, up_out, down_out), index, counts, read)
 
@@ -105,13 +93,13 @@
             out[group * peers + peer] = packed
 
 
-def unpack_kernel(me, blocks, tokens, cotangent, stage):
-    _, quarter, lanes = tokens.shape
+def unpack_kernel(me, blocks, own, far, stage):
+    _, quarter, lanes = own.shape
     side = blocks.shape[-1]
     peers = blocks.shape[0] // 2
     rows = quarter // peers
     chunks = lanes // side
-    for group in range(2):
+    for group, out in ((0, own), (1, far)):
         base = (me[0] if group == 0 else 1 - me[0]) * peers
         for peer in range(peers):
             block = blocks[base + peer].astype(F32)
@@ -119,19 +107,19 @@
                 stage[group, peer * rows : (peer + 1) * rows, q * side : (q + 1) * side] = block[
                     q * rows : (q + 1) * rows
                 ]
-        tokens[group] = stage[group, :, 0:lanes].astype(tokens.dtype)
-        cotangent[group] = stage[group, :, lanes:].astype(cotangent.dtype)
-
-
-def partial_kernel(tokens, cotangent, own, far, own_core, far_core, out):
-    _, quarter, lanes = tokens.shape
+        out[0] = stage[group, :, 0:lanes].astype(out.dtype)
+        out[1] = stage[group, :, lanes:].astype(out.dtype)
+
+
+def partial_kernel(own_rows, far_rows, own, far, own_core, far_core, out):
+    _, quarter, lanes = own_rows.shape
     for start, near, other in ((0, own, far), (quarter, own_core, far_core)):
         rows = slice(start, start + quarter)
         out[rows, 0:lanes] = (
-            dot(tokens[0], near[0:lanes, :]) + dot(tokens[1], other[0:lanes, :])
+            dot(own_rows[0], near[0:lanes, :]) + dot(far_rows[0], other[0:lanes, :])
         ).astype(out.dtype)
         out[rows, lanes:] = (
-            dot(cotangent[0], near[lanes:, :], NT) + dot(cotangent[1], other[lanes:, :], NT)
+            dot(own_rows[1], near[lanes:, :], NT) + dot(far_rows[1], other[lanes:, :], NT)
         ).astype(out.dtype)
 
 
@@ -185,18 +173,18 @@
             out[base + peer] = stage[peer].astype(out.dtype)
 
 
-def grads_kernel(acts, tokens, cotangent, own, far, own_core, far_core):
-    _, quarter, lanes = tokens.shape
+def grads_kernel(acts, far_acts, own_rows, far_rows, own, sibling):
+    _, quarter, lanes = own_rows.shape
     units = own.shape[0] - lanes
-    for group, start, out in (
-        (1, quarter, far_core),
-        (1, 0, far),
-        (0, quarter, own_core),
-        (0, 0, own),
-    ):
+    for start, out in ((quarter, sibling), (0, own)):
         rows = slice(start, start + quarter)
-        out[0:lanes, :] = dot(tokens[group], acts[rows, units:], TN).astype(out.dtype)
-        out[lanes:, :] = dot(acts[rows, 0:units], cotangent[group], TN).astype(out.dtype)
+        out[0:lanes, :] = (
+            dot(own_rows[0], acts[rows, units:], TN) + dot(far_rows[0], far_acts[rows, units:], TN)
+        ).astype(out.dtype)
+        out[lanes:, :] = (
+            dot(acts[rows, 0:units], own_rows[1], TN)
+            + dot(far_acts[rows, 0:units], far_rows[1], TN)
+        ).astype(out.dtype)
 
 
 def finish_kernel(parts, output, input_grad):
@@ -215,7 +203,7 @@
                 )
 
 
-def call(kernel, outs, args, smem=0, scratch=(), flops=0, limit=20 << 20):
+def call(kernel, outs, args, smem=0, scratch=(), flops=0, limit=12 << 20):
     moved = sum(a.size * a.dtype.itemsize for a in args) + sum(
         o.size * jnp.dtype(o.dtype).itemsize for o in outs
     )
@@ -275,24 +263,19 @@
     far = swap(own, "xl")
     own_core = swap(own, "core")
     far_core = swap(far, "core")
-    listing = jnp.concatenate([index.reshape(3, 2 * slots), counts[:, None]], axis=1)
-    listing = swap(listing, "xl")
-    far_core, listing = lax.optimization_barrier((far_core, listing))
-    far_index = listing[:, 0 : 2 * slots].reshape(3, 2, slots)
-    far_counts = listing[:, 2 * slots]
     weights = (own, far, own_core, far_core)
-    all_tokens, all_cotangent = call(
+    own_rows, far_rows = call(
         unpack_kernel,
         (shape((2, quarter, lanes), BF16),) * 2,
         (me, blocks),
         smem=1,
         scratch=(pltpu.VMEM((2, quarter, 2 * lanes), F32),),
-        flops=LONG,
+        flops=UNPACK,
     )
     parts = call(
         partial_kernel,
         (shape((2 * quarter, 3 * units), BF16),),
-        (all_tokens, all_cotangent, *weights),
+        (own_rows, far_rows, *weights),
         flops=flops,
     )
     parts = exchange(parts.reshape(row_peers, share, 3 * units), ("xh", "yl"))
@@ -306,27 +289,19 @@
         scratch=(pltpu.VMEM((quarter, 2 * lanes), F32), pltpu.VMEM((peers, packed, side), F32)),
         flops=flops,
     )
-    acts, sums = lax.optimization_barrier((acts, sums))
     sums = exchange(sums, ("xl", "yz"))
+    far_acts, far_rows = swap(acts, "xl"), swap(far_rows, "xl")
     dense = (lanes + units, lanes)
-    own_grad, far_grad, own_core, far_core = call(
+    own_grad, sibling_grad = call(
         grads_kernel,
-        (shape(dense, F32),) * 2 + (shape(dense, BF16),) * 2,
-        (acts, all_tokens, all_cotangent),
+        (shape(dense, F32), shape(dense, BF16)),
+        (acts, far_acts, own_rows, far_rows),
         flops=flops,
     )
-    tile_shape = (slots, side, side)
-    far_grads = call(
-        pair_kernel,
-        (shape(tile_shape, BF16),) * 3,
-        (far_index, far_counts, far_grad, swap(far_core, "core")),
-        smem=2,
-    )
-    far_grads = swap(jnp.concatenate(far_grads), "xl").reshape(3, *tile_shape)
     gate_grad, up_grad, down_grad = call(
         tiles_kernel,
-        (shape(tile_shape, F32),) * 3,
-        (index, counts, own_grad, swap(own_core, "core"), *far_grads),
+        (shape((slots, side, side), F32),) * 3,
+        (index, counts, own_grad, swap(sibling_grad, "core")),
         smem=2,
     )
     output, input_grad = call(finish_kernel, (shape((rows, lanes), BF16),) * 2, (sums,), flops=LONG)

time: 142 us -> 134 us (0.944)
  starting transfers between devices: 60.7 us -> 56.2 us
  blocking collectives: 37.2 us -> 33.6 us
  waiting for transfers between devices: 26.4 us -> 28.5 us
  local copies, waits for them, and re-layouts: 2.64 us -> 0.85 us
    all_to_all x2, waiting for transfers between devices: 1.53 us -> 16.1 us  [exchange(): return lax.all_to_all(blocks, axis, split_axis=0, concat_axis=0, tiled=True)]
    ppermute x7 -> x6, waiting for transfers between devices: 24.9 us -> 12.4 us  [swap(): return lax.ppermute(block, axis, [(0, 1), (1, 0)])]
    all_to_all x2, starting transfers between devices: 37.2 us -> 30.9 us  [exchange(): return lax.all_to_all(blocks, axis, split_axis=0, concat_axis=0, tiled=True)]
    all_to_all x2, blocking collectives: 37.2 us -> 33.6 us  [exchange(): return lax.all_to_all(blocks, axis, split_axis=0, concat_axis=0, tiled=True)]
    ppermute x7 -> x6, starting transfers between devices: 23.5 us -> 25.3 us  [swap(): return lax.ppermute(block, axis, [(0, 1), (1, 0)])]
    pallas_call x10 -> x9, Pallas kernels: 13.3 us -> 13.3 us  [call(): pl.pallas_call(kernel, out_shape=outs[0] if single else outs, in_specs=(S...]
  transfers between devices with their start and end apart: 9 -> 8, of which waited for: 4 -> 3; matrix products, arithmetic and copies ran while one was open for 0% -> 0% of each run, Pallas kernels for 5% -> 6%
where the time goes in v5:
time: 134 us; the launch traced here: 133 us
  starting transfers between devices  56.2 us (42%)
  blocking collectives  33.6 us (25%)
  waiting for transfers between devices  28.5 us (21%)
  Pallas kernels  13.3 us (10%)
    all_to_all x2, blocking collectives, exchange(): return lax.all_to_all(blocks, axis, split_axis=0, concat_axis=0, tiled=True)  33.6 us
    all_to_all x2, starting transfers between devices, exchange(): return lax.all_to_all(blocks, axis, split_axis=0, concat_axis=0, tiled=True)  30.9 us
    ppermute x6, starting transfers between devices, swap(): return lax.ppermute(block, axis, [(0, 1), (1, 0)])  25.3 us
    all_to_all x2, waiting for transfers between devices, exchange(): return lax.all_to_all(blocks, axis, split_axis=0, concat_axis=0, tiled=True)  16.1 us
    pallas_call x9, Pallas kernels, call(): pl.pallas_call(kernel, out_shape=outs[0] if single else outs, in_specs=(S...  13.3 us
    ppermute x6, waiting for transfers between devices, swap(): return lax.ppermute(block, axis, [(0, 1), (1, 0)])  12.4 us
  transfers between devices with their start and end apart: 8, of which 3 were waited for; matrix products, arithmetic and copies ran while one was open for 0% of the time, Pallas kernels for 6%

profile of v5, /device:TPU:1, one launch (start us, length us, event | category | flops | bytes accessed | tf_op | source)
XLA Modules:
  0.0 133.1 jit_solution(4042192251342386983)
XLA Ops:
  0.6 1.7 %shard_map.110 = bf16[64,40,128]{2,1,0:T(8,128)(2,1)} custom-call(bf16[10,512]{1,0:T(8,128)(2,1)} %tokens.1, bf16[10,512]{1,0:T(8,128)(2,1)} %cotangent.1), custom_call_target="tpu_custom_call" | custom-call | bytes 675840 | tf_op jit(solution)/shard_map/pallas_call | solution.py:211
  2.3 2.2 %shard_map.112.own = bf16[768,512]{1,0:T(8,128)(2,1)} custom-call(s32[3,2,6]{2,1,0:T(2,128)} %bitcast.6, s32[3]{0:T(128)} %bitcast.8, bf16[6,128,128]{2,1,0:T(8,128)(2,1)} %gate, bf16[6,128,128]{2,1,0:T(8,128)(2,1)} %up, bf16[6,128,128]{2,1,0:T(8,128)(2,1)} %down), custom_call_target="tpu_custom_call" | custom-call | bytes 1376412 | tf_op jit(solution)/shard_map/pallas_call | solution.py:211
  4.5 4.1 %collective-permute-start = (bf16[768,512]{1,0:T(8,128)(2,1)}, bf16[768,512]{1,0:T(8,128)(2,1)S(1)}, u32[]{:S(2)}, u32[]{:S(2)}) collective-permute-start(bf16[768,512]{1,0:T(8,128)(2,1)} %shard_map.112.own), channel_id=1, source_target_pairs={{0,128},{128,0},{1,129},{129,1},{2,130},{130,2},{3,131},{131,3},{4... | collective-permute-start | bytes 2359304 | tf_op jit(solution)/shard_map/ppermute | solution.py:227
  8.6 23.5 %all-to-all-start = ((bf16[64,40,128]{2,1,0:T(8,128)(2,1)}), bf16[64,40,128]{2,1,0:T(8,128)(2,1)}, u32[]{:S(2)}, u32[]{:S(2)}) async-start(bf16[64,40,128]{2,1,0:T(8,128)(2,1)} %shard_map.110), calls=%async_computation | async-start | bytes 1310720 | tf_op jit(solution)/shard_map/all_to_all | solution.py:223
  32.1 3.1 %collective-permute-start.1 = (bf16[768,512]{1,0:T(8,128)(2,1)}, bf16[768,512]{1,0:T(8,128)(2,1)S(1)}, u32[]{:S(2)}, u32[]{:S(2)}) collective-permute-start(bf16[768,512]{1,0:T(8,128)(2,1)} %shard_map.112.own), channel_id=1, source_target_pairs={{0,1},{1,0},{2,3},{3,2},{4,5},{5,4},{6,7},{7,6},{8,9},{9,8},{10,11... | collective-permute-start | bytes 2359304 | tf_op jit(solution)/shard_map/ppermute | solution.py:227
  35.2 0.0 collective-permute-done.far
  35.2 1.9 %collective-permute-start.2 = (bf16[768,512]{1,0:T(8,128)(2,1)S(1)}, bf16[768,512]{1,0:T(8,128)(2,1)S(1)}, u32[]{:S(2)}, u32[]{:S(2)}) collective-permute-start(bf16[768,512]{1,0:T(8,128)(2,1)S(1)} %collective-permute-done.far), channel_id=1, source_target_pairs={{0,1},{1,0},{2,3},{3,2},{4,5},{5,4},{6,7},{7,6},{8,9},{9,8},{10,11... | collective-permute-start | bytes 2359304 | tf_op jit(solution)/shard_map/ppermute | solution.py:227
  37.2 16.1 %all-to-all-done.blocks = bf16[64,40,128]{2,1,0:T(8,128)(2,1)} async-done(((bf16[64,40,128]{2,1,0:T(8,128)(2,1)}), bf16[64,40,128]{2,1,0:T(8,128)(2,1)}, u32[]{:S(2)}, u32[]{:S(2)}) %all-to-all-start) | async-done | bytes 655392 | tf_op jit(solution)/shard_map/all_to_all | solution.py:223
  53.3 1.3 %shard_map.111 = (bf16[2,160,512]{2,1,0:T(8,128)(2,1)S(1)}, bf16[2,160,512]{2,1,0:T(8,128)(2,1)S(1)}) custom-call(s32[1]{0:T(128)} %bitcast.me, bf16[64,40,128]{2,1,0:T(8,128)(2,1)} %all-to-all-done.blocks), custom_call_target="tpu_custom_call" | custom-call | bytes 1310724 | tf_op jit(solution)/shard_map/pallas_call | solution.py:211
  54.7 0.0 copy-start.2
  54.7 0.0 collective-permute-done.1.own_core
  54.7 0.0 collective-permute-done.2.far_core
  54.7 0.0 copy-done
  54.7 0.8 shard_map.113
  55.5 0.0 copy-done.2
  55.5 18.8 %all_to_all.20.parts = bf16[8,40,768]{2,1,0:T(8,128)(2,1)S(1)} all-to-all(bf16[8,40,768]{2,1,0:T(8,128)(2,1)S(1)} %bitcast.5), channel_id=1, replica_groups=mesh['xh'=4,'xl'=2,'yl'=2,'yz'=32,'core'=2] {'xh','yl'}, dimensions={0} | all-to-all | bytes 983040 | tf_op jit(solution)/shard_map/all_to_all | solution.py:223
  74.3 0.1 shard_map.114
  74.4 14.8 %all_to_all.21 = bf16[8,40,768]{2,1,0:T(8,128)(2,1)} all-to-all(bf16[8,40,768]{2,1,0:T(8,128)(2,1)S(1)} %shard_map.114), channel_id=1, replica_groups=mesh['xh'=4,'xl'=2,'yl'=2,'yz'=32,'core'=2] {'xh','yl'}, dimensions={0} | all-to-all | bytes 983040 | tf_op jit(solution)/shard_map/all_to_all | solution.py:223
  89.2 8.1 %collective-permute-start.3 = (bf16[320,768]{1,0:T(8,128)(2,1)}, bf16[320,768]{1,0:T(8,128)(2,1)}, u32[]{:S(2)}, u32[]{:S(2)}) collective-permute-start(bf16[320,768]{1,0:T(8,128)(2,1)} %bitcast.4.acts), channel_id=1, source_target_pairs={{0,128},{128,0},{1,129},{129,1},{2,130},{130,2},{3,131},{131,3},{4... | collective-permute-start | bytes 1474568 | tf_op jit(solution)/shard_map/ppermute | solution.py:227
  97.3 2.2 %shard_map.115 = bf16[64,40,128]{2,1,0:T(8,128)(2,1)S(1)} custom-call(s32[1]{0:T(128)} %bitcast.me, bf16[320,768]{1,0:T(8,128)(2,1)} %bitcast.4.acts, bf16[768,512]{1,0:T(8,128)(2,1)S(1)} %copy-done, bf16[768,512]{1,0:T(8,128)(2,1)S(1)} %collective-permute-done.far, bf16[768,512]{1,0:T(8,128)(2,1)S(1)} %collective-permute-done.1.own_core, ...), custom_call_target="tpu_custom_call" | custom-call | flops 503316480 | bytes 4292612 | tf_op jit(solution)/shard_map/pallas_call | solution.py:211
  99.6 0.8 copy-done.1
  100.4 7.4 %all-to-all-start.3 = ((bf16[64,40,128]{2,1,0:T(8,128)(2,1)}), bf16[64,40,128]{2,1,0:T(8,128)(2,1)S(1)}, u32[]{:S(2)}, u32[]{:S(2)}) async-start(bf16[64,40,128]{2,1,0:T(8,128)(2,1)} %copy-done.1), calls=%async_computation.3 | async-start | bytes 1310720 | tf_op jit(solution)/shard_map/all_to_all | solution.py:223
  107.8 3.0 %collective-permute-start.4 = (bf16[2,160,512]{2,1,0:T(8,128)(2,1)}, bf16[2,160,512]{2,1,0:T(8,128)(2,1)S(1)}, u32[]{:S(2)}, u32[]{:S(2)}) collective-permute-start(bf16[2,160,512]{2,1,0:T(8,128)(2,1)} %copy-done.2), channel_id=1, source_target_pairs={{0,128},{128,0},{1,129},{129,1},{2,130},{130,2},{3,131},{131,3},{4... | collective-permute-start | bytes 983048 | tf_op jit(solution)/shard_map/ppermute | solution.py:227
  110.8 10.5 %collective-permute-done.4.far_rows = bf16[2,160,512]{2,1,0:T(8,128)(2,1)S(1)} collective-permute-done((bf16[2,160,512]{2,1,0:T(8,128)(2,1)}, bf16[2,160,512]{2,1,0:T(8,128)(2,1)S(1)}, u32[]{:S(2)}, u32[]{:S(2)}) %collective-permute-start.4) | collective-permute-done | bytes 327712 | tf_op jit(solution)/shard_map/ppermute | solution.py:227
  121.3 0.0 collective-permute-done.3.far_acts
  121.3 2.2 %shard_map.117 = (f32[768,512]{1,0:T(8,128)S(1)}, bf16[768,512]{1,0:T(8,128)(2,1)S(1)}) custom-call(bf16[320,768]{1,0:T(8,128)(2,1)} %bitcast.4.acts, bf16[320,768]{1,0:T(8,128)(2,1)} %collective-permute-done.3.far_acts, bf16[2,160,512]{2,1,0:T(8,128)(2,1)S(1)} %get-tuple-element.19.own_rows, bf16[2,160,512]{2,1,0:T(8,128)(2,1)S(1)} %collective-permute-done.4.far_rows), custom_call_target="tpu_custom_call" | custom-call | flops 503316480 | bytes 3997696 | tf_op jit(solution)/shard_map/pallas_call | solution.py:211
  123.5 5.1 %collective-permute-start.5 = (bf16[768,512]{1,0:T(8,128)(2,1)S(1)}, bf16[768,512]{1,0:T(8,128)(2,1)S(1)}, u32[]{:S(2)}, u32[]{:S(2)}) collective-permute-start(bf16[768,512]{1,0:T(8,128)(2,1)S(1)} %get-tuple-element.27), channel_id=1, source_target_pairs={{0,1},{1,0},{2,3},{3,2},{4,5},{5,4},{6,7},{7,6},{8,9},{9,8},{10,11... | collective-permute-start | bytes 2359304 | tf_op jit(solution)/shard_map/ppermute | solution.py:227
  128.6 1.9 %collective-permute-done.5.received = bf16[768,512]{1,0:T(8,128)(2,1)S(1)} collective-permute-done((bf16[768,512]{1,0:T(8,128)(2,1)S(1)}, bf16[768,512]{1,0:T(8,128)(2,1)S(1)}, u32[]{:S(2)}, u32[]{:S(2)}) %collective-permute-start.5) | collective-permute-done | bytes 786464 | tf_op jit(solution)/shard_map/ppermute | solution.py:227
  130.5 0.0 copy-done.3
  130.5 1.9 %shard_map.118 = (f32[6,128,128]{2,1,0:T(8,128)}, f32[6,128,128]{2,1,0:T(8,128)}, f32[6,128,128]{2,1,0:T(8,128)}) custom-call(s32[3,2,6]{2,1,0:T(2,128)S(1)} %bitcast.7, s32[3]{0:T(128)S(1)} %bitcast.9, f32[768,512]{1,0:T(8,128)S(1)} %get-tuple-element.26.own, bf16[768,512]{1,0:T(8,128)(2,1)S(1)} %collective-permute-done.5.received), custom_call_target="tpu_custom_call" | custom-call | bytes 3539100 | tf_op jit(solution)/shard_map/pallas_call | solution.py:211
  132.4 0.0 all-to-all-done.3.parts
  132.4 0.7 shard_map.116
  (5 shorter events, 0.0 us)
Async XLA Ops:
  4.5 50.2 %copy-start = (bf16[768,512]{1,0:T(8,128)(2,1)S(1)}, bf16[768,512]{1,0:T(8,128)(2,1)}, u32[]{:S(2)}) copy-start(bf16[768,512]{1,0:T(8,128)(2,1)} %shard_map.112.own) | copy-start | bytes 2359300
  4.5 30.7 %collective-permute-start = (bf16[768,512]{1,0:T(8,128)(2,1)}, bf16[768,512]{1,0:T(8,128)(2,1)S(1)}, u32[]{:S(2)}, u32[]{:S(2)}) collective-permute-start(bf16[768,512]{1,0:T(8,128)(2,1)} %shard_map.112.own), channel_id=1, source_target_pairs={{0,128},{128,0},{1,129},{129,1},{2,130},{130,2},{3,131},{131,3},{4... | collective-permute-start | bytes 2359304 | tf_op jit(solution)/shard_map/ppermute | solution.py:227
  8.6 44.7 %all-to-all-start = ((bf16[64,40,128]{2,1,0:T(8,128)(2,1)}), bf16[64,40,128]{2,1,0:T(8,128)(2,1)}, u32[]{:S(2)}, u32[]{:S(2)}) async-start(bf16[64,40,128]{2,1,0:T(8,128)(2,1)} %shard_map.110), calls=%async_computation | async-start | bytes 1310720 | tf_op jit(solution)/shard_map/all_to_all | solution.py:223
  32.1 22.6 %collective-permute-start.1 = (bf16[768,512]{1,0:T(8,128)(2,1)}, bf16[768,512]{1,0:T(8,128)(2,1)S(1)}, u32[]{:S(2)}, u32[]{:S(2)}) collective-permute-start(bf16[768,512]{1,0:T(8,128)(2,1)} %shard_map.112.own), channel_id=1, source_target_pairs={{0,1},{1,0},{2,3},{3,2},{4,5},{5,4},{6,7},{7,6},{8,9},{9,8},{10,11... | collective-permute-start | bytes 2359304 | tf_op jit(solution)/shard_map/ppermute | solution.py:227
  35.2 19.5 %collective-permute-start.2 = (bf16[768,512]{1,0:T(8,128)(2,1)S(1)}, bf16[768,512]{1,0:T(8,128)(2,1)S(1)}, u32[]{:S(2)}, u32[]{:S(2)}) collective-permute-start(bf16[768,512]{1,0:T(8,128)(2,1)S(1)} %collective-permute-done.far), channel_id=1, source_target_pairs={{0,1},{1,0},{2,3},{3,2},{4,5},{5,4},{6,7},{7,6},{8,9},{9,8},{10,11... | collective-permute-start | bytes 2359304 | tf_op jit(solution)/shard_map/ppermute | solution.py:227
  54.7 0.9 copy-start.2
  89.2 32.1 %collective-permute-start.3 = (bf16[320,768]{1,0:T(8,128)(2,1)}, bf16[320,768]{1,0:T(8,128)(2,1)}, u32[]{:S(2)}, u32[]{:S(2)}) collective-permute-start(bf16[320,768]{1,0:T(8,128)(2,1)} %bitcast.4.acts), channel_id=1, source_target_pairs={{0,128},{128,0},{1,129},{129,1},{2,130},{130,2},{3,131},{131,3},{4... | collective-permute-start | bytes 1474568 | tf_op jit(solution)/shard_map/ppermute | solution.py:227
  99.6 0.8 copy-start.1
  100.4 30.1 %copy-start.3 = (s32[3,6,2]{1,2,0:T(2,128)S(1)}, s32[3,6,2]{1,2,0:T(2,128)}, u32[]{:S(2)}) copy-start(s32[3,6,2]{1,2,0:T(2,128)} %param.12) | copy-start | bytes 436
  100.4 30.1 %copy-start.4 = (s32[3,1,1]{0,2,1:T(1,128)S(1)}, s32[3,1,1]{0,2,1:T(1,128)}, u32[]{:S(2)}) copy-start(s32[3,1,1]{0,2,1:T(1,128)} %param.13) | copy-start | bytes 40
  100.4 32.0 %all-to-all-start.3 = ((bf16[64,40,128]{2,1,0:T(8,128)(2,1)}), bf16[64,40,128]{2,1,0:T(8,128)(2,1)S(1)}, u32[]{:S(2)}, u32[]{:S(2)}) async-start(bf16[64,40,128]{2,1,0:T(8,128)(2,1)} %copy-done.1), calls=%async_computation.3 | async-start | bytes 1310720 | tf_op jit(solution)/shard_map/all_to_all | solution.py:223
  107.8 13.5 %collective-permute-start.4 = (bf16[2,160,512]{2,1,0:T(8,128)(2,1)}, bf16[2,160,512]{2,1,0:T(8,128)(2,1)S(1)}, u32[]{:S(2)}, u32[]{:S(2)}) collective-permute-start(bf16[2,160,512]{2,1,0:T(8,128)(2,1)} %copy-done.2), channel_id=1, source_target_pairs={{0,128},{128,0},{1,129},{129,1},{2,130},{130,2},{3,131},{131,3},{4... | collective-permute-start | bytes 983048 | tf_op jit(solution)/shard_map/ppermute | solution.py:227
  123.5 7.0 %collective-permute-start.5 = (bf16[768,512]{1,0:T(8,128)(2,1)S(1)}, bf16[768,512]{1,0:T(8,128)(2,1)S(1)}, u32[]{:S(2)}, u32[]{:S(2)}) collective-permute-start(bf16[768,512]{1,0:T(8,128)(2,1)S(1)} %get-tuple-element.27), channel_id=1, source_target_pairs={{0,1},{1,0},{2,3},{3,2},{4,5},{5,4},{6,7},{7,6},{8,9},{9,8},{10,11... | collective-permute-start | bytes 2359304 | tf_op jit(solution)/shard_map/ppermute | solution.py:227

commit v6 on v5

--- a/solution.py
+++ b/solution.py
@@ -1,3 +1,5 @@
+import functools
+
 import jax
 import jax.numpy as jnp
 from jax import lax
@@ -8,6 +10,8 @@
 
 LONG = 1 << 36
 UNPACK = 0
+ADD = 0
+YH = 4
 F32 = jnp.float32
 BF16 = jnp.bfloat16
 VMEM = pl.BlockSpec(memory_space=pltpu.VMEM)
@@ -33,14 +37,6 @@
             dense[pl.ds(row, side), pl.ds(col, side)] = tiles[slot]
 
 
-def weights_kernel(index, counts, gate, up, down, dense):
-    lanes = dense.shape[1]
-    dense[...] = jnp.zeros_like(dense)
-    place_tiles(dense, gate, index, counts, 0, 0, 0)
-    place_tiles(dense, up, index, counts, 1, 0, lanes // 2)
-    place_tiles(dense, down, index, counts, 2, lanes, 0)
-
-
 def take_tiles(outs, index, counts, read):
     for which, out in enumerate(outs):
         slots, side, _ = out.shape
@@ -74,13 +70,17 @@
     take_tiles((gate_out, up_out, down_out), index, counts, read)
 
 
-def spread_kernel(tokens, cotangent, out, stage):
+def start_kernel(index, counts, tokens, cotangent, gate, up, down, out, dense, stage):
     rows, lanes = tokens.shape
     side = out.shape[-1]
     chunks = lanes // side
     part = rows // 2
     peers = out.shape[0] // 2
     size = 2 * chunks * part
+    dense[...] = jnp.zeros_like(dense)
+    place_tiles(dense, gate, index, counts, 0, 0, 0)
+    place_tiles(dense, up, index, counts, 1, 0, lanes // 2)
+    place_tiles(dense, down, index, counts, 2, lanes, 0)
     for start, block in ((0, tokens), (chunks, cotangent)):
         for q in range(chunks):
             piece = block[:, q * side : (q + 1) * side].astype(F32)
@@ -93,16 +93,25 @@
             out[group * peers + peer] = packed
 
 
-def unpack_kernel(me, blocks, own, far, stage):
+def copies_kernel(block, out):
+    for peer in range(out.shape[0]):
+        out[peer] = block[...]
+
+
+def block_at(group, peer, step):
+    return (peer // step) * 2 * step + group * step + peer % step
+
+
+def unpack_kernel(step, me, blocks, own, far, stage):
     _, quarter, lanes = own.shape
     side = blocks.shape[-1]
     peers = blocks.shape[0] // 2
     rows = quarter // peers
     chunks = lanes // side
     for group, out in ((0, own), (1, far)):
-        base = (me[0] if group == 0 else 1 - me[0]) * peers
+        side_of = me[0] if group == 0 else 1 - me[0]
         for peer in range(peers):
-            block = blocks[base + peer].astype(F32)
+            block = blocks[block_at(side_of, peer, step)].astype(F32)
             for q in range(2 * chunks):
                 stage[group, peer * rows : (peer + 1) * rows, q * side : (q + 1) * side] = block[
                     q * rows : (q + 1) * rows
@@ -149,7 +158,7 @@
         out[peer, :, 2 * units :] = up_act
 
 
-def apply_kernel(me, acts, own, far, own_core, far_core, out, result, stage):
+def apply_kernel(step, me, acts, own, far, own_core, far_core, out, result, stage):
     quarter = result.shape[0]
     lanes = own.shape[1]
     units = own.shape[0] - lanes
@@ -164,13 +173,17 @@
         result[:, lanes:] = dot(acts[near, units:], first[0:lanes, :], NT) + dot(
             acts[other, units:], second[0:lanes, :], NT
         )
-        base = (me[0] if group == 0 else 1 - me[0]) * peers
+        side_of = me[0] if group == 0 else 1 - me[0]
         for peer in range(peers):
             for q in range(2 * lanes // side):
                 stage[peer, q * rows : (q + 1) * rows, :] = result[
                     peer * rows : (peer + 1) * rows, q * side : (q + 1) * side
                 ]
-            out[base + peer] = stage[peer].astype(out.dtype)
+            out[block_at(side_of, peer, step)] = stage[peer].astype(out.dtype)
+
+
+def add_kernel(parts, out):
+    out[...] = sum_parts(parts, 0, parts.shape[0])
 
 
 def grads_kernel(acts, far_acts, own_rows, far_rows, own, sibling):
@@ -231,7 +244,8 @@
     rows, lanes = tokens.shape
     slots, side, _ = gate_tiles.shape
     row_peers = lax.axis_size("xh") * lax.axis_size("yl")
-    peers = lax.axis_size("yz")
+    step, depth = lax.axis_size("yh"), lax.axis_size("z")
+    peers = step * depth
     units = 2 * side
     quarter = peers * rows // 2
     share = 2 * quarter // row_peers
@@ -242,30 +256,24 @@
     me = lax.axis_index("xl").astype(jnp.int32).reshape(1)
     shape = jax.ShapeDtypeStruct
 
-    spread = call(
-        spread_kernel,
-        (shape((2 * peers, packed, side), BF16),),
-        (tokens, cotangent),
+    dense = (lanes + units, lanes)
+    spread, own = call(
+        start_kernel,
+        (shape((2 * step, packed, side), BF16), shape(dense, BF16)),
+        (index, counts, tokens, cotangent, gate_tiles, up_tiles, down_tiles),
+        smem=2,
         scratch=(pltpu.VMEM((2 * packed, side), F32),),
         limit=None,
     )
-    spread, gate_tiles, up_tiles, down_tiles = lax.optimization_barrier(
-        (spread, gate_tiles, up_tiles, down_tiles)
-    )
-    blocks = exchange(spread, ("xl", "yz"))
-    own = call(
-        weights_kernel,
-        (shape((lanes + units, lanes), BF16),),
-        (index, counts, gate_tiles, up_tiles, down_tiles),
-        smem=2,
-        limit=None,
-    )
+    blocks = exchange(spread, ("xl", "yh")).reshape(2 * step * packed, side)
+    blocks = call(copies_kernel, (shape((depth, *blocks.shape), BF16),), (blocks,))
+    blocks = exchange(blocks, "z").reshape(2 * peers, packed, side)
     far = swap(own, "xl")
     own_core = swap(own, "core")
     far_core = swap(far, "core")
     weights = (own, far, own_core, far_core)
     own_rows, far_rows = call(
-        unpack_kernel,
+        functools.partial(unpack_kernel, step),
         (shape((2, quarter, lanes), BF16),) * 2,
         (me, blocks),
         smem=1,
@@ -282,39 +290,41 @@
     acts = call(units_kernel, (shape(parts.shape, BF16),), (parts,))
     acts = exchange(acts, ("xh", "yl")).reshape(2 * quarter, 3 * units)
     sums = call(
-        apply_kernel,
+        functools.partial(apply_kernel, step),
         (shape((2 * peers, packed, side), BF16),),
         (me, acts, *weights),
         smem=1,
         scratch=(pltpu.VMEM((quarter, 2 * lanes), F32), pltpu.VMEM((peers, packed, side), F32)),
         flops=flops,
     )
-    sums = exchange(sums, ("xl", "yz"))
+    sums = exchange(sums.reshape(depth, 2 * step * packed, side), "z")
+    sums = call(add_kernel, (shape(sums.shape[1:], F32),), (sums,), flops=ADD)
+    sums = exchange(sums.reshape(2 * step, packed, side), ("xl", "yh"))
     far_acts, far_rows = swap(acts, "xl"), swap(far_rows, "xl")
-    dense = (lanes + units, lanes)
     own_grad, sibling_grad = call(
         grads_kernel,
         (shape(dense, F32), shape(dense, BF16)),
         (acts, far_acts, own_rows, far_rows),
         flops=flops,
     )
+    output, input_grad = call(finish_kernel, (shape((rows, lanes), BF16),) * 2, (sums,), flops=LONG)
+    index, output, input_grad = lax.optimization_barrier((index, output, input_grad))
     gate_grad, up_grad, down_grad = call(
         tiles_kernel,
         (shape((slots, side, side), F32),) * 3,
         (index, counts, own_grad, swap(sibling_grad, "core")),
         smem=2,
     )
-    output, input_grad = call(finish_kernel, (shape((rows, lanes), BF16),) * 2, (sums,), flops=LONG)
     return (output, input_grad, gate_grad, up_grad, down_grad)
 
 
 def solution(mesh):
     row_size, col_size = mesh.shape["row"], mesh.shape["col"]
     split = Mesh(
-        mesh.devices.reshape(row_size // 4, 2, 2, col_size // 2, 2),
-        ("xh", "xl", "yl", "yz", "core"),
-    )
-    row, col = ("xh", "xl", "yl"), ("yz", "core")
+        mesh.devices.reshape(row_size // 4, 2, 2, YH, col_size // (2 * YH), 2),
+        ("xh", "xl", "yl", "yh", "z", "core"),
+    )
+    row, col = ("xh", "xl", "yl"), ("yh", "z", "core")
     blocks = P(col, row)
     tiles = P(row, col, None)
     small = P(None, row, col)

time: 134 us -> 150 us (1.12)
  blocking collectives: 33.6 us -> 61.3 us
  starting transfers between devices: 56.2 us -> 44.5 us
  local copies, waits for them, and re-layouts: 0.85 us -> 4.38 us
  waiting for transfers between devices: 28.5 us -> 26.3 us
  Pallas kernels: 13.3 us -> 11.5 us
    all_to_all x2 -> x3, blocking collectives: 33.6 us -> 61.3 us  [exchange(): return lax.all_to_all(blocks, axis, split_axis=0, concat_axis=0, tiled=True)]
    ppermute x6, waiting for transfers between devices: 12.4 us -> 1.47 us  [swap(): return lax.ppermute(block, axis, [(0, 1), (1, 0)])]
    all_to_all x2 -> x3, waiting for transfers between devices: 16.1 us -> 24.8 us  [exchange(): return lax.all_to_all(blocks, axis, split_axis=0, concat_axis=0, tiled=True)]
    all_to_all x2 -> x3, starting transfers between devices: 30.9 us -> 23.5 us  [exchange(): return lax.all_to_all(blocks, axis, split_axis=0, concat_axis=0, tiled=True)]
    ppermute x6, starting transfers between devices: 25.3 us -> 21.1 us  [swap(): return lax.ppermute(block, axis, [(0, 1), (1, 0)])]
    unnamed x10 -> x22, local copies, waits for them, and re-layouts: 0.85 us -> 4.38 us
    pallas_call x9 -> x10, Pallas kernels: 13.3 us -> 11.5 us  [call(): pl.pallas_call(kernel, out_shape=outs[0] if single else outs, in_specs=(S...]
  transfers between devices with their start and end apart: 8 -> 9, of which waited for: 3 -> 3; matrix products, arithmetic and copies ran while one was open for 0% -> 0% of each run, Pallas kernels for 6% -> 3%
where the time goes in v6:
time: 150 us; the launch traced here: 149 us
  blocking collectives  61.3 us (41%)
  starting transfers between devices  44.5 us (30%)
  waiting for transfers between devices  26.3 us (18%)
  Pallas kernels  11.5 us (8%)
  local copies, waits for them, and re-layouts  4.38 us (3%)
    all_to_all x3, blocking collectives, exchange(): return lax.all_to_all(blocks, axis, split_axis=0, concat_axis=0, tiled=True)  61.3 us
    all_to_all x3, waiting for transfers between devices, exchange(): return lax.all_to_all(blocks, axis, split_axis=0, concat_axis=0, tiled=True)  24.8 us
    all_to_all x3, starting transfers between devices, exchange(): return lax.all_to_all(blocks, axis, split_axis=0, concat_axis=0, tiled=True)  23.5 us
    ppermute x6, starting transfers between devices, swap(): return lax.ppermute(block, axis, [(0, 1), (1, 0)])  21.1 us
    pallas_call x10, Pallas kernels, call(): pl.pallas_call(kernel, out_shape=outs[0] if single else outs, in_specs=(S...  11.5 us
    unnamed x22, local copies, waits for them, and re-layouts  4.38 us
  transfers between devices with their start and end apart: 9, of which 3 were waited for; matrix products, arithmetic and copies ran while one was open for 0% of the time, Pallas kernels for 3%

profile of v6, /device:TPU:1, one launch (start us, length us, event | category | flops | bytes accessed | tf_op | source)
XLA Modules:
  0.0 148.9 jit_solution(6804190007704815994)
XLA Ops:
  0.6 2.3 %shard_map.110 = (bf16[8,40,128]{2,1,0:T(8,128)(2,1)}, bf16[768,512]{1,0:T(8,128)(2,1)}) custom-call(s32[3,2,6]{2,1,0:T(2,128)} %bitcast.15, s32[3]{0:T(128)} %bitcast.17, bf16[10,512]{1,0:T(8,128)(2,1)} %tokens.1, bf16[10,512]{1,0:T(8,128)(2,1)} %cotangent.1, bf16[6,128,128]{2,1,0:T(8,128)(2,1)} %gate.1, bf16[6,128,128]{2,1,0:T(8,128)(2,1)} %up.1, ...), custom_call_target="tpu_custom_call" | custom-call | bytes 1478812 | tf_op jit(solution)/shard_map/pallas_call | solution.py:224
  2.9 4.1 %collective-permute-start = (bf16[768,512]{1,0:T(8,128)(2,1)}, bf16[768,512]{1,0:T(8,128)(2,1)S(1)}, u32[]{:S(2)}, u32[]{:S(2)}) collective-permute-start(bf16[768,512]{1,0:T(8,128)(2,1)} %get-tuple-element.22.own), channel_id=1, source_target_pairs={{0,128},{128,0},{1,129},{129,1},{2,130},{130,2},{3,131},{131,3},{4... | collective-permute-start | bytes 2359304 | tf_op jit(solution)/shard_map/ppermute | solution.py:240
  7.0 23.2 %all_to_all.30 = bf16[8,40,128]{2,1,0:T(8,128)(2,1)S(1)} all-to-all(bf16[8,40,128]{2,1,0:T(8,128)(2,1)} %get-tuple-element.19), channel_id=1, replica_groups=mesh['xh'=4,'xl'=2,'yl'=2,'yh'=4,'z'=8,'core'=2] {'xl','yh'}, dimensions={0} | all-to-all | bytes 163840 | tf_op jit(solution)/shard_map/all_to_all | solution.py:236
  30.3 0.9 shard_map.111
  31.2 16.4 %all-to-all-start.1 = ((bf16[8,320,128]{2,1,0:T(8,128)(2,1)}), bf16[8,320,128]{2,1,0:T(8,128)(2,1)}, u32[]{:S(2)}, u32[]{:S(2)}) async-start(bf16[8,320,128]{2,1,0:T(8,128)(2,1)} %shard_map.111), calls=%async_computation.1 | async-start | bytes 1310720 | tf_op jit(solution)/shard_map/all_to_all | solution.py:236
  47.6 4.2 %collective-permute-start.1 = (bf16[768,512]{1,0:T(8,128)(2,1)S(1)}, bf16[768,512]{1,0:T(8,128)(2,1)S(1)}, u32[]{:S(2)}, u32[]{:S(2)}) collective-permute-start(bf16[768,512]{1,0:T(8,128)(2,1)S(1)} %copy-done), channel_id=1, source_target_pairs={{0,1},{1,0},{2,3},{3,2},{4,5},{5,4},{6,7},{7,6},{8,9},{9,8},{10,11... | collective-permute-start | bytes 2359304 | tf_op jit(solution)/shard_map/ppermute | solution.py:240
  51.8 1.9 %collective-permute-start.2 = (bf16[768,512]{1,0:T(8,128)(2,1)S(1)}, bf16[768,512]{1,0:T(8,128)(2,1)S(1)}, u32[]{:S(2)}, u32[]{:S(2)}) collective-permute-start(bf16[768,512]{1,0:T(8,128)(2,1)S(1)} %collective-permute-done.far), channel_id=1, source_target_pairs={{0,1},{1,0},{2,3},{3,2},{4,5},{5,4},{6,7},{7,6},{8,9},{9,8},{10,11... | collective-permute-start | bytes 2359304 | tf_op jit(solution)/shard_map/ppermute | solution.py:240
  53.8 12.2 %all-to-all-done.1 = bf16[8,320,128]{2,1,0:T(8,128)(2,1)} async-done(((bf16[8,320,128]{2,1,0:T(8,128)(2,1)}), bf16[8,320,128]{2,1,0:T(8,128)(2,1)}, u32[]{:S(2)}, u32[]{:S(2)}) %all-to-all-start.1) | async-done | bytes 655392 | tf_op jit(solution)/shard_map/all_to_all | solution.py:236
  66.0 1.3 shard_map.112
  67.4 0.0 copy-start.4
  67.4 0.8 shard_map.113
  68.2 20.0 %all_to_all.31.parts = bf16[8,40,768]{2,1,0:T(8,128)(2,1)S(1)} all-to-all(bf16[8,40,768]{2,1,0:T(8,128)(2,1)S(1)} %bitcast.13), channel_id=1, replica_groups=mesh['xh'=4,'xl'=2,'yl'=2,'yh'=4,'z'=8,'core'=2] {'xh','yl'}, dimensions={0} | all-to-all | bytes 983040 | tf_op jit(solution)/shard_map/all_to_all | solution.py:236
  88.3 0.1 shard_map.114
  88.4 18.1 %all_to_all.32 = bf16[8,40,768]{2,1,0:T(8,128)(2,1)S(1)} all-to-all(bf16[8,40,768]{2,1,0:T(8,128)(2,1)S(1)} %shard_map.114), channel_id=1, replica_groups=mesh['xh'=4,'xl'=2,'yl'=2,'yh'=4,'z'=8,'core'=2] {'xh','yl'}, dimensions={0} | all-to-all | bytes 983040 | tf_op jit(solution)/shard_map/all_to_all | solution.py:236
  106.4 1.2 shard_map.115
  107.7 0.8 copy-done.1
  108.5 3.7 %all-to-all-start.4 = ((bf16[8,320,128]{2,1,0:T(8,128)(2,1)}), bf16[8,320,128]{2,1,0:T(8,128)(2,1)S(1)}, u32[]{:S(2)}, u32[]{:S(2)}) async-start(bf16[8,320,128]{2,1,0:T(8,128)(2,1)} %bitcast.9), calls=%async_computation.4 | async-start | bytes 1310720 | tf_op jit(solution)/shard_map/all_to_all | solution.py:236
  112.2 1.9 %collective-permute-start.3 = (bf16[320,768]{1,0:T(8,128)(2,1)}, bf16[320,768]{1,0:T(8,128)(2,1)S(1)}, u32[]{:S(2)}, u32[]{:S(2)}) collective-permute-start(bf16[320,768]{1,0:T(8,128)(2,1)} %bitcast.11), channel_id=1, source_target_pairs={{0,128},{128,0},{1,129},{129,1},{2,130},{130,2},{3,131},{131,3},{4... | collective-permute-start | bytes 1474568 | tf_op jit(solution)/shard_map/ppermute | solution.py:240
  114.1 3.4 %collective-permute-start.4 = (bf16[2,160,512]{2,1,0:T(8,128)(2,1)}, bf16[2,160,512]{2,1,0:T(8,128)(2,1)S(1)}, u32[]{:S(2)}, u32[]{:S(2)}) collective-permute-start(bf16[2,160,512]{2,1,0:T(8,128)(2,1)} %copy-done.4), channel_id=1, source_target_pairs={{0,128},{128,0},{1,129},{129,1},{2,130},{130,2},{3,131},{131,3},{4... | collective-permute-start | bytes 983048 | tf_op jit(solution)/shard_map/ppermute | solution.py:240
  117.5 12.6 %all-to-all-done.4.parts = bf16[8,320,128]{2,1,0:T(8,128)(2,1)S(1)} async-done(((bf16[8,320,128]{2,1,0:T(8,128)(2,1)}), bf16[8,320,128]{2,1,0:T(8,128)(2,1)S(1)}, u32[]{:S(2)}, u32[]{:S(2)}) %all-to-all-start.4) | async-done | bytes 655392 | tf_op jit(solution)/shard_map/all_to_all | solution.py:236
  130.1 0.8 shard_map.116
  130.8 3.4 %all-to-all-start.5 = ((f32[8,40,128]{2,1,0:T(8,128)}), f32[8,40,128]{2,1,0:T(8,128)S(1)}, u32[]{:S(2)}, u32[]{:S(2)}) async-start(f32[8,40,128]{2,1,0:T(8,128)} %bitcast.8), calls=%async_computation.5 | async-start | bytes 327680 | tf_op jit(solution)/shard_map/all_to_all | solution.py:236
  134.2 0.0 copy-start.9
  134.2 0.7 copy-done.9
  134.9 0.8 copy-done.7
  135.7 1.0 copy-done.8
  136.8 1.0 copy-done.10
  137.7 1.5 %shard_map.118 = (f32[768,512]{1,0:T(8,128)S(1)}, bf16[768,512]{1,0:T(8,128)(2,1)}) custom-call(bf16[320,768]{1,0:T(8,128)(2,1)S(1)} %bitcast.12, bf16[320,768]{1,0:T(8,128)(2,1)S(1)} %copy-done.8, bf16[2,160,512]{2,1,0:T(8,128)(2,1)S(1)} %get-tuple-element.20.own_rows, bf16[2,160,512]{2,1,0:T(8,128)(2,1)S(1)} %copy-done.10), custom_call_target="tpu_custom_call" | custom-call | flops 503316480 | bytes 3997696 | tf_op jit(solution)/shard_map/pallas_call | solution.py:224
  139.2 5.6 %collective-permute-start.5 = (bf16[768,512]{1,0:T(8,128)(2,1)}, bf16[768,512]{1,0:T(8,128)(2,1)S(1)}, u32[]{:S(2)}, u32[]{:S(2)}) collective-permute-start(bf16[768,512]{1,0:T(8,128)(2,1)} %get-tuple-element.29), channel_id=1, source_target_pairs={{0,1},{1,0},{2,3},{3,2},{4,5},{5,4},{6,7},{7,6},{8,9},{9,8},{10,11... | collective-permute-start | bytes 2359304 | tf_op jit(solution)/shard_map/ppermute | solution.py:240
  144.8 0.6 shard_map.117
  145.5 1.5 collective-permute-done.5.received
  146.9 1.9 %shard_map.119 = (f32[6,128,128]{2,1,0:T(8,128)}, f32[6,128,128]{2,1,0:T(8,128)}, f32[6,128,128]{2,1,0:T(8,128)}) custom-call(s32[3,2,6]{2,1,0:T(2,128)S(1)} %bitcast.16, s32[3]{0:T(128)S(1)} %bitcast.18, f32[768,512]{1,0:T(8,128)S(1)} %get-tuple-element.28.own, bf16[768,512]{1,0:T(8,128)(2,1)S(1)} %collective-permute-done.5.received), custom_call_target="tpu_custom_call" | custom-call | bytes 3539100 | tf_op jit(solution)/shard_map/pallas_call | solution.py:224
  (21 shorter events, 0.0 us)
Async XLA Ops:
  2.9 44.7 %copy-start = (bf16[768,512]{1,0:T(8,128)(2,1)S(1)}, bf16[768,512]{1,0:T(8,128)(2,1)}, u32[]{:S(2)}) copy-start(bf16[768,512]{1,0:T(8,128)(2,1)} %get-tuple-element.22.own) | copy-start | bytes 2359300
  2.9 48.9 %collective-permute-start = (bf16[768,512]{1,0:T(8,128)(2,1)}, bf16[768,512]{1,0:T(8,128)(2,1)S(1)}, u32[]{:S(2)}, u32[]{:S(2)}) collective-permute-start(bf16[768,512]{1,0:T(8,128)(2,1)} %get-tuple-element.22.own), channel_id=1, source_target_pairs={{0,128},{128,0},{1,129},{129,1},{2,130},{130,2},{3,131},{131,3},{4... | collective-permute-start | bytes 2359304 | tf_op jit(solution)/shard_map/ppermute | solution.py:240
  31.2 34.8 %all-to-all-start.1 = ((bf16[8,320,128]{2,1,0:T(8,128)(2,1)}), bf16[8,320,128]{2,1,0:T(8,128)(2,1)}, u32[]{:S(2)}, u32[]{:S(2)}) async-start(bf16[8,320,128]{2,1,0:T(8,128)(2,1)} %shard_map.111), calls=%async_computation.1 | async-start | bytes 1310720 | tf_op jit(solution)/shard_map/all_to_all | solution.py:236
  47.6 19.8 %collective-permute-start.1 = (bf16[768,512]{1,0:T(8,128)(2,1)S(1)}, bf16[768,512]{1,0:T(8,128)(2,1)S(1)}, u32[]{:S(2)}, u32[]{:S(2)}) collective-permute-start(bf16[768,512]{1,0:T(8,128)(2,1)S(1)} %copy-done), channel_id=1, source_target_pairs={{0,1},{1,0},{2,3},{3,2},{4,5},{5,4},{6,7},{7,6},{8,9},{9,8},{10,11... | collective-permute-start | bytes 2359304 | tf_op jit(solution)/shard_map/ppermute | solution.py:240
  51.8 15.6 %collective-permute-start.2 = (bf16[768,512]{1,0:T(8,128)(2,1)S(1)}, bf16[768,512]{1,0:T(8,128)(2,1)S(1)}, u32[]{:S(2)}, u32[]{:S(2)}) collective-permute-start(bf16[768,512]{1,0:T(8,128)(2,1)S(1)} %collective-permute-done.far), channel_id=1, source_target_pairs={{0,1},{1,0},{2,3},{3,2},{4,5},{5,4},{6,7},{7,6},{8,9},{9,8},{10,11... | collective-permute-start | bytes 2359304 | tf_op jit(solution)/shard_map/ppermute | solution.py:240
  67.4 0.9 copy-start.4
  106.4 1.2 copy-start.2
  107.7 0.8 copy-start.1
  108.5 27.2 %copy-start.3 = (bf16[8,40,768]{2,1,0:T(8,128)(2,1)S(1)}, bf16[8,40,768]{2,1,0:T(8,128)(2,1)}, u32[]{:S(2)}) copy-start(bf16[8,40,768]{2,1,0:T(8,128)(2,1)} %copy-done.2) | copy-start | bytes 1474564
  108.5 21.6 %all-to-all-start.4 = ((bf16[8,320,128]{2,1,0:T(8,128)(2,1)}), bf16[8,320,128]{2,1,0:T(8,128)(2,1)S(1)}, u32[]{:S(2)}, u32[]{:S(2)}) async-start(bf16[8,320,128]{2,1,0:T(8,128)(2,1)} %bitcast.9), calls=%async_computation.4 | async-start | bytes 1310720 | tf_op jit(solution)/shard_map/all_to_all | solution.py:236
  112.2 22.8 %collective-permute-start.3 = (bf16[320,768]{1,0:T(8,128)(2,1)}, bf16[320,768]{1,0:T(8,128)(2,1)S(1)}, u32[]{:S(2)}, u32[]{:S(2)}) collective-permute-start(bf16[320,768]{1,0:T(8,128)(2,1)} %bitcast.11), channel_id=1, source_target_pairs={{0,128},{128,0},{1,129},{129,1},{2,130},{130,2},{3,131},{131,3},{4... | collective-permute-start | bytes 1474568 | tf_op jit(solution)/shard_map/ppermute | solution.py:240
  114.1 20.1 %collective-permute-start.4 = (bf16[2,160,512]{2,1,0:T(8,128)(2,1)}, bf16[2,160,512]{2,1,0:T(8,128)(2,1)S(1)}, u32[]{:S(2)}, u32[]{:S(2)}) collective-permute-start(bf16[2,160,512]{2,1,0:T(8,128)(2,1)} %copy-done.4), channel_id=1, source_target_pairs={{0,128},{128,0},{1,129},{129,1},{2,130},{130,2},{3,131},{131,3},{4... | collective-permute-start | bytes 983048 | tf_op jit(solution)/shard_map/ppermute | solution.py:240
  130.8 14.0 %all-to-all-start.5 = ((f32[8,40,128]{2,1,0:T(8,128)}), f32[8,40,128]{2,1,0:T(8,128)S(1)}, u32[]{:S(2)}, u32[]{:S(2)}) async-start(f32[8,40,128]{2,1,0:T(8,128)} %bitcast.8), calls=%async_computation.5 | async-start | bytes 327680 | tf_op jit(solution)/shard_map/all_to_all | solution.py:236
  134.2 0.7 copy-start.9
  134.9 0.8 copy-start.7
  135.7 1.0 copy-start.8
  136.8 1.0 copy-start.10
  139.2 7.7 %copy-start.5 = (s32[3,6,2]{1,2,0:T(2,128)S(1)}, s32[3,6,2]{1,2,0:T(2,128)}, u32[]{:S(2)}) copy-start(s32[3,6,2]{1,2,0:T(2,128)} %param.12) | copy-start | bytes 436
  139.2 7.7 %copy-start.6 = (s32[3,1,1]{0,2,1:T(1,128)S(1)}, s32[3,1,1]{0,2,1:T(1,128)}, u32[]{:S(2)}) copy-start(s32[3,1,1]{0,2,1:T(1,128)} %param.13) | copy-start | bytes 40
  139.2 7.7 %collective-permute-start.5 = (bf16[768,512]{1,0:T(8,128)(2,1)}, bf16[768,512]{1,0:T(8,128)(2,1)S(1)}, u32[]{:S(2)}, u32[]{:S(2)}) collective-permute-start(bf16[768,512]{1,0:T(8,128)(2,1)} %get-tuple-element.29), channel_id=1, source_target_pairs={{0,1},{1,0},{2,3},{3,2},{4,5},{5,4},{6,7},{7,6},{8,9},{9,8},{10,11... | collective-permute-start | bytes 2359304 | tf_op jit(solution)/shard_map/ppermute | solution.py:240

commit v7 on v5

--- a/solution.py
+++ b/solution.py
@@ -33,14 +33,6 @@
             dense[pl.ds(row, side), pl.ds(col, side)] = tiles[slot]
 
 
-def weights_kernel(index, counts, gate, up, down, dense):
-    lanes = dense.shape[1]
-    dense[...] = jnp.zeros_like(dense)
-    place_tiles(dense, gate, index, counts, 0, 0, 0)
-    place_tiles(dense, up, index, counts, 1, 0, lanes // 2)
-    place_tiles(dense, down, index, counts, 2, lanes, 0)
-
-
 def take_tiles(outs, index, counts, read):
     for which, out in enumerate(outs):
         slots, side, _ = out.shape
@@ -74,13 +66,17 @@
     take_tiles((gate_out, up_out, down_out), index, counts, read)
 
 
-def spread_kernel(tokens, cotangent, out, stage):
+def start_kernel(index, counts, tokens, cotangent, gate, up, down, out, dense, stage):
     rows, lanes = tokens.shape
     side = out.shape[-1]
     chunks = lanes // side
     part = rows // 2
     peers = out.shape[0] // 2
     size = 2 * chunks * part
+    dense[...] = jnp.zeros_like(dense)
+    place_tiles(dense, gate, index, counts, 0, 0, 0)
+    place_tiles(dense, up, index, counts, 1, 0, lanes // 2)
+    place_tiles(dense, down, index, counts, 2, lanes, 0)
     for start, block in ((0, tokens), (chunks, cotangent)):
         for q in range(chunks):
             piece = block[:, q * side : (q + 1) * side].astype(F32)
@@ -242,24 +238,16 @@
     me = lax.axis_index("xl").astype(jnp.int32).reshape(1)
     shape = jax.ShapeDtypeStruct
 
-    spread = call(
-        spread_kernel,
-        (shape((2 * peers, packed, side), BF16),),
-        (tokens, cotangent),
+    dense = (lanes + units, lanes)
+    spread, own = call(
+        start_kernel,
+        (shape((2 * peers, packed, side), BF16), shape(dense, BF16)),
+        (index, counts, tokens, cotangent, gate_tiles, up_tiles, down_tiles),
+        smem=2,
         scratch=(pltpu.VMEM((2 * packed, side), F32),),
         limit=None,
     )
-    spread, gate_tiles, up_tiles, down_tiles = lax.optimization_barrier(
-        (spread, gate_tiles, up_tiles, down_tiles)
-    )
     blocks = exchange(spread, ("xl", "yz"))
-    own = call(
-        weights_kernel,
-        (shape((lanes + units, lanes), BF16),),
-        (index, counts, gate_tiles, up_tiles, down_tiles),
-        smem=2,
-        limit=None,
-    )
     far = swap(own, "xl")
     own_core = swap(own, "core")
     far_core = swap(far, "core")
@@ -291,7 +279,6 @@
     )
     sums = exchange(sums, ("xl", "yz"))
     far_acts, far_rows = swap(acts, "xl"), swap(far_rows, "xl")
-    dense = (lanes + units, lanes)
     own_grad, sibling_grad = call(
         grads_kernel,
         (shape(dense, F32), shape(dense, BF16)),

time: 134 us -> 132 us (0.985)
  waiting for transfers between devices: 28.5 us -> 24.3 us
  blocking collectives: 33.6 us -> 37.8 us
  Pallas kernels: 13.3 us -> 11.8 us
    all_to_all x2, waiting for transfers between devices: 16.1 us -> 11.9 us  [exchange(): return lax.all_to_all(blocks, axis, split_axis=0, concat_axis=0, tiled=True)]
    all_to_all x2, blocking collectives: 33.6 us -> 37.8 us  [exchange(): return lax.all_to_all(blocks, axis, split_axis=0, concat_axis=0, tiled=True)]
    pallas_call x9 -> x8, Pallas kernels: 13.3 us -> 11.8 us  [call(): pl.pallas_call(kernel, out_shape=outs[0] if single else outs, in_specs=(S...]
where the time goes in v7:
time: 132 us
  starting transfers between devices  56.1 us (42%)
  blocking collectives  37.8 us (29%)
  waiting for transfers between devices  24.3 us (18%)
  Pallas kernels  11.8 us (9%)
    all_to_all x2, blocking collectives, exchange(): return lax.all_to_all(blocks, axis, split_axis=0, concat_axis=0, tiled=True)  37.8 us
    all_to_all x2, starting transfers between devices, exchange(): return lax.all_to_all(blocks, axis, split_axis=0, concat_axis=0, tiled=True)  30.9 us
    ppermute x6, starting transfers between devices, swap(): return lax.ppermute(block, axis, [(0, 1), (1, 0)])  25.2 us
    ppermute x6, waiting for transfers between devices, swap(): return lax.ppermute(block, axis, [(0, 1), (1, 0)])  12.4 us
    all_to_all x2, waiting for transfers between devices, exchange(): return lax.all_to_all(blocks, axis, split_axis=0, concat_axis=0, tiled=True)  11.9 us
    pallas_call x8, Pallas kernels, call(): pl.pallas_call(kernel, out_shape=outs[0] if single else outs, in_specs=(S...  11.8 us
  transfers between devices with their start and end apart: 8, of which 3 were waited for; matrix products, arithmetic and copies ran while one was open for 0% of the time, Pallas kernels for 6%

profile of v7, /device:TPU:1, one launch (start us, length us, event | category | flops | bytes accessed | tf_op | source)
XLA Modules:
  0.0 131.7 jit_solution(8213381899158694560)
XLA Ops:
  0.6 2.5 %shard_map.110 = (bf16[64,40,128]{2,1,0:T(8,128)(2,1)}, bf16[768,512]{1,0:T(8,128)(2,1)}) custom-call(s32[3,2,6]{2,1,0:T(2,128)} %bitcast.6, s32[3]{0:T(128)} %bitcast.8, bf16[10,512]{1,0:T(8,128)(2,1)} %tokens.1, bf16[10,512]{1,0:T(8,128)(2,1)} %cotangent.1, bf16[6,128,128]{2,1,0:T(8,128)(2,1)} %gate.1, bf16[6,128,128]{2,1,0:T(8,128)(2,1)} %up.1, ...), custom_call_target="tpu_custom_call" | custom-call | bytes 2052252 | tf_op jit(solution)/shard_map/pallas_call | solution.py:207
  3.1 4.1 %collective-permute-start = (bf16[768,512]{1,0:T(8,128)(2,1)}, bf16[768,512]{1,0:T(8,128)(2,1)S(1)}, u32[]{:S(2)}, u32[]{:S(2)}) collective-permute-start(bf16[768,512]{1,0:T(8,128)(2,1)} %get-tuple-element.19.own), channel_id=1, source_target_pairs={{0,128},{128,0},{1,129},{129,1},{2,130},{130,2},{3,131},{131,3},{4... | collective-permute-start | bytes 2359304 | tf_op jit(solution)/shard_map/ppermute | solution.py:223
  7.2 23.4 %all-to-all-start = ((bf16[64,40,128]{2,1,0:T(8,128)(2,1)}), bf16[64,40,128]{2,1,0:T(8,128)(2,1)}, u32[]{:S(2)}, u32[]{:S(2)}) async-start(bf16[64,40,128]{2,1,0:T(8,128)(2,1)} %get-tuple-element.16), calls=%async_computation | async-start | bytes 1310720 | tf_op jit(solution)/shard_map/all_to_all | solution.py:219
  30.7 3.1 %collective-permute-start.1 = (bf16[768,512]{1,0:T(8,128)(2,1)}, bf16[768,512]{1,0:T(8,128)(2,1)S(1)}, u32[]{:S(2)}, u32[]{:S(2)}) collective-permute-start(bf16[768,512]{1,0:T(8,128)(2,1)} %get-tuple-element.19.own), channel_id=1, source_target_pairs={{0,1},{1,0},{2,3},{3,2},{4,5},{5,4},{6,7},{7,6},{8,9},{9,8},{10,11... | collective-permute-start | bytes 2359304 | tf_op jit(solution)/shard_map/ppermute | solution.py:223
  33.8 0.0 collective-permute-done.far
  33.8 1.9 %collective-permute-start.2 = (bf16[768,512]{1,0:T(8,128)(2,1)S(1)}, bf16[768,512]{1,0:T(8,128)(2,1)S(1)}, u32[]{:S(2)}, u32[]{:S(2)}) collective-permute-start(bf16[768,512]{1,0:T(8,128)(2,1)S(1)} %collective-permute-done.far), channel_id=1, source_target_pairs={{0,1},{1,0},{2,3},{3,2},{4,5},{5,4},{6,7},{7,6},{8,9},{9,8},{10,11... | collective-permute-start | bytes 2359304 | tf_op jit(solution)/shard_map/ppermute | solution.py:223
  35.8 11.9 %all-to-all-done.blocks = bf16[64,40,128]{2,1,0:T(8,128)(2,1)} async-done(((bf16[64,40,128]{2,1,0:T(8,128)(2,1)}), bf16[64,40,128]{2,1,0:T(8,128)(2,1)}, u32[]{:S(2)}, u32[]{:S(2)}) %all-to-all-start) | async-done | bytes 655392 | tf_op jit(solution)/shard_map/all_to_all | solution.py:219
  47.7 1.3 %shard_map.111 = (bf16[2,160,512]{2,1,0:T(8,128)(2,1)S(1)}, bf16[2,160,512]{2,1,0:T(8,128)(2,1)S(1)}) custom-call(s32[1]{0:T(128)} %bitcast.me, bf16[64,40,128]{2,1,0:T(8,128)(2,1)} %all-to-all-done.blocks), custom_call_target="tpu_custom_call" | custom-call | bytes 1310724 | tf_op jit(solution)/shard_map/pallas_call | solution.py:207
  49.0 0.0 copy-start.2
  49.0 0.0 collective-permute-done.1.own_core
  49.0 0.0 collective-permute-done.2.far_core
  49.0 0.0 copy-done
  49.1 0.8 shard_map.112
  49.9 0.0 copy-done.2
  49.9 23.0 %all_to_all.20.parts = bf16[8,40,768]{2,1,0:T(8,128)(2,1)S(1)} all-to-all(bf16[8,40,768]{2,1,0:T(8,128)(2,1)S(1)} %bitcast.5), channel_id=1, replica_groups=mesh['xh'=4,'xl'=2,'yl'=2,'yz'=32,'core'=2] {'xh','yl'}, dimensions={0} | all-to-all | bytes 983040 | tf_op jit(solution)/shard_map/all_to_all | solution.py:219
  72.9 0.1 shard_map.113
  73.0 14.8 %all_to_all.21 = bf16[8,40,768]{2,1,0:T(8,128)(2,1)} all-to-all(bf16[8,40,768]{2,1,0:T(8,128)(2,1)S(1)} %shard_map.113), channel_id=1, replica_groups=mesh['xh'=4,'xl'=2,'yl'=2,'yz'=32,'core'=2] {'xh','yl'}, dimensions={0} | all-to-all | bytes 983040 | tf_op jit(solution)/shard_map/all_to_all | solution.py:219
  87.8 8.1 %collective-permute-start.3 = (bf16[320,768]{1,0:T(8,128)(2,1)}, bf16[320,768]{1,0:T(8,128)(2,1)}, u32[]{:S(2)}, u32[]{:S(2)}) collective-permute-start(bf16[320,768]{1,0:T(8,128)(2,1)} %bitcast.4.acts), channel_id=1, source_target_pairs={{0,128},{128,0},{1,129},{129,1},{2,130},{130,2},{3,131},{131,3},{4... | collective-permute-start | bytes 1474568 | tf_op jit(solution)/shard_map/ppermute | solution.py:223
  95.8 2.2 %shard_map.114 = bf16[64,40,128]{2,1,0:T(8,128)(2,1)S(1)} custom-call(s32[1]{0:T(128)} %bitcast.me, bf16[320,768]{1,0:T(8,128)(2,1)} %bitcast.4.acts, bf16[768,512]{1,0:T(8,128)(2,1)S(1)} %copy-done, bf16[768,512]{1,0:T(8,128)(2,1)S(1)} %collective-permute-done.far, bf16[768,512]{1,0:T(8,128)(2,1)S(1)} %collective-permute-done.1.own_core, ...), custom_call_target="tpu_custom_call" | custom-call | flops 503316480 | bytes 4292612 | tf_op jit(solution)/shard_map/pallas_call | solution.py:207
  98.1 0.0 copy-start.1
  98.1 0.8 copy-done.1
  98.9 7.5 %all-to-all-start.3 = ((bf16[64,40,128]{2,1,0:T(8,128)(2,1)}), bf16[64,40,128]{2,1,0:T(8,128)(2,1)S(1)}, u32[]{:S(2)}, u32[]{:S(2)}) async-start(bf16[64,40,128]{2,1,0:T(8,128)(2,1)} %copy-done.1), calls=%async_computation.3 | async-start | bytes 1310720 | tf_op jit(solution)/shard_map/all_to_all | solution.py:219
  106.4 3.0 %collective-permute-start.4 = (bf16[2,160,512]{2,1,0:T(8,128)(2,1)}, bf16[2,160,512]{2,1,0:T(8,128)(2,1)S(1)}, u32[]{:S(2)}, u32[]{:S(2)}) collective-permute-start(bf16[2,160,512]{2,1,0:T(8,128)(2,1)} %copy-done.2), channel_id=1, source_target_pairs={{0,128},{128,0},{1,129},{129,1},{2,130},{130,2},{3,131},{131,3},{4... | collective-permute-start | bytes 983048 | tf_op jit(solution)/shard_map/ppermute | solution.py:223
  109.4 10.5 %collective-permute-done.4.far_rows = bf16[2,160,512]{2,1,0:T(8,128)(2,1)S(1)} collective-permute-done((bf16[2,160,512]{2,1,0:T(8,128)(2,1)}, bf16[2,160,512]{2,1,0:T(8,128)(2,1)S(1)}, u32[]{:S(2)}, u32[]{:S(2)}) %collective-permute-start.4) | collective-permute-done | bytes 327712 | tf_op jit(solution)/shard_map/ppermute | solution.py:223
  120.0 0.0 collective-permute-done.3.far_acts
  120.0 2.2 %shard_map.116 = (f32[768,512]{1,0:T(8,128)S(1)}, bf16[768,512]{1,0:T(8,128)(2,1)S(1)}) custom-call(bf16[320,768]{1,0:T(8,128)(2,1)} %bitcast.4.acts, bf16[320,768]{1,0:T(8,128)(2,1)} %collective-permute-done.3.far_acts, bf16[2,160,512]{2,1,0:T(8,128)(2,1)S(1)} %get-tuple-element.17.own_rows, bf16[2,160,512]{2,1,0:T(8,128)(2,1)S(1)} %collective-permute-done.4.far_rows), custom_call_target="tpu_custom_call" | custom-call | flops 503316480 | bytes 3997696 | tf_op jit(solution)/shard_map/pallas_call | solution.py:207
  122.2 5.0 %collective-permute-start.5 = (bf16[768,512]{1,0:T(8,128)(2,1)S(1)}, bf16[768,512]{1,0:T(8,128)(2,1)S(1)}, u32[]{:S(2)}, u32[]{:S(2)}) collective-permute-start(bf16[768,512]{1,0:T(8,128)(2,1)S(1)} %get-tuple-element.23), channel_id=1, source_target_pairs={{0,1},{1,0},{2,3},{3,2},{4,5},{5,4},{6,7},{7,6},{8,9},{9,8},{10,11... | collective-permute-start | bytes 2359304 | tf_op jit(solution)/shard_map/ppermute | solution.py:223
  127.2 1.9 %collective-permute-done.5.received = bf16[768,512]{1,0:T(8,128)(2,1)S(1)} collective-permute-done((bf16[768,512]{1,0:T(8,128)(2,1)S(1)}, bf16[768,512]{1,0:T(8,128)(2,1)S(1)}, u32[]{:S(2)}, u32[]{:S(2)}) %collective-permute-start.5) | collective-permute-done | bytes 786464 | tf_op jit(solution)/shard_map/ppermute | solution.py:223
  129.1 0.0 copy-done.4
  129.1 1.9 %shard_map.117 = (f32[6,128,128]{2,1,0:T(8,128)}, f32[6,128,128]{2,1,0:T(8,128)}, f32[6,128,128]{2,1,0:T(8,128)}) custom-call(s32[3,2,6]{2,1,0:T(2,128)S(1)} %bitcast.7, s32[3]{0:T(128)S(1)} %bitcast.9, f32[768,512]{1,0:T(8,128)S(1)} %get-tuple-element.22.own, bf16[768,512]{1,0:T(8,128)(2,1)S(1)} %collective-permute-done.5.received), custom_call_target="tpu_custom_call" | custom-call | bytes 3539100 | tf_op jit(solution)/shard_map/pallas_call | solution.py:207
  131.0 0.0 all-to-all-done.3.parts
  131.0 0.7 shard_map.115
  (4 shorter events, 0.0 us)
Async XLA Ops:
  3.1 45.9 %copy-start = (bf16[768,512]{1,0:T(8,128)(2,1)S(1)}, bf16[768,512]{1,0:T(8,128)(2,1)}, u32[]{:S(2)}) copy-start(bf16[768,512]{1,0:T(8,128)(2,1)} %get-tuple-element.19.own) | copy-start | bytes 2359300
  3.1 30.7 %collective-permute-start = (bf16[768,512]{1,0:T(8,128)(2,1)}, bf16[768,512]{1,0:T(8,128)(2,1)S(1)}, u32[]{:S(2)}, u32[]{:S(2)}) collective-permute-start(bf16[768,512]{1,0:T(8,128)(2,1)} %get-tuple-element.19.own), channel_id=1, source_target_pairs={{0,128},{128,0},{1,129},{129,1},{2,130},{130,2},{3,131},{131,3},{4... | collective-permute-start | bytes 2359304 | tf_op jit(solution)/shard_map/ppermute | solution.py:223
  7.2 40.4 %all-to-all-start = ((bf16[64,40,128]{2,1,0:T(8,128)(2,1)}), bf16[64,40,128]{2,1,0:T(8,128)(2,1)}, u32[]{:S(2)}, u32[]{:S(2)}) async-start(bf16[64,40,128]{2,1,0:T(8,128)(2,1)} %get-tuple-element.16), calls=%async_computation | async-start | bytes 1310720 | tf_op jit(solution)/shard_map/all_to_all | solution.py:219
  30.7 18.4 %collective-permute-start.1 = (bf16[768,512]{1,0:T(8,128)(2,1)}, bf16[768,512]{1,0:T(8,128)(2,1)S(1)}, u32[]{:S(2)}, u32[]{:S(2)}) collective-permute-start(bf16[768,512]{1,0:T(8,128)(2,1)} %get-tuple-element.19.own), channel_id=1, source_target_pairs={{0,1},{1,0},{2,3},{3,2},{4,5},{5,4},{6,7},{7,6},{8,9},{9,8},{10,11... | collective-permute-start | bytes 2359304 | tf_op jit(solution)/shard_map/ppermute | solution.py:223
  33.8 15.2 %collective-permute-start.2 = (bf16[768,512]{1,0:T(8,128)(2,1)S(1)}, bf16[768,512]{1,0:T(8,128)(2,1)S(1)}, u32[]{:S(2)}, u32[]{:S(2)}) collective-permute-start(bf16[768,512]{1,0:T(8,128)(2,1)S(1)} %collective-permute-done.far), channel_id=1, source_target_pairs={{0,1},{1,0},{2,3},{3,2},{4,5},{5,4},{6,7},{7,6},{8,9},{9,8},{10,11... | collective-permute-start | bytes 2359304 | tf_op jit(solution)/shard_map/ppermute | solution.py:223
  49.0 0.9 copy-start.2
  87.8 32.2 %collective-permute-start.3 = (bf16[320,768]{1,0:T(8,128)(2,1)}, bf16[320,768]{1,0:T(8,128)(2,1)}, u32[]{:S(2)}, u32[]{:S(2)}) collective-permute-start(bf16[320,768]{1,0:T(8,128)(2,1)} %bitcast.4.acts), channel_id=1, source_target_pairs={{0,128},{128,0},{1,129},{129,1},{2,130},{130,2},{3,131},{131,3},{4... | collective-permute-start | bytes 1474568 | tf_op jit(solution)/shard_map/ppermute | solution.py:223
  98.1 0.9 copy-start.1
  98.9 30.1 %copy-start.3 = (s32[3,6,2]{1,2,0:T(2,128)S(1)}, s32[3,6,2]{1,2,0:T(2,128)}, u32[]{:S(2)}) copy-start(s32[3,6,2]{1,2,0:T(2,128)} %param.12) | copy-start | bytes 436
  98.9 30.1 %copy-start.4 = (s32[3,1,1]{0,2,1:T(1,128)S(1)}, s32[3,1,1]{0,2,1:T(1,128)}, u32[]{:S(2)}) copy-start(s32[3,1,1]{0,2,1:T(1,128)} %param.13) | copy-start | bytes 40
  98.9 32.1 %all-to-all-start.3 = ((bf16[64,40,128]{2,1,0:T(8,128)(2,1)}), bf16[64,40,128]{2,1,0:T(8,128)(2,1)S(1)}, u32[]{:S(2)}, u32[]{:S(2)}) async-start(bf16[64,40,128]{2,1,0:T(8,128)(2,1)} %copy-done.1), calls=%async_computation.3 | async-start | bytes 1310720 | tf_op jit(solution)/shard_map/all_to_all | solution.py:219
  106.4 13.6 %collective-permute-start.4 = (bf16[2,160,512]{2,1,0:T(8,128)(2,1)}, bf16[2,160,512]{2,1,0:T(8,128)(2,1)S(1)}, u32[]{:S(2)}, u32[]{:S(2)}) collective-permute-start(bf16[2,160,512]{2,1,0:T(8,128)(2,1)} %copy-done.2), channel_id=1, source_target_pairs={{0,128},{128,0},{1,129},{129,1},{2,130},{130,2},{3,131},{131,3},{4... | collective-permute-start | bytes 983048 | tf_op jit(solution)/shard_map/ppermute | solution.py:223
  122.2 6.9 %collective-permute-start.5 = (bf16[768,512]{1,0:T(8,128)(2,1)S(1)}, bf16[768,512]{1,0:T(8,128)(2,1)S(1)}, u32[]{:S(2)}, u32[]{:S(2)}) collective-permute-start(bf16[768,512]{1,0:T(8,128)(2,1)S(1)} %get-tuple-element.23), channel_id=1, source_target_pairs={{0,1},{1,0},{2,3},{3,2},{4,5},{5,4},{6,7},{7,6},{8,9},{9,8},{10,11... | collective-permute-start | bytes 2359304 | tf_op jit(solution)/shard_map/ppermute | solution.py:223
